TPU v7x, 256 devices: a whole 4x4x8 slice. The times are simulated.
256 devices in a mesh: ctx: 16 (over z, core), exp: 16 (over x, y).
Axes of the slice: x: 4, y: 4, z: 8, core: 2. Of those that a mesh axis runs over, the one named last changes fastest.
Arguments:
- mixer_input: bfloat16 [2048, 4096], P('ctx', 'exp'), may hold values from -6 to 6
- mixer_gate: bfloat16 [2048, 4096], P('ctx', 'exp'), may hold values from -6 to 6
- step_low: bfloat16 [2048, 128], P('ctx'), may hold values from -16 to 16
- step_proj: bfloat16 [128, 4096], P(None, 'exp'), may hold values from -0.5 to 0.5
- step_bias: float32 [4096], P('exp'), may hold values from -1 to 1
- decay_rate: float32 [16, 4096], P(None, 'exp'), may hold values from 2.4414063e-05 to 0.1
- input_coef: float32 [16, 2048], P(None, 'ctx'), may hold values from -6 to 6
- output_coef: float32 [16, 2048], P(None, 'ctx'), may hold values from -0.625 to 0.625
- conv_taps: float32 [4, 4096], P(None, 'exp'), may hold values from -3 to 3
- conv_bias: float32 [4096], P('exp'), may hold values from -0.5 to 0.5
- skip_gain: float32 [4096], P('exp'), may hold values from 0.5 to 1.5
- out_weight: bfloat16 [4096, 2048], P('exp'), may hold values from -0.09375 to 0.09375
- residual: bfloat16 [2048, 2048], P(('ctx', 'exp')), may hold values from -6 to 6
- norm_gain: float32 [2048], replicated, may hold values from 0.5 to 1.5
- expert_ids: int32 [2048, 2], P(('ctx', 'exp')), may hold values from 0 to 15, all different within a row; in each aligned block of 8 rows (0 to 7, 8 to 15, ...) at most 2 rows name the same one
- gate_scores: float32 [2048, 2], P(('ctx', 'exp')), may hold values from 0.1 to 1
- gate_weight: bfloat16 [16, 2048, 14336], P('exp', None, 'ctx'), may hold values from -0.125 to 0.125
- up_weight: bfloat16 [16, 2048, 14336], P('exp', None, 'ctx'), may hold values from -0.125 to 0.125
- down_weight: bfloat16 [16, 14336, 2048], P('exp', 'ctx'), may hold values from -0.046875 to 0.046875
- cotangent: bfloat16 [2048, 2048], P(('ctx', 'exp')), may hold values from -6 to 6
Outputs:
- layer_out: bfloat16 [2048, 2048], P(('ctx', 'exp'))
- grad_hidden: float32 [2048, 2048], P(('ctx', 'exp'))
- grad_scores: float32 [2048, 2], P(('ctx', 'exp'))
Inputs may be any that keep to these rules, and one draw needn't show every extreme that they name: `expert_ids`: A token's two experts differ. In each device's block of 8 consecutive tokens, no expert is named by more than 2 of the block's choices, and in every draw some expert is named exactly 2 times in some block.
All inputs are finite; a program needn't handle non-finite values.
Results may differ from a plain program's by a relative error of at most 0.013.
Values may be sent and summed in bfloat16 or wider, within the bound.
No kernel may reach another device: no remote copies, remote signals or barrier semaphores. Data moves between devices by JAX's collectives and lax.ppermute only.
A program may use at most 128 MiB of HBM per device.

v0:
```python
import jax
import jax.numpy as jnp
from jax import lax
from jax.experimental import pallas as pl
from jax.experimental.pallas import tpu as pltpu
from jax.sharding import Mesh
from jax.sharding import PartitionSpec as P

BF16 = jnp.bfloat16
F32 = jnp.float32
VMEM = pl.BlockSpec(memory_space=pltpu.VMEM)
SMEM = pl.BlockSpec(memory_space=pltpu.SMEM)
GROUP = 8


def contract_last(left, right):
    return lax.dot_general(left, right, (((1,), (1,)), ((), ())), preferred_element_type=F32)


def contract_first(left, right):
    return lax.dot_general(left, right, (((0,), (0,)), ((), ())), preferred_element_type=F32)


def local_state_body(
    x_ref, halo_ref, low_ref, proj_ref, bias_ref, decay_ref, bcoef_ref, taps_ref, cbias_ref,
    summary_ref, step_ref, inner_ref, pad_ref, drive_ref,
):
    length = x_ref.shape[0]
    taps = taps_ref.shape[0]
    halo = halo_ref.shape[0]
    pad_ref[0:halo] = halo_ref[...].astype(F32)
    pad_ref[halo:] = x_ref[...].astype(F32)
    filtered = cbias_ref[...]
    for k in range(taps):
        first = halo - taps + 1 + k
        filtered = filtered + taps_ref[k : k + 1] * pad_ref[first : first + length]
    inner = jax.nn.silu(filtered)
    inner_ref[...] = inner
    pre = jnp.dot(low_ref[...], proj_ref[...], preferred_element_type=F32) + bias_ref[...]
    step = jnp.maximum(pre, 0.0) + jnp.log1p(jnp.exp(-jnp.abs(pre)))
    step_ref[...] = step
    drive_ref[...] = step * inner
    rate = -decay_ref[...]
    shape = rate.shape

    def group(g, carry):
        state, coef = carry
        rows = pl.ds(pl.multiple_of(g * GROUP, GROUP), GROUP)
        steps = step_ref[rows]
        drives = drive_ref[rows]
        for k in range(GROUP):
            factor = jnp.exp(jnp.broadcast_to(steps[k : k + 1], shape) * rate)
            push = jnp.broadcast_to(drives[k : k + 1], shape) * jnp.broadcast_to(
                coef[:, k : k + 1], shape
            )
            state = factor * state + push
        return state, pltpu.roll(coef, coef.shape[1] - GROUP, 1)

    state, _ = lax.fori_loop(0, length // GROUP, group, (jnp.zeros(shape, F32), bcoef_ref[...]))
    count = shape[0]
    summary_ref[0:count] = state
    summary_ref[count:] = jnp.broadcast_to(
        jnp.sum(step, axis=0, keepdims=True), (summary_ref.shape[0] - count, shape[1])
    )


def readout_body(
    mine_ref, gathered_ref, decay_ref, bcoef_ref, ccoef_ref, step_ref, inner_ref, skip_ref,
    gate_ref, weight_ref, out_ref, drive_ref, read_ref,
):
    rate = -decay_ref[...]
    shape = rate.shape
    count = shape[0]
    length = step_ref.shape[0]
    block = gathered_ref.shape[1]
    mine = mine_ref[0]
    state = jnp.zeros(shape, F32)
    for c in range(gathered_ref.shape[0] - 1):
        total = gathered_ref[c, count : count + 1]
        longer = jnp.exp(jnp.broadcast_to(total, shape) * rate) * state + gathered_ref[c, 0:count]
        state = jnp.where(c < mine, longer, state)
    drive_ref[...] = step_ref[...] * inner_ref[...]

    def group(g, carry):
        state, bcoef, ccoef = carry
        rows = pl.ds(pl.multiple_of(g * GROUP, GROUP), GROUP)
        steps = step_ref[rows]
        drives = drive_ref[rows]
        reads = []
        for k in range(GROUP):
            factor = jnp.exp(jnp.broadcast_to(steps[k : k + 1], shape) * rate)
            push = jnp.broadcast_to(drives[k : k + 1], shape) * jnp.broadcast_to(
                bcoef[:, k : k + 1], shape
            )
            state = factor * state + push
            reads.append(
                jnp.sum(state * jnp.broadcast_to(ccoef[:, k : k + 1], shape), axis=0, keepdims=True)
            )
        read_ref[rows] = jnp.concatenate(reads, axis=0)
        turn = bcoef.shape[1] - GROUP
        return state, pltpu.roll(bcoef, turn, 1), pltpu.roll(ccoef, turn, 1)

    lax.fori_loop(0, length // GROUP, group, (state, bcoef_ref[...], ccoef_ref[...]))
    output = read_ref[...] + skip_ref[...] * inner_ref[...]
    output = output * jax.nn.silu(gate_ref[...].astype(F32))
    out_ref[...] = jnp.dot(
        output.astype(BF16), weight_ref[...], preferred_element_type=F32
    ).astype(BF16)


def gated_grads(gate_pre, up_pre, grad_act):
    sigma = jax.nn.sigmoid(gate_pre)
    grad_gate = (grad_act * up_pre * sigma * (1.0 + gate_pre * (1.0 - sigma))).astype(BF16)
    grad_up = (grad_act * (gate_pre * sigma)).astype(BF16)
    return (grad_gate, grad_up)


def make_per_device(interpret):
    def mixer_share(
        mixer_input, mixer_gate, step_low, step_proj, step_bias, decay_rate, input_coef,
        output_coef, conv_taps, conv_bias, skip_gain, out_weight,
    ):
        length, width = mixer_input.shape
        count = decay_rate.shape[0]
        halo = 8
        ranks = lax.axis_size("z") * lax.axis_size("core")
        tail = lax.ppermute(
            mixer_input[length - halo :], ("z", "core"), [(i, i + 1) for i in range(ranks - 1)]
        )
        sums = jax.ShapeDtypeStruct((count + 8, width), F32)
        rows = jax.ShapeDtypeStruct((length, width), F32)
        summary, step, inner = pl.pallas_call(
            local_state_body,
            out_shape=(sums, rows, rows),
            in_specs=[VMEM] * 9,
            out_specs=(VMEM, VMEM, VMEM),
            scratch_shapes=[pltpu.VMEM((length + halo, width), F32), pltpu.VMEM((length, width), F32)],
            interpret=interpret,
            name="local_state",
        )(
            mixer_input, tail, step_low, step_proj, step_bias[None], decay_rate, input_coef,
            conv_taps, conv_bias[None],
        )
        gathered = lax.all_gather(summary, ("z", "core"), axis=0)
        mine = lax.axis_index(("z", "core")).astype(jnp.int32).reshape(1)
        return pl.pallas_call(
            readout_body,
            out_shape=jax.ShapeDtypeStruct((length, out_weight.shape[1]), BF16),
            in_specs=[SMEM] + [VMEM] * 9,
            out_specs=VMEM,
            scratch_shapes=[pltpu.VMEM((length, width), F32), pltpu.VMEM((length, width), F32)],
            interpret=interpret,
            name="readout",
        )(
            mine, gathered, decay_rate, input_coef, output_coef, step, inner, skip_gain[None],
            mixer_gate, out_weight,
        )

    def per_device(
        mixer_input, mixer_gate, step_low, step_proj, step_bias, decay_rate, input_coef,
        output_coef, conv_taps, conv_bias, skip_gain, out_weight, residual, norm_gain,
        expert_ids, gate_scores, gate_weight, up_weight, down_weight, cotangent,
    ):
        tok_rows, width = residual.shape
        experts = lax.axis_size("exp")
        depth = lax.axis_size("z")
        capacity = 4 * tok_rows // experts
        slot_count = experts * capacity
        swap = [(0, 1), (1, 0)]

        def sibling(value):
            return lax.ppermute(value, "core", swap)

        def exchange(slots):
            return lax.all_to_all(slots, ("z", "exp"), split_axis=0, concat_axis=0, tiled=True)

        def to_all(rows):
            return exchange(jnp.broadcast_to(rows[None], (depth,) + rows.shape).reshape(-1, width))

        def from_all(rows):
            back = exchange(rows).reshape(depth, slot_count, width)
            return jnp.sum(back.astype(F32), axis=0).astype(BF16)

        flat_ids = expert_ids.reshape(-1)
        choice = jnp.arange(flat_ids.shape[0], dtype=jnp.int32)
        same = (flat_ids[:, None] == flat_ids[None, :]) & (choice[None, :] < choice[:, None])
        slot = jnp.sum(same.astype(jnp.int32), axis=1)
        target = flat_ids * capacity + slot
        placing = (target[:, None] == jnp.arange(slot_count, dtype=jnp.int32)[None, :]).astype(BF16)

        outer = cotangent.astype(F32)
        grad_rows = (gate_scores[:, :, None] * outer[:, None, :]).reshape(-1, width).astype(BF16)
        rows_d = to_all(contract_first(placing, grad_rows).astype(BF16))

        gates = (gate_weight[0], sibling(gate_weight[0]))
        ups = (up_weight[0], sibling(up_weight[0]))
        downs = (down_weight[0], sibling(down_weight[0]))

        share = mixer_share(
            mixer_input, mixer_gate, step_low, step_proj, step_bias, decay_rate, input_coef,
            output_coef, conv_taps, conv_bias, skip_gain, out_weight,
        )
        shares = lax.all_to_all(share, "exp", split_axis=0, concat_axis=0, tiled=True)
        shares = shares.reshape(experts, tok_rows, width).astype(F32)
        hidden = residual.astype(F32) + jnp.sum(shares, axis=0)
        scale = lax.rsqrt(jnp.mean(hidden * hidden, axis=1, keepdims=True) + 1e-05)
        normed = (hidden * scale * norm_gain).astype(BF16)
        rows_x = to_all(contract_first(placing, jnp.repeat(normed, 2, axis=0)).astype(BF16))

        grad_acts = [contract_last(rows_d, down) for down in downs]
        partial_out = 0.0
        grads = []
        for gate_mat, up_mat, down_mat, grad_act in zip(gates, ups, downs, grad_acts):
            gate_pre = jnp.dot(rows_x, gate_mat, preferred_element_type=F32)
            up_pre = jnp.dot(rows_x, up_mat, preferred_element_type=F32)
            activated = (jax.nn.silu(gate_pre) * up_pre).astype(BF16)
            grads.append(gated_grads(gate_pre, up_pre, grad_act))
            partial_out = partial_out + jnp.dot(activated, down_mat, preferred_element_type=F32)
        expert_out = from_all(partial_out.astype(BF16))
        partial_in = 0.0
        for gate_mat, up_mat, (grad_gate, grad_up) in zip(gates, ups, grads):
            partial_in = partial_in + contract_last(grad_gate, gate_mat)
            partial_in = partial_in + contract_last(grad_up, up_mat)
        grad_in = from_all(partial_in.astype(BF16))

        per_choice = jnp.dot(placing, expert_out, preferred_element_type=F32)
        per_choice = per_choice.reshape(tok_rows, 2, width)
        moe = jnp.sum(gate_scores[:, :, None] * per_choice, axis=1)
        layer_out = (hidden + moe).astype(BF16)
        grad_scores = jnp.sum(outer[:, None, :] * per_choice, axis=2)
        grad_normed = jnp.sum(
            jnp.dot(placing, grad_in, preferred_element_type=F32).reshape(tok_rows, 2, width),
            axis=1,
        )
        scaled = grad_normed * norm_gain
        grad_hidden = (
            outer
            + scale * scaled
            - hidden * scale**3 * jnp.mean(hidden * scaled, axis=1, keepdims=True)
        )
        return (layer_out, grad_hidden, grad_scores)

    return per_device


def solution(mesh, interpret=False):
    ctx, exp = mesh.devices.shape
    split = Mesh(mesh.devices.reshape(ctx // 2, 2, exp), ("z", "core", "exp"))
    both = ("z", "core")
    rows = P(("z", "core", "exp"), None)
    in_specs = (
        P(both, "exp"),
        P(both, "exp"),
        P(both, None),
        P(None, "exp"),
        P("exp"),
        P(None, "exp"),
        P(None, both),
        P(None, both),
        P(None, "exp"),
        P("exp"),
        P("exp"),
        P("exp", None),
        rows,
        P(),
        rows,
        rows,
        P("exp", None, both),
        P("exp", None, both),
        P("exp", both, None),
        rows,
    )
    return jax.shard_map(
        make_per_device(interpret),
        mesh=split,
        in_specs=in_specs,
        out_specs=(rows, rows, rows),
        check_vma=False,
    )
```

profile of v0, /device:TPU:2, one launch (start us, length us, event | category | flops | bytes accessed | tf_op | source)
XLA Modules:
  0.0 226.5 jit_solution(9084562042555516194)
XLA Ops:
  1.4 1.7 collective-permute-start
  4.5 3.3 %local_state.1 = (f32[24,256]{1,0:T(8,128)}, f32[128,256]{1,0:T(8,128)}, f32[128,256]{1,0:T(8,128)}) custom-call(bf16[128,256]{1,0:T(8,128)(2,1)} %x_ref.1, bf16[8,256]{1,0:T(8,128)(2,1)} %copy-done.13, bf16[128,128]{1,0:T(8,128)(2,1)} %low_ref.1, bf16[128,256]{1,0:T(8,128)(2,1)} %proj_ref.1, f32[1,256]{1,0:T(1,128)} %bitcast.45, f32[16,256]{1,0:T(8,128)} %decay_ref.3, ...), custom_call_target="tpu_custom_call" | custom-call | tf_op jit(solution)/shard_map/local_state/pallas_call | solution.py:132
  7.8 25.0 %all-gather = f32[384,256]{1,0:T(8,128)} all-gather(f32[24,256]{1,0:T(8,128)} %get-tuple-element.6), channel_id=2, replica_groups=mesh['z'=8,'core'=2,'exp'=16] {'z','core'}, dimensions={0}, use_global_device_ids=true | all-gather | bytes 417792 | tf_op jit(solution)/shard_map/all_gather | solution.py:144
  32.8 4.7 %readout.1 = bf16[128,2048]{1,0:T(8,128)(2,1)} custom-call(s32[1]{0:T(128)} %bitcast.mine_ref, f32[16,24,256]{2,1,0:T(8,128)} %bitcast.44, f32[16,256]{1,0:T(8,128)} %decay_ref.3, f32[16,128]{1,0:T(8,128)} %bcoef_ref.3, f32[16,128]{1,0:T(8,128)} %ccoef_ref.1, f32[128,256]{1,0:T(8,128)} %get-tuple-element.7.step_ref, f32[128,256]{1,0:T(8,128)} %get-tuple-element.8.inner_ref, ...), custom_call_target="tpu_custom_call" | custom-call | tf_op jit(solution)/shard_map/readout/pallas_call | solution.py:146
  37.6 7.6 %all-to-all-start = ((bf16[16,8,2048]{2,1,0:T(8,128)(2,1)}), bf16[16,8,2048]{2,1,0:T(8,128)(2,1)S(1)}, u32[]{:S(2)}, u32[]{:S(2)}) async-start(bf16[16,8,2048]{2,1,0:T(8,128)(2,1)} %bitcast.43), calls=%async_computation | async-start | bytes 1048576 | tf_op jit(solution)/shard_map/all_to_all | solution.py:203
  46.1 1.5 all_to_all.41
  47.6 7.3 %all-to-all-done = bf16[16,8,2048]{2,1,0:T(8,128)(2,1)S(1)} async-done(((bf16[16,8,2048]{2,1,0:T(8,128)(2,1)}), bf16[16,8,2048]{2,1,0:T(8,128)(2,1)S(1)}, u32[]{:S(2)}, u32[]{:S(2)}) %all-to-all-start) | async-done | bytes 524320 | tf_op jit(solution)/shard_map/all_to_all | solution.py:203
  54.9 9.5 %all-to-all-start.3 = ((bf16[128,2,2048]{2,1,0:T(2,128)(2,1)}), bf16[128,2,2048]{2,1,0:T(2,128)(2,1)S(1)}, u32[]{:S(2)}, u32[]{:S(2)}) async-start(bf16[128,2,2048]{2,1,0:T(2,128)(2,1)} %all_to_all.41), calls=%async_computation.3 | async-start | bytes 2097152 | tf_op jit(solution)/shard_map/all_to_all | solution.py:175
  66.9 27.8 %all-to-all-done.3 = bf16[128,2,2048]{2,1,0:T(2,128)(2,1)S(1)} async-done(((bf16[128,2,2048]{2,1,0:T(2,128)(2,1)}), bf16[128,2,2048]{2,1,0:T(2,128)(2,1)S(1)}, u32[]{:S(2)}, u32[]{:S(2)}) %all-to-all-start.3) | async-done | bytes 1048608 | tf_op jit(solution)/shard_map/all_to_all | solution.py:175
  94.7 6.5 %all-to-all-start.1 = ((bf16[128,2,2048]{2,1,0:T(2,128)(2,1)}), bf16[128,2,2048]{2,1,0:T(2,128)(2,1)S(1)}, u32[]{:S(2)}, u32[]{:S(2)}) async-start(bf16[128,2,2048]{2,1,0:T(2,128)(2,1)} %all_to_all.36), calls=%async_computation.1 | async-start | bytes 2097152 | tf_op jit(solution)/shard_map/all_to_all | solution.py:175
  102.3 4.3 %fusion.23 = f32[256,896]{1,0:T(8,128)} fusion(bf16[256,2048]{1,0:T(8,128)(2,1)S(1)} %all_to_all.43, bf16[1,896,2048]{2,1,0:T(8,128)(2,1)} %param.38), kind=kOutput, calls=%fused_computation.52 | convolution fusion | flops 939524096 | bytes 5636096 | tf_op jit(solution)/shard_map/dot_general | solution.py:17
  106.5 24.6 %all-to-all-done.1 = bf16[128,2,2048]{2,1,0:T(2,128)(2,1)S(1)} async-done(((bf16[128,2,2048]{2,1,0:T(2,128)(2,1)}), bf16[128,2,2048]{2,1,0:T(2,128)(2,1)S(1)}, u32[]{:S(2)}, u32[]{:S(2)}) %all-to-all-start.1) | async-done | bytes 1048608 | tf_op jit(solution)/shard_map/all_to_all | solution.py:175
  131.6 3.5 %fusion.30 = f32[256,896]{1,0:T(8,128)S(1)} fusion(bf16[256,2048]{1,0:T(8,128)(2,1)S(1)} %all_to_all.38, bf16[1,2048,896]{2,1,0:T(8,128)(2,1)} %param.36), kind=kOutput, calls=%fused_computation.59 | convolution fusion | flops 939524096 | bytes 5636096 | tf_op jit(solution)/shard_map/dot_general | solution.py:214
  138.8 3.3 %fusion.38 = f32[256,896]{1,0:T(8,128)S(1)} fusion(bf16[256,2048]{1,0:T(8,128)(2,1)S(1)} %all_to_all.38, bf16[2048,896]{1,0:T(8,128)(2,1)} %collective-permute-done.1), kind=kOutput, calls=%fused_computation.67 | convolution fusion | flops 939524096 | bytes 5636096 | tf_op jit(solution)/shard_map/dot_general | solution.py:214
  142.2 3.6 %fusion.39 = f32[256,896]{1,0:T(8,128)S(1)} fusion(bf16[256,2048]{1,0:T(8,128)(2,1)S(1)} %all_to_all.38, bf16[2048,896]{1,0:T(8,128)(2,1)} %collective-permute-done.2), kind=kOutput, calls=%fused_computation.68 | convolution fusion | flops 939524096 | bytes 5636096 | tf_op jit(solution)/shard_map/dot_general | solution.py:215
  146.8 3.4 %fusion.2 = bf16[256,2048]{1,0:T(8,128)(2,1)S(1)} fusion(f32[256,2048]{1,0:T(8,128)S(1)} %fusion.5, bf16[896,2048]{1,0:T(8,128)(2,1)} %collective-permute-done.3, f32[256,896]{1,0:T(8,128)S(1)} %fusion.39, f32[256,896]{1,0:T(8,128)S(1)} %fusion.38), kind=kOutput, calls=%fused_computation.5 | convolution fusion | flops 941948928 | bytes 8650752 | tf_op jit(solution)/shard_map/dot_general | solution.py:218
  151.7 6.5 %all-to-all-start.2 = ((bf16[128,2,2048]{2,1,0:T(2,128)(2,1)}), bf16[128,2,2048]{2,1,0:T(2,128)(2,1)S(1)}, u32[]{:S(2)}, u32[]{:S(2)}) async-start(bf16[128,2,2048]{2,1,0:T(2,128)(2,1)} %all_to_all.39), calls=%async_computation.2 | async-start | bytes 2097152 | tf_op jit(solution)/shard_map/all_to_all | solution.py:175
  158.3 4.1 %fusion.6 = f32[256,2048]{1,0:T(8,128)S(1)} fusion(f32[256,896]{1,0:T(8,128)} %copy-done.5, f32[256,896]{1,0:T(8,128)S(1)} %copy-done.2, f32[256,896]{1,0:T(8,128)} %copy-done.15, bf16[1,2048,896]{2,1,0:T(8,128)(2,1)} %param.36), kind=kOutput, calls=%fused_computation.21 | convolution fusion | flops 941817856 | bytes 8519680 | tf_op jit(solution)/shard_map/dot_general | solution.py:17
  163.8 3.4 %fusion.40 = f32[256,896]{1,0:T(8,128)S(1)} fusion(bf16[256,2048]{1,0:T(8,128)(2,1)S(1)} %all_to_all.43, bf16[896,2048]{1,0:T(8,128)(2,1)} %collective-permute-done.3), kind=kOutput, calls=%fused_computation.69 | convolution fusion | flops 939524096 | bytes 5636096 | tf_op jit(solution)/shard_map/dot_general | solution.py:17
  167.2 3.4 %fusion.7 = f32[256,2048]{1,0:T(8,128)S(1)} fusion(bf16[2048,896]{1,0:T(8,128)(2,1)} %collective-permute-done.2, f32[256,896]{1,0:T(8,128)S(1)} %fusion.40, f32[256,896]{1,0:T(8,128)S(1)} %copy-done.4), kind=kOutput, calls=%fused_computation.22 | convolution fusion | flops 940900352 | bytes 7602176 | tf_op jit(solution)/shard_map/dot_general | solution.py:17
  170.6 3.5 %fusion.1 = bf16[256,2048]{1,0:T(8,128)(2,1)S(1)} fusion(f32[256,2048]{1,0:T(8,128)S(1)} %fusion.7, f32[256,2048]{1,0:T(8,128)S(1)} %convolution_add_fusion.1, bf16[2048,896]{1,0:T(8,128)(2,1)} %collective-permute-done.1, f32[256,896]{1,0:T(8,128)S(1)} %copy-done.4, f32[256,896]{1,0:T(8,128)S(1)} %fusion.40, f32[256,896]{1,0:T(8,128)S(1)} %copy-done.8), kind=kOutput, calls=%fused_computation.4 | convolution fusion | flops 943390720 | bytes 11665408 | tf_op jit(solution)/shard_map/dot_general | solution.py:17
  175.7 12.2 %all-to-all-done.2 = bf16[128,2,2048]{2,1,0:T(2,128)(2,1)S(1)} async-done(((bf16[128,2,2048]{2,1,0:T(2,128)(2,1)}), bf16[128,2,2048]{2,1,0:T(2,128)(2,1)S(1)}, u32[]{:S(2)}, u32[]{:S(2)}) %all-to-all-start.2) | async-done | bytes 1048608 | tf_op jit(solution)/shard_map/all_to_all | solution.py:175
  187.9 6.5 %all-to-all-start.4 = ((bf16[128,2,2048]{2,1,0:T(2,128)(2,1)}), bf16[128,2,2048]{2,1,0:T(2,128)(2,1)S(1)}, u32[]{:S(2)}, u32[]{:S(2)}) async-start(bf16[128,2,2048]{2,1,0:T(2,128)(2,1)} %all_to_all.44), calls=%async_computation.4 | async-start | bytes 2097152 | tf_op jit(solution)/shard_map/all_to_all | solution.py:175
  195.2 28.8 %all-to-all-done.4 = bf16[128,2,2048]{2,1,0:T(2,128)(2,1)S(1)} async-done(((bf16[128,2,2048]{2,1,0:T(2,128)(2,1)}), bf16[128,2,2048]{2,1,0:T(2,128)(2,1)S(1)}, u32[]{:S(2)}, u32[]{:S(2)}) %all-to-all-start.4) | async-done | bytes 1048608 | tf_op jit(solution)/shard_map/all_to_all | solution.py:175
  (79 shorter events, 19.0 us)
Async XLA Ops:
  0.6 44.7 %copy-start.10 = (bf16[8,2048]{1,0:T(8,128)(2,1)S(1)}, bf16[8,2048]{1,0:T(8,128)(2,1)}, u32[]{:S(2)}) copy-start(bf16[8,2048]{1,0:T(8,128)(2,1)} %param.39) | copy-start | bytes 98308
  0.6 44.9 %copy-start.12 = (f32[8,2]{0,1:T(2,128)S(1)}, f32[8,2]{0,1:T(2,128)}, u32[]{:S(2)}) copy-start(f32[8,2]{0,1:T(2,128)} %param.35) | copy-start | bytes 196
  1.4 2.6 %collective-permute-start = (bf16[8,256]{1,0:T(8,128)(2,1)S(1)}, bf16[8,256]{1,0:T(8,128)(2,1)S(1)}, u32[]{:S(2)}, u32[]{:S(2)}) collective-permute-start(bf16[8,256]{1,0:T(8,128)(2,1)S(1)} %slice.3), channel_id=1, source_target_pairs={{0,16},{16,32},{32,48},{48,64},{64,80},{80,96},{96,112},{112,128},... | collective-permute-start | bytes 12296 | tf_op jit(solution)/shard_map/ppermute | solution.py:127
  37.6 27.1 %copy-start.9 = (bf16[8,2048]{1,0:T(8,128)(2,1)S(1)}, bf16[8,2048]{1,0:T(8,128)(2,1)}, u32[]{:S(2)}) copy-start(bf16[8,2048]{1,0:T(8,128)(2,1)} %param.32) | copy-start | bytes 98308
  37.6 27.3 %copy-start.11 = (f32[2048]{0:T(1024)S(1)}, f32[2048]{0:T(1024)}, u32[]{:S(2)}) copy-start(f32[2048]{0:T(1024)} %param.33) | copy-start | bytes 24580
  37.6 17.4 %all-to-all-start = ((bf16[16,8,2048]{2,1,0:T(8,128)(2,1)}), bf16[16,8,2048]{2,1,0:T(8,128)(2,1)S(1)}, u32[]{:S(2)}, u32[]{:S(2)}) async-start(bf16[16,8,2048]{2,1,0:T(8,128)(2,1)} %bitcast.43), calls=%async_computation | async-start | bytes 1048576 | tf_op jit(solution)/shard_map/all_to_all | solution.py:203
  54.9 39.8 %all-to-all-start.3 = ((bf16[128,2,2048]{2,1,0:T(2,128)(2,1)}), bf16[128,2,2048]{2,1,0:T(2,128)(2,1)S(1)}, u32[]{:S(2)}, u32[]{:S(2)}) async-start(bf16[128,2,2048]{2,1,0:T(2,128)(2,1)} %all_to_all.41), calls=%async_computation.3 | async-start | bytes 2097152 | tf_op jit(solution)/shard_map/all_to_all | solution.py:175
  64.5 74.4 %collective-permute-start.1 = (bf16[2048,896]{1,0:T(8,128)(2,1)}, bf16[2048,896]{1,0:T(8,128)(2,1)}, u32[]{:S(2)}, u32[]{:S(2)}) collective-permute-start(bf16[2048,896]{1,0:T(8,128)(2,1)} %bitcast.49), channel_id=1, source_target_pairs={{0,16},{16,0},{1,17},{17,1},{2,18},{18,2},{3,19},{19,3},{4,20},{20... | collective-permute-start | bytes 11010056 | tf_op jit(solution)/shard_map/ppermute | solution.py:172
  94.7 36.5 %all-to-all-start.1 = ((bf16[128,2,2048]{2,1,0:T(2,128)(2,1)}), bf16[128,2,2048]{2,1,0:T(2,128)(2,1)S(1)}, u32[]{:S(2)}, u32[]{:S(2)}) async-start(bf16[128,2,2048]{2,1,0:T(2,128)(2,1)} %all_to_all.36), calls=%async_computation.1 | async-start | bytes 2097152 | tf_op jit(solution)/shard_map/all_to_all | solution.py:175
  101.2 40.9 %collective-permute-start.2 = (bf16[2048,896]{1,0:T(8,128)(2,1)}, bf16[2048,896]{1,0:T(8,128)(2,1)}, u32[]{:S(2)}, u32[]{:S(2)}) collective-permute-start(bf16[2048,896]{1,0:T(8,128)(2,1)} %bitcast.42), channel_id=1, source_target_pairs={{0,16},{16,0},{1,17},{17,1},{2,18},{18,2},{3,19},{19,3},{4,20},{20... | collective-permute-start | bytes 11010056 | tf_op jit(solution)/shard_map/ppermute | solution.py:172
  101.3 44.5 %collective-permute-start.3 = (bf16[896,2048]{1,0:T(8,128)(2,1)}, bf16[896,2048]{1,0:T(8,128)(2,1)}, u32[]{:S(2)}, u32[]{:S(2)}) collective-permute-start(bf16[896,2048]{1,0:T(8,128)(2,1)} %bitcast.48), channel_id=1, source_target_pairs={{0,16},{16,0},{1,17},{17,1},{2,18},{18,2},{3,19},{19,3},{4,20},{20... | collective-permute-start | bytes 11010056 | tf_op jit(solution)/shard_map/ppermute | solution.py:172
  131.6 3.5 %copy-start = (bf16[1,2048,896]{2,1,0:T(8,128)(2,1)S(1)}, bf16[1,2048,896]{2,1,0:T(8,128)(2,1)}, u32[]{:S(2)}) copy-start(bf16[1,2048,896]{2,1,0:T(8,128)(2,1)} %param.37) | copy-start | bytes 11010052
  135.1 3.7 %copy-start.5 = (f32[256,896]{1,0:T(8,128)}, f32[256,896]{1,0:T(8,128)S(1)}, u32[]{:S(2)}) copy-start(f32[256,896]{1,0:T(8,128)S(1)} %fusion.30) | copy-start | bytes 2752516
  135.1 2.4 %copy-start.14 = (bf16[1,896,2048]{2,1,0:T(8,128)(2,1)S(1)}, bf16[1,896,2048]{2,1,0:T(8,128)(2,1)}, u32[]{:S(2)}) copy-start(bf16[1,896,2048]{2,1,0:T(8,128)(2,1)} %param.38) | copy-start | bytes 11010052
  137.5 1.3 copy-start.15
  142.2 3.7 %copy-start.3 = (f32[256,896]{1,0:T(8,128)}, f32[256,896]{1,0:T(8,128)S(1)}, u32[]{:S(2)}) copy-start(f32[256,896]{1,0:T(8,128)S(1)} %fusion.38) | copy-start | bytes 2752516
  145.8 1.0 copy-start.7
  150.2 8.0 %copy-start.2 = (f32[256,896]{1,0:T(8,128)S(1)}, f32[256,896]{1,0:T(8,128)}, u32[]{:S(2)}) copy-start(f32[256,896]{1,0:T(8,128)} %fusion.23) | copy-start | bytes 2752516
  151.7 36.2 %all-to-all-start.2 = ((bf16[128,2,2048]{2,1,0:T(2,128)(2,1)}), bf16[128,2,2048]{2,1,0:T(2,128)(2,1)S(1)}, u32[]{:S(2)}, u32[]{:S(2)}) async-start(bf16[128,2,2048]{2,1,0:T(2,128)(2,1)} %all_to_all.39), calls=%async_computation.2 | async-start | bytes 2097152 | tf_op jit(solution)/shard_map/all_to_all | solution.py:175
  158.2 4.2 %copy-start.1 = (bf16[1,2048,896]{2,1,0:T(8,128)(2,1)S(1)}, bf16[1,2048,896]{2,1,0:T(8,128)(2,1)}, u32[]{:S(2)}) copy-start(bf16[1,2048,896]{2,1,0:T(8,128)(2,1)} %param.37) | copy-start | bytes 11010052
  158.2 4.2 %copy-start.6 = (f32[256,896]{1,0:T(8,128)S(1)}, f32[256,896]{1,0:T(8,128)}, u32[]{:S(2)}) copy-start(f32[256,896]{1,0:T(8,128)} %copy-done.5) | copy-start | bytes 2752516
  163.8 3.4 %copy-start.4 = (f32[256,896]{1,0:T(8,128)S(1)}, f32[256,896]{1,0:T(8,128)}, u32[]{:S(2)}) copy-start(f32[256,896]{1,0:T(8,128)} %copy-done.3) | copy-start | bytes 2752516
  167.2 3.5 %copy-start.8 = (f32[256,896]{1,0:T(8,128)S(1)}, f32[256,896]{1,0:T(8,128)}, u32[]{:S(2)}) copy-start(f32[256,896]{1,0:T(8,128)} %copy-done.7) | copy-start | bytes 2752516
  187.9 36.1 %all-to-all-start.4 = ((bf16[128,2,2048]{2,1,0:T(2,128)(2,1)}), bf16[128,2,2048]{2,1,0:T(2,128)(2,1)S(1)}, u32[]{:S(2)}, u32[]{:S(2)}) async-start(bf16[128,2,2048]{2,1,0:T(2,128)(2,1)} %all_to_all.44), calls=%async_computation.4 | async-start | bytes 2097152 | tf_op jit(solution)/shard_map/all_to_all | solution.py:175
  (1 other events, 0.6 us)
where the time goes:
time: 228 us; the launch traced here: 226 us
  waiting for transfers between devices  101 us (44%)
  starting transfers between devices  39.1 us (17%)
  matrix products  38.2 us (17%)
  blocking collectives  25 us (11%)
  local copies, waits for them, and re-layouts  12.6 us (6%)
  Pallas kernels  8.03 us (4%)
    all_to_all x4, waiting for transfers between devices, exchange(): lax.all_to_all(slots, ('z', 'exp'), split_axis=0, concat_axis=0, tiled=True)  93.4 us
    all_to_all x4, starting transfers between devices, exchange(): lax.all_to_all(slots, ('z', 'exp'), split_axis=0, concat_axis=0, tiled=True)  29.1 us
    all_gather x1, blocking collectives, mixer_share(): gathered = lax.all_gather(summary, ('z', 'core'), axis=0)  25 us
    dot_general x6, matrix products, contract_last(): lax.dot_general(left, right, (((1,), (1,)), ((), ())), preferred_element_...  20.1 us
    all_to_all x1, starting transfers between devices, per_device(): lax.all_to_all(share, 'exp', split_axis=0, concat_axis=0, tiled=True)  7.61 us
    all_to_all x1, waiting for transfers between devices, per_device(): lax.all_to_all(share, 'exp', split_axis=0, concat_axis=0, tiled=True)  7.32 us
    all_to_all x6, local copies, waits for them, and re-layouts, exchange(): lax.all_to_all(slots, ('z', 'exp'), split_axis=0, concat_axis=0, tiled=True)  6.82 us
    dot_general x2, matrix products, per_device(): gate_pre = jnp.dot(rows_x, gate_mat, preferred_element_type=F32)  6.78 us
  transfers between devices with their start and end apart: 9, of which 5 were waited for; matrix products, arithmetic and copies ran while one was open for 16% of the time, Pallas kernels for 0%

commit v1 on v0

v1 whole, which is shorter than its diff:
```python
from functools import partial

import jax
import jax.numpy as jnp
from jax import lax
from jax.experimental import pallas as pl
from jax.experimental.pallas import tpu as pltpu
from jax.sharding import Mesh
from jax.sharding import PartitionSpec as P

BF16 = jnp.bfloat16
F32 = jnp.float32
VMEM = pl.BlockSpec(memory_space=pltpu.VMEM)
SMEM = pl.BlockSpec(memory_space=pltpu.SMEM)
GROUP = 8
LANES = 128


def contract_last(left, right):
    return lax.dot_general(left, right, (((1,), (1,)), ((), ())), preferred_element_type=F32)


def contract_first(left, right):
    return lax.dot_general(left, right, (((0,), (0,)), ((), ())), preferred_element_type=F32)


def local_state_body(
    x_ref, halo_ref, low_ref, proj_ref, bias_ref, decay_ref, bcoef_ref, taps_ref, cbias_ref,
    summary_ref, step_ref, inner_ref, pad_ref, drive_ref,
):
    length = x_ref.shape[0]
    taps = taps_ref.shape[0]
    halo = halo_ref.shape[0]
    pad_ref[0:halo] = halo_ref[...].astype(F32)
    pad_ref[halo:] = x_ref[...].astype(F32)
    filtered = cbias_ref[...]
    for k in range(taps):
        first = halo - taps + 1 + k
        filtered = filtered + taps_ref[k : k + 1] * pad_ref[first : first + length]
    inner = jax.nn.silu(filtered)
    inner_ref[...] = inner
    pre = jnp.dot(low_ref[...], proj_ref[...], preferred_element_type=F32) + bias_ref[...]
    step = jnp.maximum(pre, 0.0) + jnp.log1p(jnp.exp(-jnp.abs(pre)))
    step_ref[...] = step
    drive_ref[...] = step * inner
    rate = -decay_ref[...]
    shape = rate.shape

    def group(g, carry):
        state, coef = carry
        rows = pl.ds(pl.multiple_of(g * GROUP, GROUP), GROUP)
        steps = step_ref[rows]
        drives = drive_ref[rows]
        for k in range(GROUP):
            factor = jnp.exp(jnp.broadcast_to(steps[k : k + 1], shape) * rate)
            push = jnp.broadcast_to(drives[k : k + 1], shape) * jnp.broadcast_to(
                coef[:, k : k + 1], shape
            )
            state = factor * state + push
        return state, pltpu.roll(coef, coef.shape[1] - GROUP, 1)

    state, _ = lax.fori_loop(0, length // GROUP, group, (jnp.zeros(shape, F32), bcoef_ref[...]))
    count = shape[0]
    summary_ref[0:count] = state
    summary_ref[count:] = jnp.broadcast_to(
        jnp.sum(step, axis=0, keepdims=True), (summary_ref.shape[0] - count, shape[1])
    )


def readout_body(
    mine_ref, gathered_ref, decay_ref, bcoef_ref, ccoef_ref, step_ref, inner_ref, skip_ref,
    gate_ref, weight_ref, out_ref, drive_ref, read_ref,
):
    rate = -decay_ref[...]
    shape = rate.shape
    count = shape[0]
    length = step_ref.shape[0]
    block = gathered_ref.shape[1]
    mine = mine_ref[0]
    state = jnp.zeros(shape, F32)
    for c in range(gathered_ref.shape[0] - 1):
        total = gathered_ref[c, count : count + 1]
        longer = jnp.exp(jnp.broadcast_to(total, shape) * rate) * state + gathered_ref[c, 0:count]
        state = jnp.where(c < mine, longer, state)
    drive_ref[...] = step_ref[...] * inner_ref[...]

    def group(g, carry):
        state, bcoef, ccoef = carry
        rows = pl.ds(pl.multiple_of(g * GROUP, GROUP), GROUP)
        steps = step_ref[rows]
        drives = drive_ref[rows]
        reads = []
        for k in range(GROUP):
            factor = jnp.exp(jnp.broadcast_to(steps[k : k + 1], shape) * rate)
            push = jnp.broadcast_to(drives[k : k + 1], shape) * jnp.broadcast_to(
                bcoef[:, k : k + 1], shape
            )
            state = factor * state + push
            reads.append(
                jnp.sum(state * jnp.broadcast_to(ccoef[:, k : k + 1], shape), axis=0, keepdims=True)
            )
        read_ref[rows] = jnp.concatenate(reads, axis=0)
        turn = bcoef.shape[1] - GROUP
        return state, pltpu.roll(bcoef, turn, 1), pltpu.roll(ccoef, turn, 1)

    lax.fori_loop(0, length // GROUP, group, (state, bcoef_ref[...], ccoef_ref[...]))
    output = read_ref[...] + skip_ref[...] * inner_ref[...]
    output = output * jax.nn.silu(gate_ref[...].astype(F32))
    out_ref[...] = jnp.dot(
        output.astype(BF16), weight_ref[...], preferred_element_type=F32
    ).astype(BF16)


def slot_maps(info, slots):
    lane = lax.broadcasted_iota(jnp.int32, (info.shape[0], slots), 1)
    block = lax.broadcasted_iota(jnp.int32, (info.shape[0], slots), 0) // GROUP
    maps = []
    for k in range(2):
        base = jnp.broadcast_to(info[:, k : k + 1].astype(jnp.int32), lane.shape)
        maps.append(jnp.where(lane == base + 2 * block, 1.0, 0.0))
    return maps


def prepare_body(ids_ref, scores_ref, cotangent_ref, rows_ref, info_ref, *, stride):
    shape = (cotangent_ref.shape[0], LANES)
    width = cotangent_ref.shape[1]
    row = lax.broadcasted_iota(jnp.int32, shape, 0)
    lane = lax.broadcasted_iota(jnp.int32, shape, 1)
    ids = [jnp.broadcast_to(ids_ref[:, k : k + 1], shape) for k in range(2)]
    fields = []
    for k in range(2):
        slot = jnp.zeros(shape, jnp.int32)
        for back in range(1, shape[0]):
            for other in ids:
                hit = (pltpu.roll(other, back, 0) == ids[k]) & (row >= back)
                slot = slot + hit.astype(jnp.int32)
        fields.append((stride * ids[k] + slot).astype(F32))
    for k in range(2):
        score = jnp.broadcast_to(scores_ref[:, k : k + 1], shape)
        high = score.astype(BF16).astype(F32)
        fields += [high, score - high]
    info = jnp.zeros(shape, F32)
    for place, field in enumerate(fields):
        info = jnp.where(lane == place, field, info)
    info = info.astype(BF16)
    info_ref[...] = info
    outer = cotangent_ref[...].astype(F32)
    for k in range(2):
        rows_ref[:, k * width : (k + 1) * width] = (scores_ref[:, k : k + 1] * outer).astype(BF16)
    rows_ref[:, 2 * width :] = info


def select_body(mine_ref, gathered_ref, rows_ref, *, stride):
    slots, width = rows_ref.shape
    tokens = gathered_ref.shape[0]
    info = gathered_ref[:, 2 * width :].astype(F32)
    lane = lax.broadcasted_iota(jnp.int32, (tokens, LANES), 1)
    block = lax.broadcasted_iota(jnp.int32, (tokens, LANES), 0) // GROUP
    rows = jnp.zeros((LANES, width), F32)
    for k in range(2):
        base = jnp.broadcast_to(info[:, k : k + 1].astype(jnp.int32), lane.shape)
        slot = base - stride * mine_ref[0]
        chosen = (slot >= 0) & (slot < 2) & (lane == slot + 2 * block)
        chosen = jnp.where(chosen, 1.0, 0.0).astype(BF16)
        rows = rows + contract_first(chosen, gathered_ref[:, k * width : (k + 1) * width])
    rows_ref[...] = rows[:slots].astype(BF16)


def norm_body(shares_ref, residual_ref, gain_ref, info_ref, hidden_ref, send_ref):
    width = residual_ref.shape[1]
    hidden = residual_ref[...].astype(F32)
    total = shares_ref[0].astype(F32)
    for c in range(1, shares_ref.shape[0]):
        total = total + shares_ref[c].astype(F32)
    hidden = hidden + total
    hidden_ref[...] = hidden
    scale = lax.rsqrt(jnp.mean(hidden * hidden, axis=1, keepdims=True) + 1e-05)
    normed = (hidden * scale * gain_ref[...]).astype(BF16)
    for c in range(send_ref.shape[0]):
        send_ref[c, :, 0:width] = normed
        send_ref[c, :, width:] = info_ref[...]


def pack_body(tokens_ref, slots_ref):
    slots, width = slots_ref.shape
    first, second = slot_maps(tokens_ref[:, width:].astype(F32), slots)
    slots_ref[...] = contract_first((first + second).astype(BF16), tokens_ref[:, 0:width]).astype(BF16)


def grad_act_body(rows_ref, own_ref, sib_ref, out_ref, *, depth):
    slots = rows_ref.shape[0]
    units = own_ref.shape[0]
    to = lax.broadcasted_iota(jnp.int32, (slots, slots), 0)
    source = lax.broadcasted_iota(jnp.int32, (slots, slots), 1)
    span = 2 * depth
    per_block = slots // depth
    wanted = ((to % span) // 2) * per_block + (to // span) * 2 + to % 2
    order = jnp.where(source == wanted, 1.0, 0.0).astype(BF16)
    rows = jnp.dot(order, rows_ref[...], preferred_element_type=F32).astype(BF16)
    out_ref[:, 0:units] = contract_last(rows, own_ref[...])
    out_ref[:, units:] = contract_last(rows, sib_ref[...])


def expert_body(
    rows_ref, grad_act_ref, gate_hbm, gate_sib_hbm, up_hbm, up_sib_hbm, down_hbm, down_sib_hbm,
    out_ref, gate_ref, up_ref, down_ref, gate_pre_ref, up_pre_ref, act_ref, grad_gate_ref,
    grad_up_ref, dots_ref, sems,
):
    width = rows_ref.shape[1]
    units = gate_ref.shape[2]
    slots = rows_ref.shape[0]
    copies = []
    order = (
        (gate_hbm, gate_ref, 0), (up_hbm, up_ref, 0), (gate_sib_hbm, gate_ref, 1),
        (up_sib_hbm, up_ref, 1), (down_hbm, down_ref, 0), (down_sib_hbm, down_ref, 1),
    )
    for index, (source, target, half) in enumerate(order):
        copies.append(pltpu.make_async_copy(source, target.at[half], sems.at[index]))
        copies[-1].start()
    rows = rows_ref[...]
    dots_ref[...] = jnp.zeros(dots_ref.shape, F32)
    tall = 16
    for half in range(2):
        copies[2 * half].wait()
        gate_pre_ref[...] = jnp.dot(rows, gate_ref[half], preferred_element_type=F32)
        copies[2 * half + 1].wait()
        up_pre_ref[...] = jnp.dot(rows, up_ref[half], preferred_element_type=F32)

        def chunk(r, carry):
            at = pl.ds(pl.multiple_of(r * tall, tall), tall)
            dots = dots_ref[at]
            for c in range(units // LANES):
                lanes = slice(c * LANES, (c + 1) * LANES)
                far = slice(half * units + c * LANES, half * units + (c + 1) * LANES)
                gate_pre = gate_pre_ref[at, lanes]
                up_pre = up_pre_ref[at, lanes]
                grad_act = grad_act_ref[at, far]
                sigma = jax.nn.sigmoid(gate_pre)
                gated = gate_pre * sigma
                act = (gated * up_pre).astype(BF16)
                act_ref[half, at, lanes] = act
                grad_gate_ref[half, at, lanes] = (
                    grad_act * up_pre * sigma * (1.0 + gate_pre * (1.0 - sigma))
                ).astype(BF16)
                grad_up_ref[half, at, lanes] = (grad_act * gated).astype(BF16)
                dots = dots + act.astype(F32) * grad_act
            dots_ref[at] = dots
            return carry

        lax.fori_loop(0, slots // tall, chunk, 0)
    copies[4].wait()
    share = jnp.dot(act_ref[0], down_ref[0], preferred_element_type=F32)
    copies[5].wait()
    share = share + jnp.dot(act_ref[1], down_ref[1], preferred_element_type=F32)
    out_ref[:, 0:width] = share.astype(BF16)
    share = contract_last(grad_gate_ref[0], gate_ref[0]) + contract_last(grad_up_ref[0], up_ref[0])
    share = share + contract_last(grad_gate_ref[1], gate_ref[1])
    share = share + contract_last(grad_up_ref[1], up_ref[1])
    out_ref[:, width : 2 * width] = share.astype(BF16)
    dots = jnp.broadcast_to(jnp.sum(dots_ref[...], axis=1, keepdims=True), (slots, LANES))
    high = dots.astype(BF16).astype(F32)
    lane = lax.broadcasted_iota(jnp.int32, (slots, LANES), 1)
    out_ref[:, 2 * width :] = jnp.where(lane == 0, high, dots - high).astype(BF16)


def combine_body(back_ref, tokens_ref, out_ref):
    slots = back_ref.shape[0]
    width = (back_ref.shape[1] - LANES) // 2
    info = tokens_ref[:, width:].astype(F32)
    first, second = slot_maps(info, slots)
    back = back_ref[:, 0:width]
    total = jnp.zeros((info.shape[0], width), F32)
    for part in range(2):
        weighted = first * info[:, 2 + part : 3 + part] + second * info[:, 4 + part : 5 + part]
        total = total + jnp.dot(weighted.astype(BF16), back, preferred_element_type=F32)
    out_ref[:, 0:width] = total.astype(BF16)
    both = (first + second).astype(BF16)
    out_ref[:, width : 2 * width] = jnp.dot(
        both, back_ref[:, width : 2 * width], preferred_element_type=F32
    ).astype(BF16)
    lane = lax.broadcasted_iota(jnp.int32, (info.shape[0], LANES), 1)
    for k, chosen in enumerate((first, second)):
        dots = jnp.dot(chosen.astype(BF16), back_ref[:, 2 * width :], preferred_element_type=F32)
        dots = jnp.broadcast_to(dots[:, 0:1] + dots[:, 1:2], dots.shape)
        high = dots.astype(BF16).astype(F32)
        start = 2 * width + k * LANES
        out_ref[:, start : start + LANES] = jnp.where(lane == 0, high, dots - high).astype(BF16)


def finish_body(
    back_ref, hidden_ref, gain_ref, cotangent_ref, scores_ref, layer_ref, grad_ref, dots_ref
):
    width = hidden_ref.shape[1]
    total = back_ref[0].astype(F32)
    for c in range(1, back_ref.shape[0]):
        total = total + back_ref[c].astype(F32)
    hidden = hidden_ref[...]
    layer_ref[...] = (hidden + total[:, 0:width]).astype(BF16)
    scale = lax.rsqrt(jnp.mean(hidden * hidden, axis=1, keepdims=True) + 1e-05)
    scaled = total[:, width : 2 * width] * gain_ref[...]
    outer = cotangent_ref[...].astype(F32)
    grad_ref[...] = (
        outer
        + scale * scaled
        - hidden * (scale * scale * scale) * jnp.mean(hidden * scaled, axis=1, keepdims=True)
    )
    for k in range(2):
        start = 2 * width + k * LANES
        dots = total[:, start : start + 1] + total[:, start + 1 : start + 2]
        dots_ref[:, k : k + 1] = dots / scores_ref[:, k : k + 1]


def make_per_device(interpret):
    def call(body, name, outs, ins, scratch=(), operands=(), **options):
        params = {}
        if options:
            body = partial(body, **options)
        return pl.pallas_call(
            body,
            out_shape=outs,
            in_specs=ins,
            out_specs=jax.tree.map(lambda _: VMEM, outs),
            scratch_shapes=list(scratch),
            interpret=interpret,
            name=name,
            compiler_params=pltpu.CompilerParams(vmem_limit_bytes=60 * 1024 * 1024),
            **params,
        )(*operands)

    def per_device(
        mixer_input, mixer_gate, step_low, step_proj, step_bias, decay_rate, input_coef,
        output_coef, conv_taps, conv_bias, skip_gain, out_weight, residual, norm_gain,
        expert_ids, gate_scores, gate_weight, up_weight, down_weight, cotangent,
    ):
        length, channels = mixer_input.shape
        count = decay_rate.shape[0]
        tok_rows, width = residual.shape
        units = gate_weight.shape[2]
        experts = lax.axis_size("exp")
        depth = lax.axis_size("z")
        ranks = depth * lax.axis_size("core")
        slots = 2 * experts * depth
        stride = 2 * depth
        swap = [(0, 1), (1, 0)]
        shape = jax.ShapeDtypeStruct

        def sibling(value):
            return lax.ppermute(value, "core", swap)

        def exchange(rows, axis):
            return lax.all_to_all(rows, axis, split_axis=0, concat_axis=0, tiled=True)

        grad_rows, info = call(
            prepare_body, "prepare",
            (shape((tok_rows, 2 * width + LANES), BF16), shape((tok_rows, LANES), BF16)),
            [VMEM] * 3, operands=(expert_ids, gate_scores, cotangent), stride=stride,
        )
        block_rows = lax.all_gather(grad_rows, "exp", axis=0, tiled=True)

        halo = 8
        tail = lax.ppermute(
            mixer_input[length - halo :], ("z", "core"), [(i, i + 1) for i in range(ranks - 1)]
        )
        gates = (gate_weight[0], sibling(gate_weight[0]))
        ups = (up_weight[0], sibling(up_weight[0]))
        downs = (down_weight[0], sibling(down_weight[0]))

        rows = shape((length, channels), F32)
        summary, step, inner = call(
            local_state_body, "local_state", (shape((count + 8, channels), F32), rows, rows),
            [VMEM] * 9,
            (pltpu.VMEM((length + halo, channels), F32), pltpu.VMEM((length, channels), F32)),
            (
                mixer_input, tail, step_low, step_proj, step_bias[None], decay_rate, input_coef,
                conv_taps, conv_bias[None],
            ),
        )
        gathered = lax.all_gather(summary, ("z", "core"), axis=0)
        mine = lax.axis_index(("z", "core")).astype(jnp.int32).reshape(1)
        share = call(
            readout_body, "readout", shape((length, width), BF16), [SMEM] + [VMEM] * 9,
            (pltpu.VMEM((length, channels), F32), pltpu.VMEM((length, channels), F32)),
            (
                mine, gathered, decay_rate, input_coef, output_coef, step, inner,
                skip_gain[None], mixer_gate, out_weight,
            ),
        )
        shares = exchange(share, "exp").reshape(experts, tok_rows, width)
        hidden, send = call(
            norm_body, "norm",
            (shape((tok_rows, width), F32), shape((depth, tok_rows, width + LANES), BF16)),
            [VMEM] * 4, operands=(shares, residual, norm_gain[None], info),
        )
        tokens = exchange(send.reshape(depth * tok_rows, width + LANES), "z")
        packed = call(pack_body, "pack", shape((slots, width), BF16), [VMEM], operands=(tokens,))
        rows_x = exchange(packed, "exp")

        expert = lax.axis_index("exp").astype(jnp.int32).reshape(1)
        chosen = call(
            select_body, "select", shape((2 * experts, width), BF16), [SMEM, VMEM],
            operands=(expert, block_rows), stride=stride,
        )
        rows_d = lax.all_gather(chosen, "z", axis=0, tiled=True)
        grad_act = call(
            grad_act_body, "grad_act", shape((slots, 2 * units), F32), [VMEM] * 3,
            operands=(rows_d,) + downs, depth=depth,
        )
        result = call(
            expert_body, "expert", shape((slots, 2 * width + LANES), BF16),
            [VMEM] * 2 + [pl.BlockSpec(memory_space=pl.ANY)] * 6,
            (
                pltpu.VMEM((2, width, units), BF16),
                pltpu.VMEM((2, width, units), BF16),
                pltpu.VMEM((2, units, width), BF16),
                pltpu.VMEM((slots, units), F32),
                pltpu.VMEM((slots, units), F32),
                pltpu.VMEM((2, slots, units), BF16),
                pltpu.VMEM((2, slots, units), BF16),
                pltpu.VMEM((2, slots, units), BF16),
                pltpu.VMEM((slots, LANES), F32),
                pltpu.SemaphoreType.DMA((6,)),
            ),
            (rows_x, grad_act) + gates + ups + downs,
        )
        back = exchange(result, "exp")
        shares_back = call(
            combine_body, "combine", shape((depth * tok_rows, 2 * width + 2 * LANES), BF16),
            [VMEM] * 2, operands=(back, tokens),
        )
        mine_back = exchange(shares_back, "z").reshape(depth, tok_rows, 2 * width + 2 * LANES)
        return call(
            finish_body, "finish",
            (
                shape((tok_rows, width), BF16), shape((tok_rows, width), F32),
                shape(gate_scores.shape, F32),
            ),
            [VMEM] * 5,
            operands=(mine_back, hidden, norm_gain[None], cotangent, gate_scores),
        )

    return per_device


def solution(mesh, interpret=False):
    ctx, exp = mesh.devices.shape
    split = Mesh(mesh.devices.reshape(ctx // 2, 2, exp), ("z", "core", "exp"))
    both = ("z", "core")
    rows = P(("z", "core", "exp"), None)
    in_specs = (
        P(both, "exp"),
        P(both, "exp"),
        P(both, None),
        P(None, "exp"),
        P("exp"),
        P(None, "exp"),
        P(None, both),
        P(None, both),
        P(None, "exp"),
        P("exp"),
        P("exp"),
        P("exp", None),
        rows,
        P(),
        rows,
        rows,
        P("exp", None, both),
        P("exp", None, both),
        P("exp", both, None),
        rows,
    )
    return jax.shard_map(
        make_per_device(interpret),
        mesh=split,
        in_specs=in_specs,
        out_specs=(rows, rows, rows),
        check_vma=False,
    )
```

time: 228 us -> 200 us (0.88)
  waiting for transfers between devices: 101 us -> 19.7 us
  blocking collectives: 25 us -> 92.9 us
  Pallas kernels: 8.03 us -> 47.7 us
  matrix products: 38.2 us -> 0 us
  starting transfers between devices: 39.1 us -> 17.1 us
  between operations: 1.13 us -> 14.1 us
  local copies, waits for them, and re-layouts: 12.6 us -> 7.05 us
    all_to_all x5 -> x2, waiting for transfers between devices: 101 us -> 2.03 us  [exchange(): return lax.all_to_all(rows, axis, split_axis=0, concat_axis=0, tiled=True)]
    all_to_all x0 -> x3, blocking collectives: none -> 68.9 us  [exchange(): return lax.all_to_all(rows, axis, split_axis=0, concat_axis=0, tiled=True)]
    pallas_call x2 -> x10, Pallas kernels: 8.03 us -> 47.7 us  [call(): pl.pallas_call(body, out_shape=outs, in_specs=ins, out_specs=jax.tree.map...]
    dot_general x16 -> x0, matrix products: 38.2 us -> none  [the longest x6 20.1 us: contract_last(): lax.dot_general(left, right, (((1,), (1,)), ((), ())), preferred_element_...]
    all_to_all x5 -> x2, starting transfers between devices: 36.7 us -> 14.1 us  [exchange(): return lax.all_to_all(rows, axis, split_axis=0, concat_axis=0, tiled=True)]
    all_gather x0 -> x2, waiting for transfers between devices: none -> 15.2 us  [the longest x1 9.2 us: per_device(): rows_d = lax.all_gather(chosen, 'z', axis=0, tiled=True)]
    all_to_all x6 -> x0, local copies, waits for them, and re-layouts: 6.82 us -> none  [exchange(): lax.all_to_all(slots, ('z', 'exp'), split_axis=0, concat_axis=0, tiled=True)]
    ppermute x1, waiting for transfers between devices: 0.01 us -> 2.44 us  [per_device(): lax.ppermute(mixer_input[length - halo:], ('z', 'core'), [(i, i + 1) for...]
  transfers between devices with their start and end apart: 9 -> 8, of which waited for: 5 -> 4; matrix products, arithmetic and copies ran while one was open for 16% -> 0% of each run, Pallas kernels for 0% -> 11%
where the time goes in v1:
time: 200 us; the launch traced here: 199 us
  blocking collectives  92.9 us (46%)
  Pallas kernels  47.7 us (24%)
  waiting for transfers between devices  19.7 us (10%)
  starting transfers between devices  17.1 us (9%)
  between operations  14.1 us (7%)
  local copies, waits for them, and re-layouts  7.05 us (4%)
    all_to_all x3, blocking collectives, exchange(): return lax.all_to_all(rows, axis, split_axis=0, concat_axis=0, tiled=True)  68.9 us
    pallas_call x10, Pallas kernels, call(): pl.pallas_call(body, out_shape=outs, in_specs=ins, out_specs=jax.tree.map...  47.7 us
    all_gather x1, blocking collectives, per_device(): gathered = lax.all_gather(summary, ('z', 'core'), axis=0)  24 us
    all_to_all x2, starting transfers between devices, exchange(): return lax.all_to_all(rows, axis, split_axis=0, concat_axis=0, tiled=True)  14.1 us
    all_gather x1, waiting for transfers between devices, per_device(): rows_d = lax.all_gather(chosen, 'z', axis=0, tiled=True)  9.2 us
    all_gather x1, waiting for transfers between devices, per_device(): block_rows = lax.all_gather(grad_rows, 'exp', axis=0, tiled=True)  6 us
    unnamed x8, local copies, waits for them, and re-layouts  5.06 us
  transfers between devices with their start and end apart: 8, of which 4 were waited for; matrix products, arithmetic and copies ran while one was open for 0% of the time, Pallas kernels for 11%

profile of v1, /device:TPU:2, one launch (start us, length us, event | category | flops | bytes accessed | tf_op | source)
XLA Modules:
  0.0 198.6 jit_solution(14853133374333823340)
XLA Ops:
  7.2 1.3 copy.24.scores_ref
  8.5 1.3 copy.23.ids_ref
  9.9 1.5 prepare.1
  12.8 2.3 %collective-permute-start = (bf16[8,256]{1,0:T(8,128)(2,1)S(1)}, bf16[8,256]{1,0:T(8,128)(2,1)S(1)}, u32[]{:S(2)}, u32[]{:S(2)}) collective-permute-start(bf16[8,256]{1,0:T(8,128)(2,1)S(1)} %slice.3), channel_id=1, source_target_pairs={{0,16},{16,32},{32,48},{48,64},{64,80},{80,96},{96,112},{112,128},... | collective-permute-start | bytes 12296 | tf_op jit(solution)/shard_map/ppermute | solution.py:361
  15.1 2.4 %collective-permute-done.halo_ref = bf16[8,256]{1,0:T(8,128)(2,1)S(1)} collective-permute-done((bf16[8,256]{1,0:T(8,128)(2,1)S(1)}, bf16[8,256]{1,0:T(8,128)(2,1)S(1)}, u32[]{:S(2)}, u32[]{:S(2)}) %collective-permute-start) | collective-permute-done | bytes 4128 | tf_op jit(solution)/shard_map/ppermute | solution.py:361
  18.2 3.3 %local_state.1 = (f32[24,256]{1,0:T(8,128)}, f32[128,256]{1,0:T(8,128)}, f32[128,256]{1,0:T(8,128)}) custom-call(bf16[128,256]{1,0:T(8,128)(2,1)} %x_ref.1, bf16[8,256]{1,0:T(8,128)(2,1)} %copy-done.2, bf16[128,128]{1,0:T(8,128)(2,1)} %low_ref.1, bf16[128,256]{1,0:T(8,128)(2,1)} %proj_ref.1, f32[1,256]{1,0:T(1,128)} %bitcast.35, f32[16,256]{1,0:T(8,128)} %decay_ref.3, ...), custom_call_target="tpu_custom_call" | custom-call | tf_op jit(solution)/shard_map/local_state/pallas_call | solution.py:318
  21.5 24.0 %all-gather = f32[384,256]{1,0:T(8,128)} all-gather(f32[24,256]{1,0:T(8,128)} %get-tuple-element.10), channel_id=2, replica_groups=mesh['z'=8,'core'=2,'exp'=16] {'z','core'}, dimensions={0}, use_global_device_ids=true | all-gather | bytes 417792 | tf_op jit(solution)/shard_map/all_gather | solution.py:378
  45.5 4.8 %readout.1 = bf16[128,2048]{1,0:T(8,128)(2,1)} custom-call(s32[1]{0:T(128)} %bitcast.mine_ref, f32[16,24,256]{2,1,0:T(8,128)} %bitcast.32, f32[16,256]{1,0:T(8,128)} %decay_ref.3, f32[16,128]{1,0:T(8,128)} %bcoef_ref.3, f32[16,128]{1,0:T(8,128)} %ccoef_ref.1, f32[128,256]{1,0:T(8,128)} %get-tuple-element.11.step_ref, ...), custom_call_target="tpu_custom_call" | custom-call | tf_op jit(solution)/shard_map/readout/pallas_call | solution.py:318
  50.2 7.5 %all-to-all-start = ((bf16[16,8,2048]{2,1,0:T(8,128)(2,1)}), bf16[16,8,2048]{2,1,0:T(8,128)(2,1)S(1)}, u32[]{:S(2)}, u32[]{:S(2)}) async-start(bf16[16,8,2048]{2,1,0:T(8,128)(2,1)} %bitcast.31), calls=%async_computation | async-start | bytes 1048576 | tf_op jit(solution)/shard_map/all_to_all | solution.py:351
  57.7 6.0 %all-gather.4.cloned.1.call-done.gathered_ref = bf16[128,4224]{1,0:T(8,128)(2,1)} async-done(((bf16[8,4224]{1,0:T(8,128)(2,1)}), bf16[128,4224]{1,0:T(8,128)(2,1)}) %all-gather.4.cloned.1.call-update) | async-done | bytes 1081360 | tf_op jit(solution)/shard_map/all_gather | solution.py:358
  63.7 2.4 %select.1 = bf16[32,2048]{1,0:T(8,128)(2,1)} custom-call(s32[1]{0:T(128)} %bitcast.10.mine_ref, bf16[128,4224]{1,0:T(8,128)(2,1)} %all-gather.4.cloned.1.call-done.gathered_ref), custom_call_target="tpu_custom_call" | custom-call | tf_op jit(solution)/shard_map/select/pallas_call | solution.py:318
  66.2 2.0 %all-to-all-done.shares_ref = bf16[16,8,2048]{2,1,0:T(8,128)(2,1)S(1)} async-done(((bf16[16,8,2048]{2,1,0:T(8,128)(2,1)}), bf16[16,8,2048]{2,1,0:T(8,128)(2,1)S(1)}, u32[]{:S(2)}, u32[]{:S(2)}) %all-to-all-start) | async-done | bytes 524320 | tf_op jit(solution)/shard_map/all_to_all | solution.py:351
  69.0 2.0 %norm.1 = (f32[8,2048]{1,0:T(8,128)}, bf16[8,8,2176]{2,1,0:T(8,128)(2,1)}) custom-call(bf16[16,8,2048]{2,1,0:T(8,128)(2,1)} %copy-done.1, bf16[8,2048]{1,0:T(8,128)(2,1)} %residual_ref.1, f32[1,2048]{1,0:T(1,128)} %bitcast.33, bf16[8,128]{1,0:T(8,128)(2,1)} %get-tuple-element.13.info_ref), custom_call_target="tpu_custom_call" | custom-call | tf_op jit(solution)/shard_map/norm/pallas_call | solution.py:318
  71.0 19.3 %all_to_all.48 = bf16[8,8,2176]{2,1,0:T(8,128)(2,1)} all-to-all(bf16[8,8,2176]{2,1,0:T(8,128)(2,1)} %get-tuple-element.14), channel_id=1, replica_groups=mesh['z'=8,'core'=2,'exp'=16] {'z'}, dimensions={0} | all-to-all | bytes 557056 | tf_op jit(solution)/shard_map/all_to_all | solution.py:351
  90.3 2.5 %pack.1 = bf16[256,2048]{1,0:T(8,128)(2,1)} custom-call(bf16[64,2176]{1,0:T(8,128)(2,1)} %bitcast.28), custom_call_target="tpu_custom_call" | custom-call | tf_op jit(solution)/shard_map/pack/pallas_call | solution.py:318
  92.8 6.6 %all-to-all-start.2 = ((bf16[16,16,2048]{2,1,0:T(8,128)(2,1)}), bf16[16,16,2048]{2,1,0:T(8,128)(2,1)S(1)}, u32[]{:S(2)}, u32[]{:S(2)}) async-start(bf16[16,16,2048]{2,1,0:T(8,128)(2,1)} %bitcast.23), calls=%async_computation.2 | async-start | bytes 2097152 | tf_op jit(solution)/shard_map/all_to_all | solution.py:351
  99.4 9.2 %all-gather.6.cloned.1.call-done.rows_ref = bf16[256,2048]{1,0:T(8,128)(2,1)} async-done(((bf16[32,2048]{1,0:T(8,128)(2,1)}), bf16[256,2048]{1,0:T(8,128)(2,1)}) %all-gather.6.cloned.1.call-update) | async-done | bytes 1048592 | tf_op jit(solution)/shard_map/all_gather | solution.py:403
  108.6 7.3 %grad_act.1.grad_act_ref = f32[256,1792]{1,0:T(8,128)} custom-call(bf16[256,2048]{1,0:T(8,128)(2,1)} %all-gather.6.cloned.1.call-done.rows_ref, bf16[896,2048]{1,0:T(8,128)(2,1)} %bitcast.18, bf16[896,2048]{1,0:T(8,128)(2,1)} %collective-permute-done.1.sib_ref.down_sib_hbm), custom_call_target="tpu_custom_call" | custom-call | tf_op jit(solution)/shard_map/grad_act/pallas_call | solution.py:318
  116.9 18.7 %expert.1 = bf16[256,4224]{1,0:T(8,128)(2,1)} custom-call(bf16[256,2048]{1,0:T(8,128)(2,1)} %bitcast.22, f32[256,1792]{1,0:T(8,128)} %grad_act.1.grad_act_ref, bf16[2048,896]{1,0:T(8,128)(2,1)} %bitcast.25, bf16[2048,896]{1,0:T(8,128)(2,1)} %collective-permute-done.2.gate_sib_hbm, bf16[2048,896]{1,0:T(8,128)(2,1)} %bitcast.27, ...), custom_call_target="tpu_custom_call" | custom-call | tf_op jit(solution)/shard_map/expert/pallas_call | solution.py:318
  135.6 30.9 %all_to_all.49 = bf16[16,16,4224]{2,1,0:T(8,128)(2,1)} all-to-all(bf16[16,16,4224]{2,1,0:T(8,128)(2,1)} %bitcast.20), channel_id=1, replica_groups=mesh['z'=8,'core'=2,'exp'=16] {'exp'}, dimensions={0} | all-to-all | bytes 4325376 | tf_op jit(solution)/shard_map/all_to_all | solution.py:351
  166.5 3.3 %combine.1 = bf16[64,4352]{1,0:T(8,128)(2,1)} custom-call(bf16[256,4224]{1,0:T(8,128)(2,1)} %bitcast.21, bf16[64,2176]{1,0:T(8,128)(2,1)} %bitcast.29), custom_call_target="tpu_custom_call" | custom-call | tf_op jit(solution)/shard_map/combine/pallas_call | solution.py:318
  169.9 18.7 %all_to_all.50.back_ref = bf16[8,8,4352]{2,1,0:T(8,128)(2,1)} all-to-all(bf16[8,8,4352]{2,1,0:T(8,128)(2,1)} %bitcast.30), channel_id=1, replica_groups=mesh['z'=8,'core'=2,'exp'=16] {'z'}, dimensions={0} | all-to-all | bytes 1114112 | tf_op jit(solution)/shard_map/all_to_all | solution.py:351
  188.6 1.9 finish.1
  190.5 1.3 copy.26
  (18 shorter events, 3.9 us)
Async XLA Ops:
  7.2 56.6 %all-gather.4.cloned.1.call-start = ((), (), s32[]{:S(2)}) async-start(), calls=%async_computation.5 | async-start | bytes 1148928 | tf_op jit(solution)/shard_map/all_gather | solution.py:358
  11.4 88.0 %collective-permute-start.1 = (bf16[896,2048]{1,0:T(8,128)(2,1)}, bf16[896,2048]{1,0:T(8,128)(2,1)}, u32[]{:S(2)}, u32[]{:S(2)}) collective-permute-start(bf16[896,2048]{1,0:T(8,128)(2,1)} %bitcast.17), channel_id=1, source_target_pairs={{0,16},{16,0},{1,17},{17,1},{2,18},{18,2},{3,19},{19,3},{4,20},{20... | collective-permute-start | bytes 11010056 | tf_op jit(solution)/shard_map/ppermute | solution.py:348
  11.5 104.4 %collective-permute-start.2 = (bf16[2048,896]{1,0:T(8,128)(2,1)}, bf16[2048,896]{1,0:T(8,128)(2,1)}, u32[]{:S(2)}, u32[]{:S(2)}) collective-permute-start(bf16[2048,896]{1,0:T(8,128)(2,1)} %bitcast.24), channel_id=1, source_target_pairs={{0,16},{16,0},{1,17},{17,1},{2,18},{18,2},{3,19},{19,3},{4,20},{20... | collective-permute-start | bytes 11010056 | tf_op jit(solution)/shard_map/ppermute | solution.py:348
  12.0 103.9 %collective-permute-start.3 = (bf16[2048,896]{1,0:T(8,128)(2,1)}, bf16[2048,896]{1,0:T(8,128)(2,1)}, u32[]{:S(2)}, u32[]{:S(2)}) collective-permute-start(bf16[2048,896]{1,0:T(8,128)(2,1)} %bitcast.26), channel_id=1, source_target_pairs={{0,16},{16,0},{1,17},{17,1},{2,18},{18,2},{3,19},{19,3},{4,20},{20... | collective-permute-start | bytes 11010056 | tf_op jit(solution)/shard_map/ppermute | solution.py:348
  12.8 4.8 %collective-permute-start = (bf16[8,256]{1,0:T(8,128)(2,1)S(1)}, bf16[8,256]{1,0:T(8,128)(2,1)S(1)}, u32[]{:S(2)}, u32[]{:S(2)}) collective-permute-start(bf16[8,256]{1,0:T(8,128)(2,1)S(1)} %slice.3), channel_id=1, source_target_pairs={{0,16},{16,32},{32,48},{48,64},{64,80},{80,96},{96,112},{112,128},... | collective-permute-start | bytes 12296 | tf_op jit(solution)/shard_map/ppermute | solution.py:361
  17.6 0.6 copy-start.2
  50.2 18.0 %all-to-all-start = ((bf16[16,8,2048]{2,1,0:T(8,128)(2,1)}), bf16[16,8,2048]{2,1,0:T(8,128)(2,1)S(1)}, u32[]{:S(2)}, u32[]{:S(2)}) async-start(bf16[16,8,2048]{2,1,0:T(8,128)(2,1)} %bitcast.31), calls=%async_computation | async-start | bytes 1048576 | tf_op jit(solution)/shard_map/all_to_all | solution.py:351
  57.7 50.9 %all-gather.6.cloned.1.call-start = ((), (), s32[]{:S(2)}) async-start(), calls=%async_computation.6 | async-start | bytes 1179648 | tf_op jit(solution)/shard_map/all_gather | solution.py:403
  68.2 0.8 copy-start.1
  92.8 23.1 %all-to-all-start.2 = ((bf16[16,16,2048]{2,1,0:T(8,128)(2,1)}), bf16[16,16,2048]{2,1,0:T(8,128)(2,1)S(1)}, u32[]{:S(2)}, u32[]{:S(2)}) async-start(bf16[16,16,2048]{2,1,0:T(8,128)(2,1)} %bitcast.23), calls=%async_computation.2 | async-start | bytes 2097152 | tf_op jit(solution)/shard_map/all_to_all | solution.py:351
  115.9 1.0 copy-start
Sparse Core Ops, SparseCore 0:
  11.5 52.1 all-gather.3
  66.3 42.2 all-gather.5

commit v2 on v1

v2 whole, which is shorter than its diff:
```python
from functools import partial

import jax
import jax.numpy as jnp
from jax import lax
from jax.experimental import pallas as pl
from jax.experimental.pallas import tpu as pltpu
from jax.sharding import Mesh
from jax.sharding import PartitionSpec as P

BF16 = jnp.bfloat16
F32 = jnp.float32
VMEM = pl.BlockSpec(memory_space=pltpu.VMEM)
SMEM = pl.BlockSpec(memory_space=pltpu.SMEM)
GROUP = 8
LANES = 128


def contract_last(left, right):
    return lax.dot_general(left, right, (((1,), (1,)), ((), ())), preferred_element_type=F32)


def contract_first(left, right):
    return lax.dot_general(left, right, (((0,), (0,)), ((), ())), preferred_element_type=F32)


def column(row):
    count = row.shape[1]
    lane = lax.broadcasted_iota(jnp.int32, (count, count), 1)
    sub = lax.broadcasted_iota(jnp.int32, (count, count), 0)
    spread = jnp.where(lane == sub, jnp.broadcast_to(row, (count, count)), 0.0)
    return jnp.sum(spread, axis=1, keepdims=True)


def parts_of(value, count):
    parts = []
    for _ in range(count):
        part = value.astype(BF16).astype(F32)
        parts.append(part)
        value = value - part
    return parts


def advance(state, steps, drives, coef, rate, k):
    shape = rate.shape
    factor = jnp.exp(jnp.broadcast_to(steps[k : k + 1], shape) * rate)
    push = jnp.broadcast_to(drives[k : k + 1], shape) * jnp.broadcast_to(coef[:, k : k + 1], shape)
    return factor * state + push


def convolved(pad_ref, taps_ref, bias_ref, first, rows):
    taps = taps_ref.shape[0]
    filtered = bias_ref[...]
    for k in range(taps):
        start = first - taps + 1 + k
        filtered = filtered + taps_ref[k : k + 1] * pad_ref[start : start + rows]
    return jax.nn.silu(filtered)


def token_info(ids_ref, scores_ref, stride):
    rows = ids_ref.shape[1]
    shape = (rows, LANES)
    row = lax.broadcasted_iota(jnp.int32, shape, 0)
    lane = lax.broadcasted_iota(jnp.int32, shape, 1)
    ids = [jnp.broadcast_to(column(ids_ref[k : k + 1].astype(F32)), shape) for k in range(2)]
    fields = []
    for k in range(2):
        slot = jnp.zeros(shape, F32)
        for back in range(1, rows):
            for other in ids:
                hit = (pltpu.roll(other, back, 0) == ids[k]) & (row >= back)
                slot = slot + jnp.where(hit, 1.0, 0.0)
        fields.append(stride * ids[k] + slot)
    for k in range(2):
        fields += parts_of(jnp.broadcast_to(column(scores_ref[k : k + 1]), shape), 3)
    info = jnp.zeros(shape, F32)
    for place, field in enumerate(fields):
        info = jnp.where(lane == place, field, info)
    return info


def local_state_body(
    x_ref, low_ref, proj_ref, bias_ref, decay_ref, bcoef_ref, taps_ref, cbias_ref, ids_ref,
    scores_ref, cotangent_ref, late_ref, step_ref, inner_ref, extra_ref, pad_ref, drive_ref,
    *, stride,
):
    length, channels = x_ref.shape
    pad_ref[0:GROUP] = jnp.zeros((GROUP, channels), F32)
    pad_ref[GROUP:] = x_ref[...].astype(F32)
    inner = convolved(pad_ref, taps_ref, cbias_ref, GROUP, length)
    inner_ref[...] = inner
    pre = jnp.dot(low_ref[...], proj_ref[...], preferred_element_type=F32) + bias_ref[...]
    step = jnp.maximum(pre, 0.0) + jnp.log1p(jnp.exp(-jnp.abs(pre)))
    step_ref[...] = step
    drive_ref[...] = step * inner
    rate = -decay_ref[...]
    count = rate.shape[0]
    turn = bcoef_ref.shape[1] - GROUP

    def group(g, carry):
        state, coef = carry
        rows = pl.ds(pl.multiple_of(g * GROUP, GROUP), GROUP)
        steps = step_ref[rows]
        drives = drive_ref[rows]
        for k in range(GROUP):
            state = advance(state, steps, drives, coef, rate, k)
        return state, pltpu.roll(coef, turn, 1)

    first = (jnp.zeros(rate.shape, F32), pltpu.roll(bcoef_ref[...], turn, 1))
    state, _ = lax.fori_loop(1, length // GROUP, group, first)
    late_ref[0:count] = state
    late_ref[count:] = jnp.broadcast_to(
        jnp.sum(step[GROUP:], axis=0, keepdims=True), (GROUP, channels)
    )
    tokens = cotangent_ref.shape[0]
    info = token_info(ids_ref, scores_ref, stride)
    extra_ref[0:tokens, 0:LANES] = info.astype(BF16)
    extra_ref[0:tokens, LANES:] = jnp.zeros((tokens, channels - LANES), BF16)
    for b in range(cotangent_ref.shape[1] // channels):
        rows = slice((b + 1) * tokens, (b + 2) * tokens)
        extra_ref[rows] = cotangent_ref[:, b * channels : (b + 1) * channels]


def first_group_body(
    before_ref, x_ref, taps_ref, cbias_ref, step_ref, decay_ref, bcoef_ref, late_ref, extra_ref,
    send_ref, inner_ref, pad_ref,
):
    length = x_ref.shape[0]
    pad_ref[0:GROUP] = before_ref[length - GROUP :].astype(F32)
    pad_ref[GROUP:] = x_ref[0:GROUP].astype(F32)
    inner = convolved(pad_ref, taps_ref, cbias_ref, GROUP, GROUP)
    inner_ref[...] = inner
    steps = step_ref[0:GROUP]
    drives = steps * inner
    rate = -decay_ref[...]
    count = rate.shape[0]
    coef = bcoef_ref[...]
    state = jnp.zeros(rate.shape, F32)
    for k in range(GROUP):
        state = advance(state, steps, drives, coef, rate, k)
    after = late_ref[count : count + 1]
    state = jnp.exp(jnp.broadcast_to(after, rate.shape) * rate) * state + late_ref[0:count]
    high, low = parts_of(state, 2)
    send_ref[0:count] = high.astype(BF16)
    send_ref[count : 2 * count] = low.astype(BF16)
    total = jnp.broadcast_to(
        after + jnp.sum(steps, axis=0, keepdims=True), (GROUP, rate.shape[1])
    )
    high, low = parts_of(total, 2)
    sub = lax.broadcasted_iota(jnp.int32, total.shape, 0)
    total = jnp.where(sub == 0, high, low)
    extra = extra_ref[0:GROUP].astype(F32)
    send_ref[2 * count : 2 * count + 2 * GROUP] = jnp.concatenate([total, extra], 0).astype(BF16)
    send_ref[2 * count + 2 * GROUP :] = extra_ref[GROUP:]


def readout_body(
    mine_ref, gathered_ref, decay_ref, bcoef_ref, ccoef_ref, step_ref, inner_ref, first_ref,
    skip_ref, gate_ref, weight_ref, out_ref, info_ref, drive_ref, read_ref, inner_all_ref,
    tokens_ref,
):
    rate = -decay_ref[...]
    shape = rate.shape
    count, channels = shape
    length = step_ref.shape[0]
    ranks = gathered_ref.shape[0]
    mine = mine_ref[0]
    state = jnp.zeros(shape, F32)
    for c in range(ranks - 1):
        piece = gathered_ref[c, 0 : 2 * count].astype(F32)
        sums = gathered_ref[c, 2 * count : 2 * count + 2 * GROUP].astype(F32)
        total = jnp.broadcast_to(sums[0:1] + sums[1:2], shape)
        longer = jnp.exp(total * rate) * state + (piece[0:count] + piece[count:])
        state = jnp.where(c < mine, longer, state)
    inner_all_ref[...] = inner_ref[...]
    inner_all_ref[0:GROUP] = first_ref[...]
    drive_ref[...] = step_ref[...] * inner_all_ref[...]
    turn = bcoef_ref.shape[1] - GROUP

    def group(g, carry):
        state, bcoef, ccoef = carry
        rows = pl.ds(pl.multiple_of(g * GROUP, GROUP), GROUP)
        steps = step_ref[rows]
        drives = drive_ref[rows]
        reads = []
        for k in range(GROUP):
            state = advance(state, steps, drives, bcoef, rate, k)
            reads.append(
                jnp.sum(state * jnp.broadcast_to(ccoef[:, k : k + 1], shape), axis=0, keepdims=True)
            )
        read_ref[rows] = jnp.concatenate(reads, axis=0)
        return state, pltpu.roll(bcoef, turn, 1), pltpu.roll(ccoef, turn, 1)

    lax.fori_loop(0, length // GROUP, group, (state, bcoef_ref[...], ccoef_ref[...]))
    output = read_ref[...] + skip_ref[...] * inner_all_ref[...]
    output = output * jax.nn.silu(gate_ref[...].astype(F32))
    share = jnp.dot(output.astype(BF16), weight_ref[...], preferred_element_type=F32).astype(BF16)
    experts, tall, width = out_ref.shape
    rows = length // experts
    slots = tall - rows
    depth = slots // 2
    tokens = info_ref.shape[0] // depth
    core = lax.rem(mine, ranks // depth)
    start = 2 * count + GROUP
    for z in range(depth):
        at = slice(z * tokens, (z + 1) * tokens)
        place = z * (ranks // depth) + core
        extra = gathered_ref[place, 2 * count : 2 * count + 2 * GROUP].astype(F32)
        info_ref[at] = extra[GROUP:, 0:LANES]
        for b in range(width // channels):
            first = start + (b + 1) * tokens
            tokens_ref[at, b * channels : (b + 1) * channels] = gathered_ref[
                place, first : first + tokens
            ].astype(F32)
    info = info_ref[...]
    chosen = slot_maps(info, experts * slots)
    packed = jnp.zeros((experts * slots, width), F32)
    for k in range(2):
        at = 2 + 3 * k
        score = info[:, at : at + 1] + info[:, at + 1 : at + 2] + info[:, at + 2 : at + 3]
        grad_rows = (score * tokens_ref[...]).astype(BF16)
        packed = packed + contract_first(chosen[k].astype(BF16), grad_rows)
    packed = packed.astype(BF16)
    for e in range(experts):
        out_ref[e, 0:slots] = packed[e * slots : (e + 1) * slots]
        out_ref[e, slots:] = share[e * rows : (e + 1) * rows]


def slot_maps(info, slots):
    lane = lax.broadcasted_iota(jnp.int32, (info.shape[0], slots), 1)
    block = lax.broadcasted_iota(jnp.int32, (info.shape[0], slots), 0) // GROUP
    maps = []
    for k in range(2):
        base = jnp.broadcast_to(info[:, k : k + 1].astype(jnp.int32), lane.shape)
        maps.append(jnp.where(lane == base + 2 * block, 1.0, 0.0))
    return maps


def norm_body(shares_ref, residual_ref, gain_ref, hidden_ref, send_ref):
    rows = residual_ref.shape[0]
    start = shares_ref.shape[1] - rows
    total = shares_ref[0, start:].astype(F32)
    for c in range(1, shares_ref.shape[0]):
        total = total + shares_ref[c, start:].astype(F32)
    hidden = residual_ref[...].astype(F32) + total
    hidden_ref[...] = hidden
    scale = lax.rsqrt(jnp.mean(hidden * hidden, axis=1, keepdims=True) + 1e-05)
    normed = (hidden * scale * gain_ref[...]).astype(BF16)
    for c in range(send_ref.shape[0]):
        send_ref[c] = normed


def pack_body(tokens_ref, info_ref, slots_ref):
    first, second = slot_maps(info_ref[...], slots_ref.shape[0])
    slots_ref[...] = contract_first((first + second).astype(BF16), tokens_ref[...]).astype(BF16)


def grad_act_body(shares_ref, own_ref, sib_ref, out_ref, rows_ref):
    units = own_ref.shape[0]
    experts = shares_ref.shape[0]
    slots = rows_ref.shape[0] // experts
    for e in range(experts):
        rows_ref[e * slots : (e + 1) * slots] = shares_ref[e, 0:slots]
    rows = rows_ref[...]
    out_ref[:, 0:units] = contract_last(rows, own_ref[...])
    out_ref[:, units:] = contract_last(rows, sib_ref[...])


def expert_body(
    rows_ref, grad_act_ref, gate_hbm, gate_sib_hbm, up_hbm, up_sib_hbm, down_hbm, down_sib_hbm,
    out_ref, gate_ref, up_ref, down_ref, gate_pre_ref, up_pre_ref, act_ref, grad_gate_ref,
    grad_up_ref, dots_ref, sems,
):
    width = rows_ref.shape[1]
    units = gate_ref.shape[2]
    slots = rows_ref.shape[0]
    copies = []
    order = (
        (gate_hbm, gate_ref, 0), (up_hbm, up_ref, 0), (gate_sib_hbm, gate_ref, 1),
        (up_sib_hbm, up_ref, 1), (down_hbm, down_ref, 0), (down_sib_hbm, down_ref, 1),
    )
    for index, (source, target, half) in enumerate(order):
        copies.append(pltpu.make_async_copy(source, target.at[half], sems.at[index]))
        copies[-1].start()
    rows = rows_ref[...]
    dots_ref[...] = jnp.zeros(dots_ref.shape, F32)
    tall = 16
    for half in range(2):
        copies[2 * half].wait()
        gate_pre_ref[...] = jnp.dot(rows, gate_ref[half], preferred_element_type=F32)
        copies[2 * half + 1].wait()
        up_pre_ref[...] = jnp.dot(rows, up_ref[half], preferred_element_type=F32)

        def chunk(r, carry):
            at = pl.ds(pl.multiple_of(r * tall, tall), tall)
            dots = dots_ref[at]
            for c in range(units // LANES):
                lanes = slice(c * LANES, (c + 1) * LANES)
                far = slice(half * units + c * LANES, half * units + (c + 1) * LANES)
                gate_pre = gate_pre_ref[at, lanes]
                up_pre = up_pre_ref[at, lanes]
                grad_act = grad_act_ref[at, far]
                sigma = jax.nn.sigmoid(gate_pre)
                gated = gate_pre * sigma
                act = (gated * up_pre).astype(BF16)
                act_ref[half, at, lanes] = act
                grad_gate_ref[half, at, lanes] = (
                    grad_act * up_pre * sigma * (1.0 + gate_pre * (1.0 - sigma))
                ).astype(BF16)
                grad_up_ref[half, at, lanes] = (grad_act * gated).astype(BF16)
                dots = dots + act.astype(F32) * grad_act
            dots_ref[at] = dots
            return carry

        lax.fori_loop(0, slots // tall, chunk, 0)
    copies[4].wait()
    share = jnp.dot(act_ref[0], down_ref[0], preferred_element_type=F32)
    copies[5].wait()
    share = share + jnp.dot(act_ref[1], down_ref[1], preferred_element_type=F32)
    out_ref[:, 0:width] = share.astype(BF16)
    share = contract_last(grad_gate_ref[0], gate_ref[0]) + contract_last(grad_up_ref[0], up_ref[0])
    share = share + contract_last(grad_gate_ref[1], gate_ref[1])
    share = share + contract_last(grad_up_ref[1], up_ref[1])
    out_ref[:, width : 2 * width] = share.astype(BF16)
    dots = jnp.broadcast_to(jnp.sum(dots_ref[...], axis=1, keepdims=True), (slots, LANES))
    high = dots.astype(BF16).astype(F32)
    lane = lax.broadcasted_iota(jnp.int32, (slots, LANES), 1)
    out_ref[:, 2 * width :] = jnp.where(lane == 0, high, dots - high).astype(BF16)


def combine_body(back_ref, info_ref, out_ref):
    slots = back_ref.shape[0]
    width = (back_ref.shape[1] - LANES) // 2
    info = info_ref[...]
    tokens = info.shape[0]
    first, second = slot_maps(info, slots)
    weights = [
        first * info[:, 2 + part : 3 + part] + second * info[:, 5 + part : 6 + part]
        for part in range(2)
    ]
    total = jnp.dot(
        jnp.concatenate(weights, 0).astype(BF16), back_ref[:, 0:width], preferred_element_type=F32
    )
    out_ref[:, 0:width] = (total[0:tokens] + total[tokens:]).astype(BF16)
    both = (first + second).astype(BF16)
    out_ref[:, width : 2 * width] = jnp.dot(
        both, back_ref[:, width : 2 * width], preferred_element_type=F32
    ).astype(BF16)
    lane = lax.broadcasted_iota(jnp.int32, (tokens, LANES), 1)
    for k, chosen in enumerate((first, second)):
        dots = jnp.dot(chosen.astype(BF16), back_ref[:, 2 * width :], preferred_element_type=F32)
        dots = jnp.broadcast_to(dots[:, 0:1] + dots[:, 1:2], dots.shape)
        high = dots.astype(BF16).astype(F32)
        start = 2 * width + k * LANES
        out_ref[:, start : start + LANES] = jnp.where(lane == 0, high, dots - high).astype(BF16)


def finish_body(
    back_ref, hidden_ref, gain_ref, cotangent_ref, scores_ref, layer_ref, grad_ref, dots_ref
):
    rows, width = hidden_ref.shape
    total = back_ref[0].astype(F32)
    for c in range(1, back_ref.shape[0]):
        total = total + back_ref[c].astype(F32)
    hidden = hidden_ref[...]
    layer_ref[...] = (hidden + total[:, 0:width]).astype(BF16)
    scale = lax.rsqrt(jnp.mean(hidden * hidden, axis=1, keepdims=True) + 1e-05)
    scaled = total[:, width : 2 * width] * gain_ref[...]
    outer = cotangent_ref[...].astype(F32)
    grad_ref[...] = (
        outer
        + scale * scaled
        - hidden * (scale * scale * scale) * jnp.mean(hidden * scaled, axis=1, keepdims=True)
    )
    lane = lax.broadcasted_iota(jnp.int32, (rows, rows), 1)
    sub = lax.broadcasted_iota(jnp.int32, (rows, rows), 0)
    for k in range(2):
        start = 2 * width + k * LANES
        dots = total[:, start : start + 1] + total[:, start + 1 : start + 2]
        spread = jnp.where(lane == sub, jnp.broadcast_to(dots, lane.shape), 0.0)
        dots = jnp.sum(spread, axis=0, keepdims=True)
        dots_ref[k : k + 1] = dots / scores_ref[k : k + 1]


def make_per_device(interpret):
    def call(body, name, outs, ins, scratch=(), operands=(), **options):
        params = {}
        if options:
            body = partial(body, **options)
        return pl.pallas_call(
            body,
            out_shape=outs,
            in_specs=ins,
            out_specs=jax.tree.map(lambda _: VMEM, outs),
            scratch_shapes=list(scratch),
            interpret=interpret,
            name=name,
            compiler_params=pltpu.CompilerParams(vmem_limit_bytes=60 * 1024 * 1024),
            **params,
        )(*operands)

    def per_device(
        mixer_input, mixer_gate, step_low, step_proj, step_bias, decay_rate, input_coef,
        output_coef, conv_taps, conv_bias, skip_gain, out_weight, residual, norm_gain,
        expert_ids, gate_scores, gate_weight, up_weight, down_weight, cotangent,
    ):
        length, channels = mixer_input.shape
        count = decay_rate.shape[0]
        tok_rows, width = residual.shape
        units = gate_weight.shape[2]
        experts = lax.axis_size("exp")
        depth = lax.axis_size("z")
        ranks = depth * lax.axis_size("core")
        slots = 2 * experts * depth
        stride = 2 * depth
        swap = [(0, 1), (1, 0)]
        shape = jax.ShapeDtypeStruct

        def sibling(value):
            return lax.ppermute(value, "core", swap)

        def exchange(rows, axis):
            return lax.all_to_all(rows, axis, split_axis=0, concat_axis=0, tiled=True)

        before = lax.ppermute(mixer_input, ("z", "core"), [(i, i + 1) for i in range(ranks - 1)])
        gates = (gate_weight[0], sibling(gate_weight[0]))
        ups = (up_weight[0], sibling(up_weight[0]))
        downs = (down_weight[0], sibling(down_weight[0]))
        scores = gate_scores.T

        rows = shape((length, channels), F32)
        extra_rows = tok_rows * (1 + width // channels)
        late, step, inner, extra = call(
            local_state_body, "local_state",
            (
                shape((count + GROUP, channels), F32), rows, rows,
                shape((extra_rows, channels), BF16),
            ),
            [VMEM] * 11,
            (pltpu.VMEM((length + GROUP, channels), F32), pltpu.VMEM((length, channels), F32)),
            (
                mixer_input, step_low, step_proj, step_bias[None], decay_rate, input_coef,
                conv_taps, conv_bias[None], expert_ids.T, scores, cotangent,
            ),
            stride=stride,
        )
        summary, inner_first = call(
            first_group_body, "first_group",
            (
                shape((2 * count + GROUP + extra_rows, channels), BF16),
                shape((GROUP, channels), F32),
            ),
            [VMEM] * 9, (pltpu.VMEM((2 * GROUP, channels), F32),),
            (
                before, mixer_input, conv_taps, conv_bias[None], step, decay_rate, input_coef,
                late, extra,
            ),
        )
        gathered = lax.all_gather(summary, ("z", "core"), axis=0)
        mine = lax.axis_index(("z", "core")).astype(jnp.int32).reshape(1)
        tall = tok_rows + stride
        share, info = call(
            readout_body, "readout",
            (shape((experts, tall, width), BF16), shape((depth * tok_rows, LANES), F32)),
            [SMEM] + [VMEM] * 10,
            (
                pltpu.VMEM((length, channels), F32), pltpu.VMEM((length, channels), F32),
                pltpu.VMEM((length, channels), F32), pltpu.VMEM((depth * tok_rows, width), F32),
            ),
            (
                mine, gathered, decay_rate, input_coef, output_coef, step, inner, inner_first,
                skip_gain[None], mixer_gate, out_weight,
            ),
        )
        shares = exchange(share.reshape(experts * tall, width), "exp")
        shares = shares.reshape(experts, tall, width)
        hidden, send = call(
            norm_body, "norm",
            (shape((tok_rows, width), F32), shape((depth, tok_rows, width), BF16)),
            [VMEM] * 3, operands=(shares, residual, norm_gain[None]),
        )
        tokens = exchange(send.reshape(depth * tok_rows, width), "z")
        packed = call(
            pack_body, "pack", shape((slots, width), BF16), [VMEM] * 2, operands=(tokens, info)
        )
        rows_x = exchange(packed, "exp")
        grad_act = call(
            grad_act_body, "grad_act", shape((slots, 2 * units), F32), [VMEM] * 3,
            (pltpu.VMEM((slots, width), BF16),), (shares,) + downs,
        )
        result = call(
            expert_body, "expert", shape((slots, 2 * width + LANES), BF16),
            [VMEM] * 2 + [pl.BlockSpec(memory_space=pl.ANY)] * 6,
            (
                pltpu.VMEM((2, width, units), BF16),
                pltpu.VMEM((2, width, units), BF16),
                pltpu.VMEM((2, units, width), BF16),
                pltpu.VMEM((slots, units), F32),
                pltpu.VMEM((slots, units), F32),
                pltpu.VMEM((2, slots, units), BF16),
                pltpu.VMEM((2, slots, units), BF16),
                pltpu.VMEM((2, slots, units), BF16),
                pltpu.VMEM((slots, LANES), F32),
                pltpu.SemaphoreType.DMA((6,)),
            ),
            (rows_x, grad_act) + gates + ups + downs,
        )
        back = exchange(result, "exp")
        shares_back = call(
            combine_body, "combine", shape((depth * tok_rows, 2 * width + 2 * LANES), BF16),
            [VMEM] * 2, operands=(back, info),
        )
        mine_back = exchange(shares_back, "z").reshape(depth, tok_rows, 2 * width + 2 * LANES)
        layer_out, grad_hidden, dots = call(
            finish_body, "finish",
            (
                shape((tok_rows, width), BF16), shape((tok_rows, width), F32),
                shape(scores.shape, F32),
            ),
            [VMEM] * 5,
            operands=(mine_back, hidden, norm_gain[None], cotangent, scores),
        )
        return layer_out, grad_hidden, dots.T

    return per_device


def solution(mesh, interpret=False):
    ctx, exp = mesh.devices.shape
    split = Mesh(mesh.devices.reshape(ctx // 2, 2, exp), ("z", "core", "exp"))
    both = ("z", "core")
    rows = P(("z", "core", "exp"), None)
    in_specs = (
        P(both, "exp"),
        P(both, "exp"),
        P(both, None),
        P(None, "exp"),
        P("exp"),
        P(None, "exp"),
        P(None, both),
        P(None, both),
        P(None, "exp"),
        P("exp"),
        P("exp"),
        P("exp", None),
        rows,
        P(),
        rows,
        rows,
        P("exp", None, both),
        P("exp", None, both),
        P("exp", both, None),
        rows,
    )
    return jax.shard_map(
        make_per_device(interpret),
        mesh=split,
        in_specs=in_specs,
        out_specs=(rows, rows, rows),
        check_vma=False,
    )
```

time: 200 us -> 186 us (0.930)
  blocking collectives: 92.9 us -> 121 us
  waiting for transfers between devices: 19.7 us -> 6.09 us
  between operations: 14.1 us -> 0.68 us
  starting transfers between devices: 17.1 us -> 9.03 us
  local copies, waits for them, and re-layouts: 7.05 us -> 1.63 us
    all_to_all x3 -> x4, blocking collectives: 68.9 us -> 94.4 us  [exchange(): return lax.all_to_all(rows, axis, split_axis=0, concat_axis=0, tiled=True)]
    all_gather x2 -> x0, waiting for transfers between devices: 15.2 us -> none  [the longest x1 9.2 us: per_device(): rows_d = lax.all_gather(chosen, 'z', axis=0, tiled=True)]
    all_to_all x2 -> x1, starting transfers between devices: 14.1 us -> 6.03 us  [exchange(): return lax.all_to_all(rows, axis, split_axis=0, concat_axis=0, tiled=True)]
    all_to_all x2 -> x1, waiting for transfers between devices: 2.03 us -> 5.92 us  [exchange(): return lax.all_to_all(rows, axis, split_axis=0, concat_axis=0, tiled=True)]
    unnamed x8 -> x4, local copies, waits for them, and re-layouts: 5.06 us -> 1.63 us
    all_gather x1, blocking collectives: 24 us -> 26.3 us  [per_device(): gathered = lax.all_gather(summary, ('z', 'core'), axis=0)]
    ppermute x1, waiting for transfers between devices: 2.44 us -> 0.17 us  [per_device(): lax.ppermute(mixer_input, ('z', 'core'), [(i, i + 1) for i in range(ranks...]
    pallas_call x10 -> x9, Pallas kernels: 47.7 us -> 46.8 us  [call(): pl.pallas_call(body, out_shape=outs, in_specs=ins, out_specs=jax.tree.map...]
  transfers between devices with their start and end apart: 8 -> 5, of which waited for: 4 -> 2; matrix products, arithmetic and copies ran while one was open for 0% -> 0% of each run, Pallas kernels for 11% -> 12%
where the time goes in v2:
time: 186 us; the launch traced here: 185 us
  blocking collectives  121 us (65%)
  Pallas kernels  46.8 us (25%)
  starting transfers between devices  9.03 us (5%)
  waiting for transfers between devices  6.09 us (3%)
    all_to_all x4, blocking collectives, exchange(): return lax.all_to_all(rows, axis, split_axis=0, concat_axis=0, tiled=True)  94.4 us
    pallas_call x9, Pallas kernels, call(): pl.pallas_call(body, out_shape=outs, in_specs=ins, out_specs=jax.tree.map...  46.8 us
    all_gather x1, blocking collectives, per_device(): gathered = lax.all_gather(summary, ('z', 'core'), axis=0)  26.3 us
    all_to_all x1, starting transfers between devices, exchange(): return lax.all_to_all(rows, axis, split_axis=0, concat_axis=0, tiled=True)  6.03 us
    all_to_all x1, waiting for transfers between devices, exchange(): return lax.all_to_all(rows, axis, split_axis=0, concat_axis=0, tiled=True)  5.92 us
  transfers between devices with their start and end apart: 5, of which 2 were waited for; matrix products, arithmetic and copies ran while one was open for 0% of the time, Pallas kernels for 12%

profile of v2, /device:TPU:2, one launch (start us, length us, event | category | flops | bytes accessed | tf_op | source)
XLA Modules:
  0.0 185.0 jit_solution(11123228777597639170)
XLA Ops:
  0.6 0.1 collective-permute-start.1
  0.7 0.5 collective-permute-start.2
  1.2 0.1 collective-permute-start.3
  1.3 2.3 %collective-permute-start = (bf16[128,256]{1,0:T(8,128)(2,1)}, bf16[128,256]{1,0:T(8,128)(2,1)S(1)}, u32[]{:S(2)}, u32[]{:S(2)}) collective-permute-start(bf16[128,256]{1,0:T(8,128)(2,1)} %x_ref.3), channel_id=1, source_target_pairs={{0,16},{16,32},{32,48},{48,64},{64,80},{80,96},{96,112},{112,128},... | collective-permute-start | bytes 196616 | tf_op jit(solution)/shard_map/ppermute | solution.py:425
  3.7 3.3 %local_state.1 = (f32[24,256]{1,0:T(8,128)}, f32[128,256]{1,0:T(8,128)}, f32[128,256]{1,0:T(8,128)}, bf16[72,256]{1,0:T(8,128)(2,1)}) custom-call(bf16[128,256]{1,0:T(8,128)(2,1)} %x_ref.3, bf16[128,128]{1,0:T(8,128)(2,1)} %low_ref.1, bf16[128,256]{1,0:T(8,128)(2,1)} %proj_ref.1, f32[1,256]{1,0:T(1,128)} %bitcast.38, f32[16,256]{1,0:T(8,128)} %decay_ref.5, ...), custom_call_target="tpu_custom_call" | custom-call | tf_op jit(solution)/shard_map/local_state/pallas_call | solution.py:390
  7.0 0.2 collective-permute-done.before_ref
  7.2 0.6 copy-done.1
  7.8 1.8 first_group.1
  9.6 26.3 %all-gather = bf16[1792,256]{1,0:T(8,128)(2,1)} all-gather(bf16[112,256]{1,0:T(8,128)(2,1)} %get-tuple-element.19), channel_id=2, replica_groups=mesh['z'=8,'core'=2,'exp'=16] {'z','core'}, dimensions={0}, use_global_device_ids=true | all-gather | bytes 974848 | tf_op jit(solution)/shard_map/all_gather | solution.py:459
  35.9 5.9 %readout.1 = (bf16[16,24,2048]{2,1,0:T(8,128)(2,1)}, f32[64,128]{1,0:T(8,128)}) custom-call(s32[1]{0:T(128)} %bitcast.mine_ref, bf16[16,112,256]{2,1,0:T(8,128)(2,1)} %bitcast.29, f32[16,256]{1,0:T(8,128)} %decay_ref.5, f32[16,128]{1,0:T(8,128)} %bcoef_ref.5, f32[16,128]{1,0:T(8,128)} %ccoef_ref.1, f32[128,256]{1,0:T(8,128)} %get-tuple-element.16.step_ref, ...), custom_call_target="tpu_custom_call" | custom-call | tf_op jit(solution)/shard_map/readout/pallas_call | solution.py:390
  41.8 28.6 %all_to_all.45.shares_ref = bf16[16,24,2048]{2,1,0:T(8,128)(2,1)} all-to-all(bf16[16,24,2048]{2,1,0:T(8,128)(2,1)} %get-tuple-element.22), channel_id=1, replica_groups=mesh['z'=8,'core'=2,'exp'=16] {'exp'}, dimensions={0} | all-to-all | bytes 3145728 | tf_op jit(solution)/shard_map/all_to_all | solution.py:423
  70.4 2.3 %norm.1 = (f32[8,2048]{1,0:T(8,128)}, bf16[8,8,2048]{2,1,0:T(8,128)(2,1)}) custom-call(bf16[16,24,2048]{2,1,0:T(8,128)(2,1)} %all_to_all.45.shares_ref, bf16[8,2048]{1,0:T(8,128)(2,1)} %residual_ref.1, f32[1,2048]{1,0:T(1,128)} %bitcast.32), custom_call_target="tpu_custom_call" | custom-call | tf_op jit(solution)/shard_map/norm/pallas_call | solution.py:390
  72.7 15.2 %all_to_all.46 = bf16[8,8,2048]{2,1,0:T(8,128)(2,1)} all-to-all(bf16[8,8,2048]{2,1,0:T(8,128)(2,1)} %get-tuple-element.23), channel_id=1, replica_groups=mesh['z'=8,'core'=2,'exp'=16] {'z'}, dimensions={0} | all-to-all | bytes 524288 | tf_op jit(solution)/shard_map/all_to_all | solution.py:423
  88.0 2.5 %pack.1 = bf16[256,2048]{1,0:T(8,128)(2,1)} custom-call(bf16[64,2048]{1,0:T(8,128)(2,1)} %bitcast.31, f32[64,128]{1,0:T(8,128)} %get-tuple-element.24.info_ref), custom_call_target="tpu_custom_call" | custom-call | tf_op jit(solution)/shard_map/pack/pallas_call | solution.py:390
  90.5 6.0 %all-to-all-start.2 = ((bf16[16,16,2048]{2,1,0:T(8,128)(2,1)}), bf16[16,16,2048]{2,1,0:T(8,128)(2,1)S(1)}, u32[]{:S(2)}, u32[]{:S(2)}) async-start(bf16[16,16,2048]{2,1,0:T(8,128)(2,1)} %bitcast.24), calls=%async_computation.2 | async-start | bytes 2097152 | tf_op jit(solution)/shard_map/all_to_all | solution.py:423
  96.5 0.0 collective-permute-done.1.sib_ref.down_sib_hbm
  96.5 7.2 %grad_act.1.grad_act_ref = f32[256,1792]{1,0:T(8,128)} custom-call(bf16[16,24,2048]{2,1,0:T(8,128)(2,1)} %all_to_all.45.shares_ref, bf16[896,2048]{1,0:T(8,128)(2,1)} %bitcast.19, bf16[896,2048]{1,0:T(8,128)(2,1)} %collective-permute-done.1.sib_ref.down_sib_hbm), custom_call_target="tpu_custom_call" | custom-call | tf_op jit(solution)/shard_map/grad_act/pallas_call | solution.py:390
  103.7 5.9 %all-to-all-done.2 = bf16[16,16,2048]{2,1,0:T(8,128)(2,1)S(1)} async-done(((bf16[16,16,2048]{2,1,0:T(8,128)(2,1)}), bf16[16,16,2048]{2,1,0:T(8,128)(2,1)S(1)}, u32[]{:S(2)}, u32[]{:S(2)}) %all-to-all-start.2) | async-done | bytes 1048608 | tf_op jit(solution)/shard_map/all_to_all | solution.py:423
  109.6 1.0 copy-done
  110.6 18.7 %expert.1 = bf16[256,4224]{1,0:T(8,128)(2,1)} custom-call(bf16[256,2048]{1,0:T(8,128)(2,1)} %bitcast.23, f32[256,1792]{1,0:T(8,128)} %grad_act.1.grad_act_ref, bf16[2048,896]{1,0:T(8,128)(2,1)} %bitcast.26, bf16[2048,896]{1,0:T(8,128)(2,1)} %collective-permute-done.2.gate_sib_hbm, bf16[2048,896]{1,0:T(8,128)(2,1)} %bitcast.28, ...), custom_call_target="tpu_custom_call" | custom-call | tf_op jit(solution)/shard_map/expert/pallas_call | solution.py:390
  129.3 31.9 %all_to_all.47 = bf16[16,16,4224]{2,1,0:T(8,128)(2,1)} all-to-all(bf16[16,16,4224]{2,1,0:T(8,128)(2,1)} %bitcast.21), channel_id=1, replica_groups=mesh['z'=8,'core'=2,'exp'=16] {'exp'}, dimensions={0} | all-to-all | bytes 4325376 | tf_op jit(solution)/shard_map/all_to_all | solution.py:423
  161.3 3.1 %combine.1 = bf16[64,4352]{1,0:T(8,128)(2,1)} custom-call(bf16[256,4224]{1,0:T(8,128)(2,1)} %bitcast.22, f32[64,128]{1,0:T(8,128)} %get-tuple-element.24.info_ref), custom_call_target="tpu_custom_call" | custom-call | tf_op jit(solution)/shard_map/combine/pallas_call | solution.py:390
  164.4 18.7 %all_to_all.48.back_ref = bf16[8,8,4352]{2,1,0:T(8,128)(2,1)} all-to-all(bf16[8,8,4352]{2,1,0:T(8,128)(2,1)} %bitcast.30), channel_id=1, replica_groups=mesh['z'=8,'core'=2,'exp'=16] {'z'}, dimensions={0} | all-to-all | bytes 1114112 | tf_op jit(solution)/shard_map/all_to_all | solution.py:423
  183.1 1.9 %finish.1 = (bf16[8,2048]{1,0:T(8,128)(2,1)}, f32[8,2048]{1,0:T(8,128)}, f32[2,8]{1,0:T(2,128)}) custom-call(bf16[8,8,4352]{2,1,0:T(8,128)(2,1)} %all_to_all.48.back_ref, f32[8,2048]{1,0:T(8,128)} %get-tuple-element.25.hidden_ref, f32[1,2048]{1,0:T(1,128)} %bitcast.33, bf16[8,2048]{1,0:T(8,128)(2,1)} %cotangent_ref.3, f32[2,8]{1,0:T(2,128)} %bitcast.37), custom_call_target="tpu_custom_call" | custom-call | tf_op jit(solution)/shard_map/finish/pallas_call | solution.py:390
  (4 shorter events, 0.0 us)
Async XLA Ops:
  0.6 95.9 %collective-permute-start.1 = (bf16[896,2048]{1,0:T(8,128)(2,1)}, bf16[896,2048]{1,0:T(8,128)(2,1)}, u32[]{:S(2)}, u32[]{:S(2)}) collective-permute-start(bf16[896,2048]{1,0:T(8,128)(2,1)} %bitcast.18), channel_id=1, source_target_pairs={{0,16},{16,0},{1,17},{17,1},{2,18},{18,2},{3,19},{19,3},{4,20},{20... | collective-permute-start | bytes 11010056 | tf_op jit(solution)/shard_map/ppermute | solution.py:420
  0.7 108.9 %collective-permute-start.2 = (bf16[2048,896]{1,0:T(8,128)(2,1)}, bf16[2048,896]{1,0:T(8,128)(2,1)}, u32[]{:S(2)}, u32[]{:S(2)}) collective-permute-start(bf16[2048,896]{1,0:T(8,128)(2,1)} %bitcast.25), channel_id=1, source_target_pairs={{0,16},{16,0},{1,17},{17,1},{2,18},{18,2},{3,19},{19,3},{4,20},{20... | collective-permute-start | bytes 11010056 | tf_op jit(solution)/shard_map/ppermute | solution.py:420
  1.2 108.4 %collective-permute-start.3 = (bf16[2048,896]{1,0:T(8,128)(2,1)}, bf16[2048,896]{1,0:T(8,128)(2,1)}, u32[]{:S(2)}, u32[]{:S(2)}) collective-permute-start(bf16[2048,896]{1,0:T(8,128)(2,1)} %bitcast.27), channel_id=1, source_target_pairs={{0,16},{16,0},{1,17},{17,1},{2,18},{18,2},{3,19},{19,3},{4,20},{20... | collective-permute-start | bytes 11010056 | tf_op jit(solution)/shard_map/ppermute | solution.py:420
  1.3 5.8 %collective-permute-start = (bf16[128,256]{1,0:T(8,128)(2,1)}, bf16[128,256]{1,0:T(8,128)(2,1)S(1)}, u32[]{:S(2)}, u32[]{:S(2)}) collective-permute-start(bf16[128,256]{1,0:T(8,128)(2,1)} %x_ref.3), channel_id=1, source_target_pairs={{0,16},{16,32},{32,48},{48,64},{64,80},{80,96},{96,112},{112,128},... | collective-permute-start | bytes 196616 | tf_op jit(solution)/shard_map/ppermute | solution.py:425
  7.2 0.6 copy-start.1
  90.5 19.2 %all-to-all-start.2 = ((bf16[16,16,2048]{2,1,0:T(8,128)(2,1)}), bf16[16,16,2048]{2,1,0:T(8,128)(2,1)S(1)}, u32[]{:S(2)}, u32[]{:S(2)}) async-start(bf16[16,16,2048]{2,1,0:T(8,128)(2,1)} %bitcast.24), calls=%async_computation.2 | async-start | bytes 2097152 | tf_op jit(solution)/shard_map/all_to_all | solution.py:423
  109.6 1.0 copy-start

commit v3 on v2

--- a/solution.py
+++ b/solution.py
@@ -12,6 +12,7 @@
 F32 = jnp.float32
 VMEM = pl.BlockSpec(memory_space=pltpu.VMEM)
 SMEM = pl.BlockSpec(memory_space=pltpu.SMEM)
+ANY = pl.BlockSpec(memory_space=pl.ANY)
 GROUP = 8
 LANES = 128
 
@@ -141,8 +142,7 @@
     after = late_ref[count : count + 1]
     state = jnp.exp(jnp.broadcast_to(after, rate.shape) * rate) * state + late_ref[0:count]
     high, low = parts_of(state, 2)
-    send_ref[0:count] = high.astype(BF16)
-    send_ref[count : 2 * count] = low.astype(BF16)
+    states = jnp.concatenate([high, low], 0).astype(BF16)
     total = jnp.broadcast_to(
         after + jnp.sum(steps, axis=0, keepdims=True), (GROUP, rate.shape[1])
     )
@@ -150,12 +150,16 @@
     sub = lax.broadcasted_iota(jnp.int32, total.shape, 0)
     total = jnp.where(sub == 0, high, low)
     extra = extra_ref[0:GROUP].astype(F32)
-    send_ref[2 * count : 2 * count + 2 * GROUP] = jnp.concatenate([total, extra], 0).astype(BF16)
-    send_ref[2 * count + 2 * GROUP :] = extra_ref[GROUP:]
+    sums = jnp.concatenate([total, extra], 0).astype(BF16)
+    rest = extra_ref[GROUP:]
+    for z in range(send_ref.shape[0]):
+        send_ref[z, 0 : 2 * count] = states
+        send_ref[z, 2 * count : 2 * count + 2 * GROUP] = sums
+        send_ref[z, 2 * count + 2 * GROUP :] = rest
 
 
 def readout_body(
-    mine_ref, gathered_ref, decay_ref, bcoef_ref, ccoef_ref, step_ref, inner_ref, first_ref,
+    mine_ref, own_ref, sib_ref, decay_ref, bcoef_ref, ccoef_ref, step_ref, inner_ref, first_ref,
     skip_ref, gate_ref, weight_ref, out_ref, info_ref, drive_ref, read_ref, inner_all_ref,
     tokens_ref,
 ):
@@ -163,15 +167,21 @@
     shape = rate.shape
     count, channels = shape
     length = step_ref.shape[0]
-    ranks = gathered_ref.shape[0]
+    depth = own_ref.shape[0]
     mine = mine_ref[0]
+    core = lax.rem(mine, 2)
     state = jnp.zeros(shape, F32)
-    for c in range(ranks - 1):
-        piece = gathered_ref[c, 0 : 2 * count].astype(F32)
-        sums = gathered_ref[c, 2 * count : 2 * count + 2 * GROUP].astype(F32)
-        total = jnp.broadcast_to(sums[0:1] + sums[1:2], shape)
-        longer = jnp.exp(total * rate) * state + (piece[0:count] + piece[count:])
-        state = jnp.where(c < mine, longer, state)
+    for z in range(depth):
+        pair = []
+        for ref in (own_ref, sib_ref):
+            piece = ref[z, 0 : 2 * count].astype(F32)
+            sums = ref[z, 2 * count : 2 * count + 2 * GROUP].astype(F32)
+            total = jnp.broadcast_to(sums[0:1] + sums[1:2], shape)
+            pair.append((jnp.exp(total * rate), piece[0:count] + piece[count:]))
+        for k in range(2):
+            factor = jnp.where(core == k, pair[0][0], pair[1][0])
+            offset = jnp.where(core == k, pair[0][1], pair[1][1])
+            state = jnp.where(2 * z + k < mine, factor * state + offset, state)
     inner_all_ref[...] = inner_ref[...]
     inner_all_ref[0:GROUP] = first_ref[...]
     drive_ref[...] = step_ref[...] * inner_all_ref[...]
@@ -198,19 +208,16 @@
     experts, tall, width = out_ref.shape
     rows = length // experts
     slots = tall - rows
-    depth = slots // 2
     tokens = info_ref.shape[0] // depth
-    core = lax.rem(mine, ranks // depth)
     start = 2 * count + GROUP
     for z in range(depth):
         at = slice(z * tokens, (z + 1) * tokens)
-        place = z * (ranks // depth) + core
-        extra = gathered_ref[place, 2 * count : 2 * count + 2 * GROUP].astype(F32)
+        extra = own_ref[z, 2 * count : 2 * count + 2 * GROUP].astype(F32)
         info_ref[at] = extra[GROUP:, 0:LANES]
         for b in range(width // channels):
             first = start + (b + 1) * tokens
-            tokens_ref[at, b * channels : (b + 1) * channels] = gathered_ref[
-                place, first : first + tokens
+            tokens_ref[at, b * channels : (b + 1) * channels] = own_ref[
+                z, first : first + tokens
             ].astype(F32)
     info = info_ref[...]
     chosen = slot_maps(info, experts * slots)
@@ -236,12 +243,15 @@
     return maps
 
 
-def norm_body(shares_ref, residual_ref, gain_ref, hidden_ref, send_ref):
+def norm_body(shares_hbm, residual_ref, gain_ref, hidden_ref, send_ref, shares_ref, sem):
     rows = residual_ref.shape[0]
-    start = shares_ref.shape[1] - rows
-    total = shares_ref[0, start:].astype(F32)
+    start = shares_hbm.shape[1] - rows
+    copy = pltpu.make_async_copy(shares_hbm.at[:, start : start + rows], shares_ref, sem)
+    copy.start()
+    copy.wait()
+    total = shares_ref[0].astype(F32)
     for c in range(1, shares_ref.shape[0]):
-        total = total + shares_ref[c, start:].astype(F32)
+        total = total + shares_ref[c].astype(F32)
     hidden = residual_ref[...].astype(F32) + total
     hidden_ref[...] = hidden
     scale = lax.rsqrt(jnp.mean(hidden * hidden, axis=1, keepdims=True) + 1e-05)
@@ -255,51 +265,82 @@
     slots_ref[...] = contract_first((first + second).astype(BF16), tokens_ref[...]).astype(BF16)
 
 
-def grad_act_body(shares_ref, own_ref, sib_ref, out_ref, rows_ref):
-    units = own_ref.shape[0]
-    experts = shares_ref.shape[0]
-    slots = rows_ref.shape[0] // experts
-    for e in range(experts):
-        rows_ref[e * slots : (e + 1) * slots] = shares_ref[e, 0:slots]
-    rows = rows_ref[...]
-    out_ref[:, 0:units] = contract_last(rows, own_ref[...])
-    out_ref[:, units:] = contract_last(rows, sib_ref[...])
+def grad_act_body(shares_hbm, own_hbm, sib_hbm, out_hbm, rows_ref, down_ref, out_ref, sems):
+    experts, slots, width = rows_ref.shape
+    units = down_ref.shape[1]
+    copies = [
+        pltpu.make_async_copy(shares_hbm.at[:, 0:slots], rows_ref, sems.at[0]),
+        pltpu.make_async_copy(own_hbm, down_ref.at[0], sems.at[1]),
+        pltpu.make_async_copy(sib_hbm, down_ref.at[1], sems.at[2]),
+    ]
+    for copy in copies:
+        copy.start()
+    copies[0].wait()
+    rows = rows_ref[...].reshape(experts * slots, width)
+    sends = []
+    for half in range(2):
+        copies[1 + half].wait()
+        out_ref[half] = contract_last(rows, down_ref[half])
+        sends.append(pltpu.make_async_copy(out_ref.at[half], out_hbm.at[half], sems.at[3 + half]))
+        sends[-1].start()
+    for send in sends:
+        send.wait()
 
 
 def expert_body(
-    rows_ref, grad_act_ref, gate_hbm, gate_sib_hbm, up_hbm, up_sib_hbm, down_hbm, down_sib_hbm,
-    out_ref, gate_ref, up_ref, down_ref, gate_pre_ref, up_pre_ref, act_ref, grad_gate_ref,
-    grad_up_ref, dots_ref, sems,
+    rows_hbm, grad_act_hbm, gate_hbm, gate_sib_hbm, up_hbm, up_sib_hbm, down_hbm, down_sib_hbm,
+    out_hbm, rows_ref, grad_act_ref, gate_ref, up_ref, down_ref, gate_pre_ref, up_pre_ref, act_ref,
+    grad_gate_ref, grad_up_ref, dots_ref, out_ref, sems, out_sems,
 ):
-    width = rows_ref.shape[1]
+    slots, width = rows_ref.shape
     units = gate_ref.shape[2]
-    slots = rows_ref.shape[0]
-    copies = []
-    order = (
-        (gate_hbm, gate_ref, 0), (up_hbm, up_ref, 0), (gate_sib_hbm, gate_ref, 1),
-        (up_sib_hbm, up_ref, 1), (down_hbm, down_ref, 0), (down_sib_hbm, down_ref, 1),
+    half_width = width // 2
+    plan = (
+        ("rows", rows_hbm, rows_ref),
+        ("gate_top", gate_hbm.at[0:half_width], gate_ref.at[0, 0:half_width]),
+        ("gate_end", gate_hbm.at[half_width:width], gate_ref.at[0, half_width:width]),
+        ("up0", up_hbm, up_ref.at[0]),
+        ("grad_act", grad_act_hbm, grad_act_ref),
+        ("gate1", gate_sib_hbm, gate_ref.at[1]),
+        ("up1", up_sib_hbm, up_ref.at[1]),
+        ("down0", down_hbm, down_ref.at[0]),
+        ("down1", down_sib_hbm, down_ref.at[1]),
     )
-    for index, (source, target, half) in enumerate(order):
-        copies.append(pltpu.make_async_copy(source, target.at[half], sems.at[index]))
-        copies[-1].start()
-    rows = rows_ref[...]
+    copies = {}
+    for index, (name, source, target) in enumerate(plan):
+        copies[name] = pltpu.make_async_copy(source, target, sems.at[index])
+        copies[name].start()
     dots_ref[...] = jnp.zeros(dots_ref.shape, F32)
     tall = 16
+    copies["rows"].wait()
+    rows = rows_ref[...]
     for half in range(2):
-        copies[2 * half].wait()
-        gate_pre_ref[...] = jnp.dot(rows, gate_ref[half], preferred_element_type=F32)
-        copies[2 * half + 1].wait()
-        up_pre_ref[...] = jnp.dot(rows, up_ref[half], preferred_element_type=F32)
+        if half == 0:
+            copies["gate_top"].wait()
+            top = jnp.dot(
+                rows[:, 0:half_width], gate_ref[0, 0:half_width], preferred_element_type=F32
+            )
+            copies["gate_end"].wait()
+            gate_pre_ref[...] = top + jnp.dot(
+                rows[:, half_width:], gate_ref[0, half_width:], preferred_element_type=F32
+            )
+            copies["up0"].wait()
+            up_pre_ref[...] = jnp.dot(rows, up_ref[0], preferred_element_type=F32)
+            copies["grad_act"].wait()
+        else:
+            copies["gate1"].wait()
+            gate_pre_ref[...] = jnp.dot(rows, gate_ref[1], preferred_element_type=F32)
+            copies["up1"].wait()
+            up_pre_ref[...] = jnp.dot(rows, up_ref[1], preferred_element_type=F32)
 
         def chunk(r, carry):
             at = pl.ds(pl.multiple_of(r * tall, tall), tall)
             dots = dots_ref[at]
             for c in range(units // LANES):
                 lanes = slice(c * LANES, (c + 1) * LANES)
-                far = slice(half * units + c * LANES, half * units + (c + 1) * LANES)
                 gate_pre = gate_pre_ref[at, lanes]
                 up_pre = up_pre_ref[at, lanes]
-                grad_act = grad_act_ref[at, far]
+                grad_act = grad_act_ref[half, at, lanes]
                 sigma = jax.nn.sigmoid(gate_pre)
                 gated = gate_pre * sigma
                 act = (gated * up_pre).astype(BF16)
@@ -313,19 +354,37 @@
             return carry
 
         lax.fori_loop(0, slots // tall, chunk, 0)
-    copies[4].wait()
-    share = jnp.dot(act_ref[0], down_ref[0], preferred_element_type=F32)
-    copies[5].wait()
-    share = share + jnp.dot(act_ref[1], down_ref[1], preferred_element_type=F32)
-    out_ref[:, 0:width] = share.astype(BF16)
-    share = contract_last(grad_gate_ref[0], gate_ref[0]) + contract_last(grad_up_ref[0], up_ref[0])
-    share = share + contract_last(grad_gate_ref[1], gate_ref[1])
-    share = share + contract_last(grad_up_ref[1], up_ref[1])
-    out_ref[:, width : 2 * width] = share.astype(BF16)
+    sends = []
+
+    def send(first, last):
+        piece = pltpu.make_async_copy(
+            out_ref.at[:, first:last], out_hbm.at[:, first:last], out_sems.at[len(sends)]
+        )
+        piece.start()
+        sends.append(piece)
+
     dots = jnp.broadcast_to(jnp.sum(dots_ref[...], axis=1, keepdims=True), (slots, LANES))
     high = dots.astype(BF16).astype(F32)
     lane = lax.broadcasted_iota(jnp.int32, (slots, LANES), 1)
     out_ref[:, 2 * width :] = jnp.where(lane == 0, high, dots - high).astype(BF16)
+    send(2 * width, 2 * width + LANES)
+    copies["down0"].wait()
+    share = jnp.dot(act_ref[0], down_ref[0], preferred_element_type=F32)
+    copies["down1"].wait()
+    share = share + jnp.dot(act_ref[1], down_ref[1], preferred_element_type=F32)
+    out_ref[:, 0:width] = share.astype(BF16)
+    send(0, width)
+    for part in range(2):
+        at = slice(part * half_width, (part + 1) * half_width)
+        share = contract_last(grad_gate_ref[0], gate_ref[0, at])
+        share = share + contract_last(grad_up_ref[0], up_ref[0, at])
+        share = share + contract_last(grad_gate_ref[1], gate_ref[1, at])
+        share = share + contract_last(grad_up_ref[1], up_ref[1, at])
+        first = width + part * half_width
+        out_ref[:, first : first + half_width] = share.astype(BF16)
+        send(first, first + half_width)
+    for piece in sends:
+        piece.wait()
 
 
 def combine_body(back_ref, info_ref, out_ref):
@@ -383,20 +442,18 @@
 
 
 def make_per_device(interpret):
-    def call(body, name, outs, ins, scratch=(), operands=(), **options):
-        params = {}
+    def call(body, name, outs, ins, scratch=(), operands=(), out_spec=VMEM, **options):
         if options:
             body = partial(body, **options)
         return pl.pallas_call(
             body,
             out_shape=outs,
             in_specs=ins,
-            out_specs=jax.tree.map(lambda _: VMEM, outs),
+            out_specs=jax.tree.map(lambda _: out_spec, outs),
             scratch_shapes=list(scratch),
             interpret=interpret,
             name=name,
             compiler_params=pltpu.CompilerParams(vmem_limit_bytes=60 * 1024 * 1024),
-            **params,
         )(*operands)
 
     def per_device(
@@ -423,9 +480,6 @@
             return lax.all_to_all(rows, axis, split_axis=0, concat_axis=0, tiled=True)
 
         before = lax.ppermute(mixer_input, ("z", "core"), [(i, i + 1) for i in range(ranks - 1)])
-        gates = (gate_weight[0], sibling(gate_weight[0]))
-        ups = (up_weight[0], sibling(up_weight[0]))
-        downs = (down_weight[0], sibling(down_weight[0]))
         scores = gate_scores.T
 
         rows = shape((length, channels), F32)
@@ -447,7 +501,7 @@
         summary, inner_first = call(
             first_group_body, "first_group",
             (
-                shape((2 * count + GROUP + extra_rows, channels), BF16),
+                shape((depth, 2 * count + GROUP + extra_rows, channels), BF16),
                 shape((GROUP, channels), F32),
             ),
             [VMEM] * 9, (pltpu.VMEM((2 * GROUP, channels), F32),),
@@ -456,19 +510,28 @@
                 late, extra,
             ),
         )
-        gathered = lax.all_gather(summary, ("z", "core"), axis=0)
+        tall = summary.shape[1]
+        gathered = exchange(summary.reshape(depth * tall, channels), "z")
+        gathered_sib = sibling(gathered)
+        gathered_sib, gate_sent, up_sent, down_sent = lax.optimization_barrier(
+            (gathered_sib, gate_weight[0], up_weight[0], down_weight[0])
+        )
+        gates = (gate_weight[0], sibling(gate_sent))
+        ups = (up_weight[0], sibling(up_sent))
+        downs = (down_weight[0], sibling(down_sent))
         mine = lax.axis_index(("z", "core")).astype(jnp.int32).reshape(1)
         tall = tok_rows + stride
         share, info = call(
             readout_body, "readout",
             (shape((experts, tall, width), BF16), shape((depth * tok_rows, LANES), F32)),
-            [SMEM] + [VMEM] * 10,
+            [SMEM] + [VMEM] * 11,
             (
                 pltpu.VMEM((length, channels), F32), pltpu.VMEM((length, channels), F32),
                 pltpu.VMEM((length, channels), F32), pltpu.VMEM((depth * tok_rows, width), F32),
             ),
             (
-                mine, gathered, decay_rate, input_coef, output_coef, step, inner, inner_first,
+                mine, gathered.reshape(summary.shape), gathered_sib.reshape(summary.shape),
+                decay_rate, input_coef, output_coef, step, inner, inner_first,
                 skip_gain[None], mixer_gate, out_weight,
             ),
         )
@@ -477,7 +540,9 @@
         hidden, send = call(
             norm_body, "norm",
             (shape((tok_rows, width), F32), shape((depth, tok_rows, width), BF16)),
-            [VMEM] * 3, operands=(shares, residual, norm_gain[None]),
+            [ANY] + [VMEM] * 2,
+            (pltpu.VMEM((experts, tok_rows, width), BF16), pltpu.SemaphoreType.DMA(())),
+            (shares, residual, norm_gain[None]),
         )
         tokens = exchange(send.reshape(depth * tok_rows, width), "z")
         packed = call(
@@ -485,13 +550,22 @@
         )
         rows_x = exchange(packed, "exp")
         grad_act = call(
-            grad_act_body, "grad_act", shape((slots, 2 * units), F32), [VMEM] * 3,
-            (pltpu.VMEM((slots, width), BF16),), (shares,) + downs,
+            grad_act_body, "grad_act", shape((2, slots, units), F32), [ANY] * 3,
+            (
+                pltpu.VMEM((experts, stride, width), BF16),
+                pltpu.VMEM((2, units, width), BF16),
+                pltpu.VMEM((2, slots, units), F32),
+                pltpu.SemaphoreType.DMA((5,)),
+            ),
+            (shares,) + downs,
+            ANY,
         )
         result = call(
             expert_body, "expert", shape((slots, 2 * width + LANES), BF16),
-            [VMEM] * 2 + [pl.BlockSpec(memory_space=pl.ANY)] * 6,
-            (
+            [ANY] * 8,
+            (
+                pltpu.VMEM((slots, width), BF16),
+                pltpu.VMEM((2, slots, units), F32),
                 pltpu.VMEM((2, width, units), BF16),
                 pltpu.VMEM((2, width, units), BF16),
                 pltpu.VMEM((2, units, width), BF16),
@@ -501,9 +575,12 @@
                 pltpu.VMEM((2, slots, units), BF16),
                 pltpu.VMEM((2, slots, units), BF16),
                 pltpu.VMEM((slots, LANES), F32),
-                pltpu.SemaphoreType.DMA((6,)),
+                pltpu.VMEM((slots, 2 * width + LANES), BF16),
+                pltpu.SemaphoreType.DMA((9,)),
+                pltpu.SemaphoreType.DMA((4,)),
             ),
             (rows_x, grad_act) + gates + ups + downs,
+            ANY,
         )
         back = exchange(result, "exp")
         shares_back = call(

time: 186 us -> 185 us (level)
  waiting for transfers between devices: 6.09 us -> 9 us
  Pallas kernels: 46.8 us -> 44.1 us
    all_gather x1 -> x0, blocking collectives: 26.3 us -> none  [per_device(): gathered = lax.all_gather(summary, ('z', 'core'), axis=0)]
    all_to_all x4 -> x5, blocking collectives: 94.4 us -> 120 us  [exchange(): return lax.all_to_all(rows, axis, split_axis=0, concat_axis=0, tiled=True)]
    pallas_call x9, Pallas kernels: 46.8 us -> 44.1 us  [call(): pl.pallas_call(body, out_shape=outs, in_specs=ins, out_specs=jax.tree.map...]
  transfers between devices with their start and end apart: 5 -> 6, of which waited for: 2 -> 2; matrix products, arithmetic and copies ran while one was open for 0% -> 0% of each run, Pallas kernels for 12% -> 11%
where the time goes in v3:
time: 185 us; the launch traced here: 184 us
  blocking collectives  120 us (65%)
  Pallas kernels  44.1 us (24%)
  waiting for transfers between devices  9 us (5%)
  starting transfers between devices  8.37 us (5%)
    all_to_all x5, blocking collectives, exchange(): return lax.all_to_all(rows, axis, split_axis=0, concat_axis=0, tiled=True)  120 us
    pallas_call x9, Pallas kernels, call(): pl.pallas_call(body, out_shape=outs, in_specs=ins, out_specs=jax.tree.map...  44.1 us
    all_to_all x1, waiting for transfers between devices, exchange(): return lax.all_to_all(rows, axis, split_axis=0, concat_axis=0, tiled=True)  7.18 us
    all_to_all x1, starting transfers between devices, exchange(): return lax.all_to_all(rows, axis, split_axis=0, concat_axis=0, tiled=True)  5.97 us
  transfers between devices with their start and end apart: 6, of which 2 were waited for; matrix products, arithmetic and copies ran while one was open for 0% of the time, Pallas kernels for 11%

profile of v3, /device:TPU:2, one launch (start us, length us, event | category | flops | bytes accessed | tf_op | source)
XLA Modules:
  0.0 184.2 jit_solution(10861250286337955641)
XLA Ops:
  0.6 1.7 collective-permute-start
  2.4 3.3 %local_state.1 = (f32[24,256]{1,0:T(8,128)}, f32[128,256]{1,0:T(8,128)}, f32[128,256]{1,0:T(8,128)}, bf16[72,256]{1,0:T(8,128)(2,1)}) custom-call(bf16[128,256]{1,0:T(8,128)(2,1)} %x_ref.3, bf16[128,128]{1,0:T(8,128)(2,1)} %low_ref.1, bf16[128,256]{1,0:T(8,128)(2,1)} %proj_ref.1, f32[1,256]{1,0:T(1,128)} %bitcast.40, f32[16,256]{1,0:T(8,128)} %decay_ref.5, ...), custom_call_target="tpu_custom_call" | custom-call | tf_op jit(solution)/shard_map/local_state/pallas_call | solution.py:448
  5.7 0.6 copy-done.3
  6.3 1.9 %first_group.1 = (bf16[8,112,256]{2,1,0:T(8,128)(2,1)}, f32[8,256]{1,0:T(8,128)}) custom-call(bf16[128,256]{1,0:T(8,128)(2,1)} %copy-done.3, bf16[128,256]{1,0:T(8,128)(2,1)} %x_ref.3, f32[4,256]{1,0:T(4,128)} %taps_ref.3, f32[1,256]{1,0:T(1,128)} %bitcast.37, f32[128,256]{1,0:T(8,128)} %get-tuple-element.20.step_ref, f32[16,256]{1,0:T(8,128)} %decay_ref.5, ...), custom_call_target="tpu_custom_call" | custom-call | tf_op jit(solution)/shard_map/first_group/pallas_call | solution.py:448
  8.3 26.0 %all_to_all.54.own_ref = bf16[8,112,256]{2,1,0:T(8,128)(2,1)S(1)} all-to-all(bf16[8,112,256]{2,1,0:T(8,128)(2,1)} %get-tuple-element.23), channel_id=1, replica_groups=mesh['z'=8,'core'=2,'exp'=16] {'z'}, dimensions={0} | all-to-all | bytes 917504 | tf_op jit(solution)/shard_map/all_to_all | solution.py:480
  34.3 1.8 collective-permute-done.1
  36.1 0.1 collective-permute-start.2
  36.2 0.4 collective-permute-start.3
  36.6 0.1 collective-permute-start.4
  36.8 0.1 copy-done.2
  36.9 5.9 %readout.1 = (bf16[16,24,2048]{2,1,0:T(8,128)(2,1)}, f32[64,128]{1,0:T(8,128)}) custom-call(s32[1]{0:T(128)} %bitcast.mine_ref, bf16[8,112,256]{2,1,0:T(8,128)(2,1)} %copy-done.1, bf16[8,112,256]{2,1,0:T(8,128)(2,1)} %bitcast.33, f32[16,256]{1,0:T(8,128)} %decay_ref.5, f32[16,128]{1,0:T(8,128)} %bcoef_ref.5, f32[16,128]{1,0:T(8,128)} %ccoef_ref.1, ...), custom_call_target="tpu_custom_call" | custom-call | tf_op jit(solution)/shard_map/readout/pallas_call | solution.py:448
  42.8 28.5 %all_to_all.55.shares_hbm = bf16[16,24,2048]{2,1,0:T(8,128)(2,1)} all-to-all(bf16[16,24,2048]{2,1,0:T(8,128)(2,1)} %get-tuple-element.27), channel_id=1, replica_groups=mesh['z'=8,'core'=2,'exp'=16] {'exp'}, dimensions={0} | all-to-all | bytes 3145728 | tf_op jit(solution)/shard_map/all_to_all | solution.py:480
  71.2 2.7 %norm.1 = (f32[8,2048]{1,0:T(8,128)}, bf16[8,8,2048]{2,1,0:T(8,128)(2,1)}) custom-call(bf16[16,24,2048]{2,1,0:T(8,128)(2,1)} %all_to_all.55.shares_hbm, bf16[8,2048]{1,0:T(8,128)(2,1)} %residual_ref.1, f32[1,2048]{1,0:T(1,128)} %bitcast.34), custom_call_target="tpu_custom_call" | custom-call | tf_op jit(solution)/shard_map/norm/pallas_call | solution.py:448
  74.0 15.2 %all_to_all.56 = bf16[8,8,2048]{2,1,0:T(8,128)(2,1)} all-to-all(bf16[8,8,2048]{2,1,0:T(8,128)(2,1)} %get-tuple-element.28), channel_id=1, replica_groups=mesh['z'=8,'core'=2,'exp'=16] {'z'}, dimensions={0} | all-to-all | bytes 524288 | tf_op jit(solution)/shard_map/all_to_all | solution.py:480
  89.2 2.5 %pack.1 = bf16[256,2048]{1,0:T(8,128)(2,1)} custom-call(bf16[64,2048]{1,0:T(8,128)(2,1)} %bitcast.32, f32[64,128]{1,0:T(8,128)} %get-tuple-element.29.info_ref), custom_call_target="tpu_custom_call" | custom-call | tf_op jit(solution)/shard_map/pack/pallas_call | solution.py:448
  91.7 6.0 %all-to-all-start.3 = ((bf16[16,16,2048]{2,1,0:T(8,128)(2,1)}), bf16[16,16,2048]{2,1,0:T(8,128)(2,1)S(1)}, u32[]{:S(2)}, u32[]{:S(2)}) async-start(bf16[16,16,2048]{2,1,0:T(8,128)(2,1)} %bitcast.25), calls=%async_computation.3 | async-start | bytes 2097152 | tf_op jit(solution)/shard_map/all_to_all | solution.py:480
  97.6 5.9 %grad_act.1.grad_act_hbm = f32[2,256,896]{2,1,0:T(8,128)} custom-call(bf16[16,24,2048]{2,1,0:T(8,128)(2,1)} %all_to_all.55.shares_hbm, bf16[896,2048]{1,0:T(8,128)(2,1)} %bitcast.20, bf16[896,2048]{1,0:T(8,128)(2,1)} %collective-permute-done.2.sib_hbm.down_sib_hbm), custom_call_target="tpu_custom_call" | custom-call | tf_op jit(solution)/shard_map/grad_act/pallas_call | solution.py:448
  103.6 7.2 %all-to-all-done.3 = bf16[16,16,2048]{2,1,0:T(8,128)(2,1)S(1)} async-done(((bf16[16,16,2048]{2,1,0:T(8,128)(2,1)}), bf16[16,16,2048]{2,1,0:T(8,128)(2,1)S(1)}, u32[]{:S(2)}, u32[]{:S(2)}) %all-to-all-start.3) | async-done | bytes 1048608 | tf_op jit(solution)/shard_map/all_to_all | solution.py:480
  110.7 1.0 copy-done
  111.7 16.8 %expert.1 = bf16[256,4224]{1,0:T(8,128)(2,1)} custom-call(bf16[256,2048]{1,0:T(8,128)(2,1)} %bitcast.24, f32[2,256,896]{2,1,0:T(8,128)} %grad_act.1.grad_act_hbm, bf16[2048,896]{1,0:T(8,128)(2,1)} %bitcast.27, bf16[2048,896]{1,0:T(8,128)(2,1)} %collective-permute-done.3.gate_sib_hbm, bf16[2048,896]{1,0:T(8,128)(2,1)} %bitcast.29, ...), custom_call_target="tpu_custom_call" | custom-call | tf_op jit(solution)/shard_map/expert/pallas_call | solution.py:448
  128.5 31.9 %all_to_all.57 = bf16[16,16,4224]{2,1,0:T(8,128)(2,1)} all-to-all(bf16[16,16,4224]{2,1,0:T(8,128)(2,1)} %bitcast.22), channel_id=1, replica_groups=mesh['z'=8,'core'=2,'exp'=16] {'exp'}, dimensions={0} | all-to-all | bytes 4325376 | tf_op jit(solution)/shard_map/all_to_all | solution.py:480
  160.5 3.1 %combine.1 = bf16[64,4352]{1,0:T(8,128)(2,1)} custom-call(bf16[256,4224]{1,0:T(8,128)(2,1)} %bitcast.23, f32[64,128]{1,0:T(8,128)} %get-tuple-element.29.info_ref), custom_call_target="tpu_custom_call" | custom-call | tf_op jit(solution)/shard_map/combine/pallas_call | solution.py:448
  163.6 18.6 %all_to_all.58.back_ref = bf16[8,8,4352]{2,1,0:T(8,128)(2,1)} all-to-all(bf16[8,8,4352]{2,1,0:T(8,128)(2,1)} %bitcast.30), channel_id=1, replica_groups=mesh['z'=8,'core'=2,'exp'=16] {'z'}, dimensions={0} | all-to-all | bytes 1114112 | tf_op jit(solution)/shard_map/all_to_all | solution.py:480
  182.3 1.9 %finish.1 = (bf16[8,2048]{1,0:T(8,128)(2,1)}, f32[8,2048]{1,0:T(8,128)}, f32[2,8]{1,0:T(2,128)}) custom-call(bf16[8,8,4352]{2,1,0:T(8,128)(2,1)} %all_to_all.58.back_ref, f32[8,2048]{1,0:T(8,128)} %get-tuple-element.33.hidden_ref, f32[1,2048]{1,0:T(1,128)} %bitcast.35, bf16[8,2048]{1,0:T(8,128)(2,1)} %cotangent_ref.3, f32[2,8]{1,0:T(2,128)} %bitcast.39), custom_call_target="tpu_custom_call" | custom-call | tf_op jit(solution)/shard_map/finish/pallas_call | solution.py:448
  (10 shorter events, 0.0 us)
Async XLA Ops:
  0.6 5.1 %collective-permute-start = (bf16[128,256]{1,0:T(8,128)(2,1)}, bf16[128,256]{1,0:T(8,128)(2,1)S(1)}, u32[]{:S(2)}, u32[]{:S(2)}) collective-permute-start(bf16[128,256]{1,0:T(8,128)(2,1)} %x_ref.3), channel_id=1, source_target_pairs={{0,16},{16,32},{32,48},{48,64},{64,80},{80,96},{96,112},{112,128},... | collective-permute-start | bytes 196616 | tf_op jit(solution)/shard_map/ppermute | solution.py:482
  5.7 0.6 copy-start.3
  34.3 2.5 %copy-start.1 = (bf16[8,112,256]{2,1,0:T(8,128)(2,1)}, bf16[8,112,256]{2,1,0:T(8,128)(2,1)S(1)}, u32[]{:S(2)}) copy-start(bf16[8,112,256]{2,1,0:T(8,128)(2,1)S(1)} %all_to_all.54.own_ref) | copy-start | bytes 1376260
  34.3 1.8 collective-permute-start.1
  36.1 0.8 copy-start.2
  36.1 61.5 %collective-permute-start.2 = (bf16[896,2048]{1,0:T(8,128)(2,1)}, bf16[896,2048]{1,0:T(8,128)(2,1)}, u32[]{:S(2)}, u32[]{:S(2)}) collective-permute-start(bf16[896,2048]{1,0:T(8,128)(2,1)} %bitcast.19), channel_id=1, source_target_pairs={{0,16},{16,0},{1,17},{17,1},{2,18},{18,2},{3,19},{19,3},{4,20},{20... | collective-permute-start | bytes 11010056 | tf_op jit(solution)/shard_map/ppermute | solution.py:477
  36.2 74.5 %collective-permute-start.3 = (bf16[2048,896]{1,0:T(8,128)(2,1)}, bf16[2048,896]{1,0:T(8,128)(2,1)}, u32[]{:S(2)}, u32[]{:S(2)}) collective-permute-start(bf16[2048,896]{1,0:T(8,128)(2,1)} %bitcast.26), channel_id=1, source_target_pairs={{0,16},{16,0},{1,17},{17,1},{2,18},{18,2},{3,19},{19,3},{4,20},{20... | collective-permute-start | bytes 11010056 | tf_op jit(solution)/shard_map/ppermute | solution.py:477
  36.6 74.1 %collective-permute-start.4 = (bf16[2048,896]{1,0:T(8,128)(2,1)}, bf16[2048,896]{1,0:T(8,128)(2,1)}, u32[]{:S(2)}, u32[]{:S(2)}) collective-permute-start(bf16[2048,896]{1,0:T(8,128)(2,1)} %bitcast.28), channel_id=1, source_target_pairs={{0,16},{16,0},{1,17},{17,1},{2,18},{18,2},{3,19},{19,3},{4,20},{20... | collective-permute-start | bytes 11010056 | tf_op jit(solution)/shard_map/ppermute | solution.py:477
  91.7 19.1 %all-to-all-start.3 = ((bf16[16,16,2048]{2,1,0:T(8,128)(2,1)}), bf16[16,16,2048]{2,1,0:T(8,128)(2,1)S(1)}, u32[]{:S(2)}, u32[]{:S(2)}) async-start(bf16[16,16,2048]{2,1,0:T(8,128)(2,1)} %bitcast.25), calls=%async_computation.3 | async-start | bytes 2097152 | tf_op jit(solution)/shard_map/all_to_all | solution.py:480
  110.7 1.0 copy-start

commit v4 on v3

--- a/solution.py
+++ b/solution.py
@@ -13,6 +13,7 @@
 VMEM = pl.BlockSpec(memory_space=pltpu.VMEM)
 SMEM = pl.BlockSpec(memory_space=pltpu.SMEM)
 ANY = pl.BlockSpec(memory_space=pl.ANY)
+NEAR = "near"
 GROUP = 8
 LANES = 128
 
@@ -243,15 +244,12 @@
     return maps
 
 
-def norm_body(shares_hbm, residual_ref, gain_ref, hidden_ref, send_ref, shares_ref, sem):
+def norm_body(shares_ref, residual_ref, gain_ref, hidden_ref, send_ref):
     rows = residual_ref.shape[0]
-    start = shares_hbm.shape[1] - rows
-    copy = pltpu.make_async_copy(shares_hbm.at[:, start : start + rows], shares_ref, sem)
-    copy.start()
-    copy.wait()
-    total = shares_ref[0].astype(F32)
+    start = shares_ref.shape[1] - rows
+    total = shares_ref[0, start:].astype(F32)
     for c in range(1, shares_ref.shape[0]):
-        total = total + shares_ref[c].astype(F32)
+        total = total + shares_ref[c, start:].astype(F32)
     hidden = residual_ref[...].astype(F32) + total
     hidden_ref[...] = hidden
     scale = lax.rsqrt(jnp.mean(hidden * hidden, axis=1, keepdims=True) + 1e-05)
@@ -265,42 +263,33 @@
     slots_ref[...] = contract_first((first + second).astype(BF16), tokens_ref[...]).astype(BF16)
 
 
-def grad_act_body(shares_hbm, own_hbm, sib_hbm, out_hbm, rows_ref, down_ref, out_ref, sems):
-    experts, slots, width = rows_ref.shape
-    units = down_ref.shape[1]
+def grad_act_body(shares_ref, own_hbm, sib_hbm, out_ref, down_ref, sems):
+    experts = shares_ref.shape[0]
+    slots = out_ref.shape[1] // experts
     copies = [
-        pltpu.make_async_copy(shares_hbm.at[:, 0:slots], rows_ref, sems.at[0]),
-        pltpu.make_async_copy(own_hbm, down_ref.at[0], sems.at[1]),
-        pltpu.make_async_copy(sib_hbm, down_ref.at[1], sems.at[2]),
+        pltpu.make_async_copy(source, down_ref.at[half], sems.at[half])
+        for half, source in enumerate((own_hbm, sib_hbm))
     ]
     for copy in copies:
         copy.start()
-    copies[0].wait()
-    rows = rows_ref[...].reshape(experts * slots, width)
-    sends = []
+    rows = shares_ref[:, 0:slots].reshape(experts * slots, shares_ref.shape[2])
     for half in range(2):
-        copies[1 + half].wait()
+        copies[half].wait()
         out_ref[half] = contract_last(rows, down_ref[half])
-        sends.append(pltpu.make_async_copy(out_ref.at[half], out_hbm.at[half], sems.at[3 + half]))
-        sends[-1].start()
-    for send in sends:
-        send.wait()
 
 
 def expert_body(
-    rows_hbm, grad_act_hbm, gate_hbm, gate_sib_hbm, up_hbm, up_sib_hbm, down_hbm, down_sib_hbm,
-    out_hbm, rows_ref, grad_act_ref, gate_ref, up_ref, down_ref, gate_pre_ref, up_pre_ref, act_ref,
-    grad_gate_ref, grad_up_ref, dots_ref, out_ref, sems, out_sems,
+    rows_ref, grad_act_ref, gate_hbm, gate_sib_hbm, up_hbm, up_sib_hbm, down_hbm, down_sib_hbm,
+    out_ref, gate_ref, up_ref, down_ref, gate_pre_ref, up_pre_ref, act_ref, grad_gate_ref,
+    grad_up_ref, dots_ref, sems,
 ):
     slots, width = rows_ref.shape
     units = gate_ref.shape[2]
     half_width = width // 2
     plan = (
-        ("rows", rows_hbm, rows_ref),
         ("gate_top", gate_hbm.at[0:half_width], gate_ref.at[0, 0:half_width]),
         ("gate_end", gate_hbm.at[half_width:width], gate_ref.at[0, half_width:width]),
         ("up0", up_hbm, up_ref.at[0]),
-        ("grad_act", grad_act_hbm, grad_act_ref),
         ("gate1", gate_sib_hbm, gate_ref.at[1]),
         ("up1", up_sib_hbm, up_ref.at[1]),
         ("down0", down_hbm, down_ref.at[0]),
@@ -312,7 +301,6 @@
         copies[name].start()
     dots_ref[...] = jnp.zeros(dots_ref.shape, F32)
     tall = 16
-    copies["rows"].wait()
     rows = rows_ref[...]
     for half in range(2):
         if half == 0:
@@ -326,7 +314,6 @@
             )
             copies["up0"].wait()
             up_pre_ref[...] = jnp.dot(rows, up_ref[0], preferred_element_type=F32)
-            copies["grad_act"].wait()
         else:
             copies["gate1"].wait()
             gate_pre_ref[...] = jnp.dot(rows, gate_ref[1], preferred_element_type=F32)
@@ -354,37 +341,19 @@
             return carry
 
         lax.fori_loop(0, slots // tall, chunk, 0)
-    sends = []
-
-    def send(first, last):
-        piece = pltpu.make_async_copy(
-            out_ref.at[:, first:last], out_hbm.at[:, first:last], out_sems.at[len(sends)]
-        )
-        piece.start()
-        sends.append(piece)
-
     dots = jnp.broadcast_to(jnp.sum(dots_ref[...], axis=1, keepdims=True), (slots, LANES))
     high = dots.astype(BF16).astype(F32)
     lane = lax.broadcasted_iota(jnp.int32, (slots, LANES), 1)
     out_ref[:, 2 * width :] = jnp.where(lane == 0, high, dots - high).astype(BF16)
-    send(2 * width, 2 * width + LANES)
     copies["down0"].wait()
     share = jnp.dot(act_ref[0], down_ref[0], preferred_element_type=F32)
     copies["down1"].wait()
     share = share + jnp.dot(act_ref[1], down_ref[1], preferred_element_type=F32)
     out_ref[:, 0:width] = share.astype(BF16)
-    send(0, width)
-    for part in range(2):
-        at = slice(part * half_width, (part + 1) * half_width)
-        share = contract_last(grad_gate_ref[0], gate_ref[0, at])
-        share = share + contract_last(grad_up_ref[0], up_ref[0, at])
-        share = share + contract_last(grad_gate_ref[1], gate_ref[1, at])
-        share = share + contract_last(grad_up_ref[1], up_ref[1, at])
-        first = width + part * half_width
-        out_ref[:, first : first + half_width] = share.astype(BF16)
-        send(first, first + half_width)
-    for piece in sends:
-        piece.wait()
+    share = contract_last(grad_gate_ref[0], gate_ref[0]) + contract_last(grad_up_ref[0], up_ref[0])
+    share = share + contract_last(grad_gate_ref[1], gate_ref[1])
+    share = share + contract_last(grad_up_ref[1], up_ref[1])
+    out_ref[:, width : 2 * width] = share.astype(BF16)
 
 
 def combine_body(back_ref, info_ref, out_ref):
@@ -442,19 +411,29 @@
 
 
 def make_per_device(interpret):
-    def call(body, name, outs, ins, scratch=(), operands=(), out_spec=VMEM, **options):
+    def call(body, name, outs, ins, scratch=(), operands=(), mib=24, **options):
         if options:
             body = partial(body, **options)
+        near = operands
+        if not interpret:
+            near = [
+                value if spec is SMEM else pltpu.with_memory_space_constraint(
+                    value, pltpu.VMEM if spec is NEAR else pltpu.HBM
+                )
+                for spec, value in zip(ins, operands)
+            ]
+        else:
+            outs = jax.tree.map(lambda out: jax.ShapeDtypeStruct(out.shape, out.dtype), outs)
         return pl.pallas_call(
             body,
             out_shape=outs,
-            in_specs=ins,
-            out_specs=jax.tree.map(lambda _: out_spec, outs),
+            in_specs=[VMEM if spec is NEAR else spec for spec in ins],
+            out_specs=jax.tree.map(lambda _: VMEM, outs),
             scratch_shapes=list(scratch),
             interpret=interpret,
             name=name,
-            compiler_params=pltpu.CompilerParams(vmem_limit_bytes=60 * 1024 * 1024),
-        )(*operands)
+            compiler_params=pltpu.CompilerParams(vmem_limit_bytes=mib * 1024 * 1024),
+        )(*near)
 
     def per_device(
         mixer_input, mixer_gate, step_low, step_proj, step_bias, decay_rate, input_coef,
@@ -472,6 +451,7 @@
         stride = 2 * depth
         swap = [(0, 1), (1, 0)]
         shape = jax.ShapeDtypeStruct
+        near = pltpu.VMEM
 
         def sibling(value):
             return lax.ppermute(value, "core", swap)
@@ -482,13 +462,13 @@
         before = lax.ppermute(mixer_input, ("z", "core"), [(i, i + 1) for i in range(ranks - 1)])
         scores = gate_scores.T
 
-        rows = shape((length, channels), F32)
+        rows = near((length, channels), F32)
         extra_rows = tok_rows * (1 + width // channels)
         late, step, inner, extra = call(
             local_state_body, "local_state",
             (
-                shape((count + GROUP, channels), F32), rows, rows,
-                shape((extra_rows, channels), BF16),
+                near((count + GROUP, channels), F32), rows, rows,
+                near((extra_rows, channels), BF16),
             ),
             [VMEM] * 11,
             (pltpu.VMEM((length + GROUP, channels), F32), pltpu.VMEM((length, channels), F32)),
@@ -501,10 +481,11 @@
         summary, inner_first = call(
             first_group_body, "first_group",
             (
-                shape((depth, 2 * count + GROUP + extra_rows, channels), BF16),
-                shape((GROUP, channels), F32),
-            ),
-            [VMEM] * 9, (pltpu.VMEM((2 * GROUP, channels), F32),),
+                near((depth, 2 * count + GROUP + extra_rows, channels), BF16),
+                near((GROUP, channels), F32),
+            ),
+            [NEAR] + [VMEM] * 3 + [NEAR] + [VMEM] * 2 + [NEAR] * 2,
+            (pltpu.VMEM((2 * GROUP, channels), F32),),
             (
                 before, mixer_input, conv_taps, conv_bias[None], step, decay_rate, input_coef,
                 late, extra,
@@ -523,8 +504,8 @@
         tall = tok_rows + stride
         share, info = call(
             readout_body, "readout",
-            (shape((experts, tall, width), BF16), shape((depth * tok_rows, LANES), F32)),
-            [SMEM] + [VMEM] * 11,
+            (near((experts, tall, width), BF16), near((depth * tok_rows, LANES), F32)),
+            [SMEM] + [NEAR] * 2 + [VMEM] * 3 + [NEAR] * 3 + [VMEM] * 3,
             (
                 pltpu.VMEM((length, channels), F32), pltpu.VMEM((length, channels), F32),
                 pltpu.VMEM((length, channels), F32), pltpu.VMEM((depth * tok_rows, width), F32),
@@ -539,33 +520,24 @@
         shares = shares.reshape(experts, tall, width)
         hidden, send = call(
             norm_body, "norm",
-            (shape((tok_rows, width), F32), shape((depth, tok_rows, width), BF16)),
-            [ANY] + [VMEM] * 2,
-            (pltpu.VMEM((experts, tok_rows, width), BF16), pltpu.SemaphoreType.DMA(())),
-            (shares, residual, norm_gain[None]),
+            (near((tok_rows, width), F32), near((depth, tok_rows, width), BF16)),
+            [NEAR] + [VMEM] * 2,
+            operands=(shares, residual, norm_gain[None]),
         )
         tokens = exchange(send.reshape(depth * tok_rows, width), "z")
         packed = call(
-            pack_body, "pack", shape((slots, width), BF16), [VMEM] * 2, operands=(tokens, info)
+            pack_body, "pack", near((slots, width), BF16), [NEAR] * 2, operands=(tokens, info)
         )
         rows_x = exchange(packed, "exp")
         grad_act = call(
-            grad_act_body, "grad_act", shape((2, slots, units), F32), [ANY] * 3,
-            (
-                pltpu.VMEM((experts, stride, width), BF16),
-                pltpu.VMEM((2, units, width), BF16),
-                pltpu.VMEM((2, slots, units), F32),
-                pltpu.SemaphoreType.DMA((5,)),
-            ),
+            grad_act_body, "grad_act", near((2, slots, units), F32), [NEAR] + [ANY] * 2,
+            (pltpu.VMEM((2, units, width), BF16), pltpu.SemaphoreType.DMA((2,))),
             (shares,) + downs,
-            ANY,
         )
         result = call(
-            expert_body, "expert", shape((slots, 2 * width + LANES), BF16),
-            [ANY] * 8,
-            (
-                pltpu.VMEM((slots, width), BF16),
-                pltpu.VMEM((2, slots, units), F32),
+            expert_body, "expert", near((slots, 2 * width + LANES), BF16),
+            [NEAR] * 2 + [ANY] * 6,
+            (
                 pltpu.VMEM((2, width, units), BF16),
                 pltpu.VMEM((2, width, units), BF16),
                 pltpu.VMEM((2, units, width), BF16),
@@ -575,17 +547,15 @@
                 pltpu.VMEM((2, slots, units), BF16),
                 pltpu.VMEM((2, slots, units), BF16),
                 pltpu.VMEM((slots, LANES), F32),
-                pltpu.VMEM((slots, 2 * width + LANES), BF16),
-                pltpu.SemaphoreType.DMA((9,)),
-                pltpu.SemaphoreType.DMA((4,)),
+                pltpu.SemaphoreType.DMA((7,)),
             ),
             (rows_x, grad_act) + gates + ups + downs,
-            ANY,
+            48,
         )
         back = exchange(result, "exp")
         shares_back = call(
-            combine_body, "combine", shape((depth * tok_rows, 2 * width + 2 * LANES), BF16),
-            [VMEM] * 2, operands=(back, info),
+            combine_body, "combine", near((depth * tok_rows, 2 * width + 2 * LANES), BF16),
+            [NEAR] * 2, operands=(back, info),
         )
         mine_back = exchange(shares_back, "z").reshape(depth, tok_rows, 2 * width + 2 * LANES)
         layer_out, grad_hidden, dots = call(
@@ -594,7 +564,7 @@
                 shape((tok_rows, width), BF16), shape((tok_rows, width), F32),
                 shape(scores.shape, F32),
             ),
-            [VMEM] * 5,
+            [NEAR] * 2 + [VMEM] * 3,
             operands=(mine_back, hidden, norm_gain[None], cotangent, scores),
         )
         return layer_out, grad_hidden, dots.T

time: 185 us -> 172 us (0.930)
  Pallas kernels: 44.1 us -> 34.3 us
  blocking collectives: 120 us -> 118 us
    pallas_call x9, Pallas kernels: 44.1 us -> 34.3 us  [call(): pl.pallas_call(body, out_shape=outs, in_specs=[VMEM if spec is NEAR else...]
    all_to_all x5, blocking collectives: 120 us -> 118 us  [exchange(): return lax.all_to_all(rows, axis, split_axis=0, concat_axis=0, tiled=True)]
  transfers between devices with their start and end apart: 6 -> 6, of which waited for: 2 -> 2; matrix products, arithmetic and copies ran while one was open for 0% -> 0% of each run, Pallas kernels for 11% -> 8%
where the time goes in v4:
time: 172 us; the launch traced here: 171 us
  blocking collectives  118 us (69%)
  Pallas kernels  34.3 us (20%)
  waiting for transfers between devices  10.4 us (6%)
  starting transfers between devices  8.42 us (5%)
    all_to_all x5, blocking collectives, exchange(): return lax.all_to_all(rows, axis, split_axis=0, concat_axis=0, tiled=True)  118 us
    pallas_call x9, Pallas kernels, call(): pl.pallas_call(body, out_shape=outs, in_specs=[VMEM if spec is NEAR else...  34.3 us
    all_to_all x1, waiting for transfers between devices, exchange(): return lax.all_to_all(rows, axis, split_axis=0, concat_axis=0, tiled=True)  8.61 us
    all_to_all x1, starting transfers between devices, exchange(): return lax.all_to_all(rows, axis, split_axis=0, concat_axis=0, tiled=True)  6.03 us
  transfers between devices with their start and end apart: 6, of which 2 were waited for; matrix products, arithmetic and copies ran while one was open for 0% of the time, Pallas kernels for 8%

profile of v4, /device:TPU:2, one launch (start us, length us, event | category | flops | bytes accessed | tf_op | source)
XLA Modules:
  0.0 171.4 jit_solution(3062699419314009617)
XLA Ops:
  0.6 1.7 %collective-permute-start = (bf16[128,256]{1,0:T(8,128)(2,1)}, bf16[128,256]{1,0:T(8,128)(2,1)S(1)}, u32[]{:S(2)}, u32[]{:S(2)}) collective-permute-start(bf16[128,256]{1,0:T(8,128)(2,1)} %x_ref.3), channel_id=1, source_target_pairs={{0,16},{16,32},{32,48},{48,64},{64,80},{80,96},{96,112},{112,128},... | collective-permute-start | bytes 196616 | tf_op jit(solution)/shard_map/ppermute | solution.py:462
  2.4 2.7 %local_state.1 = (f32[24,256]{1,0:T(8,128)S(1)}, f32[128,256]{1,0:T(8,128)S(1)}, f32[128,256]{1,0:T(8,128)S(1)}, bf16[72,256]{1,0:T(8,128)(2,1)S(1)}) custom-call(bf16[128,256]{1,0:T(8,128)(2,1)} %x_ref.3, bf16[128,128]{1,0:T(8,128)(2,1)} %low_ref.1, bf16[128,256]{1,0:T(8,128)(2,1)} %proj_ref.1, f32[1,256]{1,0:T(1,128)} %bitcast.38, f32[16,256]{1,0:T(8,128)} %decay_ref.5, ...), custom_call_target="tpu_custom_call" | custom-call | tf_op jit(solution)/shard_map/local_state/pallas_call | solution.py:427
  5.1 0.0 collective-permute-done.before_ref
  5.1 1.0 first_group.1
  6.1 25.8 %all_to_all.54.own_ref = bf16[8,112,256]{2,1,0:T(8,128)(2,1)S(1)} all-to-all(bf16[8,112,256]{2,1,0:T(8,128)(2,1)S(1)} %get-tuple-element.23), channel_id=1, replica_groups=mesh['z'=8,'core'=2,'exp'=16] {'z'}, dimensions={0} | all-to-all | bytes 917504 | tf_op jit(solution)/shard_map/all_to_all | solution.py:460
  31.9 1.8 %collective-permute-done.1 = bf16[896,256]{1,0:T(8,128)(2,1)S(1)} collective-permute-done((bf16[896,256]{1,0:T(8,128)(2,1)S(1)}, bf16[896,256]{1,0:T(8,128)(2,1)S(1)}, u32[]{:S(2)}, u32[]{:S(2)}) %collective-permute-start.1) | collective-permute-done | bytes 458784 | tf_op jit(solution)/shard_map/ppermute | solution.py:457
  33.8 0.1 collective-permute-start.2
  33.9 0.4 collective-permute-start.3
  34.3 0.1 collective-permute-start.4
  34.4 4.4 %readout.1 = (bf16[16,24,2048]{2,1,0:T(8,128)(2,1)S(1)}, f32[64,128]{1,0:T(8,128)S(1)}) custom-call(s32[1]{0:T(128)} %bitcast.mine_ref, bf16[8,112,256]{2,1,0:T(8,128)(2,1)S(1)} %all_to_all.54.own_ref, bf16[8,112,256]{2,1,0:T(8,128)(2,1)S(1)} %bitcast.24, f32[16,256]{1,0:T(8,128)} %decay_ref.5, f32[16,128]{1,0:T(8,128)} %bcoef_ref.5, f32[16,128]{1,0:T(8,128)} %ccoef_ref.1, ...), custom_call_target="tpu_custom_call" | custom-call | tf_op jit(solution)/shard_map/readout/pallas_call | solution.py:427
  38.8 28.3 %all_to_all.55.shares_ref = bf16[16,24,2048]{2,1,0:T(8,128)(2,1)S(1)} all-to-all(bf16[16,24,2048]{2,1,0:T(8,128)(2,1)S(1)} %get-tuple-element.27), channel_id=1, replica_groups=mesh['z'=8,'core'=2,'exp'=16] {'exp'}, dimensions={0} | all-to-all | bytes 3145728 | tf_op jit(solution)/shard_map/all_to_all | solution.py:460
  67.1 0.9 norm.1
  68.0 13.6 %all_to_all.56 = bf16[8,8,2048]{2,1,0:T(8,128)(2,1)S(1)} all-to-all(bf16[8,8,2048]{2,1,0:T(8,128)(2,1)S(1)} %get-tuple-element.28), channel_id=1, replica_groups=mesh['z'=8,'core'=2,'exp'=16] {'z'}, dimensions={0} | all-to-all | bytes 524288 | tf_op jit(solution)/shard_map/all_to_all | solution.py:460
  81.6 1.6 pack.1
  83.2 6.0 %all-to-all-start.3 = ((bf16[16,16,2048]{2,1,0:T(8,128)(2,1)}), bf16[16,16,2048]{2,1,0:T(8,128)(2,1)}, u32[]{:S(2)}, u32[]{:S(2)}) async-start(bf16[16,16,2048]{2,1,0:T(8,128)(2,1)} %bitcast.13), calls=%async_computation.3 | async-start | bytes 2097152 | tf_op jit(solution)/shard_map/all_to_all | solution.py:460
  89.2 0.0 collective-permute-done.2.sib_hbm.down_sib_hbm
  89.2 4.6 %grad_act.1.grad_act_ref = f32[2,256,896]{2,1,0:T(8,128)S(1)} custom-call(bf16[16,24,2048]{2,1,0:T(8,128)(2,1)S(1)} %all_to_all.55.shares_ref, bf16[896,2048]{1,0:T(8,128)(2,1)} %bitcast.26, bf16[896,2048]{1,0:T(8,128)(2,1)} %collective-permute-done.2.sib_hbm.down_sib_hbm), custom_call_target="tpu_custom_call" | custom-call | tf_op jit(solution)/shard_map/grad_act/pallas_call | solution.py:427
  93.9 8.6 %all-to-all-done.3 = bf16[16,16,2048]{2,1,0:T(8,128)(2,1)} async-done(((bf16[16,16,2048]{2,1,0:T(8,128)(2,1)}), bf16[16,16,2048]{2,1,0:T(8,128)(2,1)}, u32[]{:S(2)}, u32[]{:S(2)}) %all-to-all-start.3) | async-done | bytes 1048608 | tf_op jit(solution)/shard_map/all_to_all | solution.py:460
  102.5 0.0 collective-permute-done.3.gate_sib_hbm
  102.5 16.8 %expert.1 = bf16[256,4224]{1,0:T(8,128)(2,1)S(1)} custom-call(bf16[256,2048]{1,0:T(8,128)(2,1)} %bitcast.14.rows_ref, f32[2,256,896]{2,1,0:T(8,128)S(1)} %grad_act.1.grad_act_ref, bf16[2048,896]{1,0:T(8,128)(2,1)} %bitcast.29, bf16[2048,896]{1,0:T(8,128)(2,1)} %collective-permute-done.3.gate_sib_hbm, bf16[2048,896]{1,0:T(8,128)(2,1)} %bitcast.31, ...), custom_call_target="tpu_custom_call" | custom-call | tf_op jit(solution)/shard_map/expert/pallas_call | solution.py:427
  119.3 31.9 %all_to_all.57 = bf16[16,16,4224]{2,1,0:T(8,128)(2,1)S(1)} all-to-all(bf16[16,16,4224]{2,1,0:T(8,128)(2,1)S(1)} %bitcast.19), channel_id=1, replica_groups=mesh['z'=8,'core'=2,'exp'=16] {'exp'}, dimensions={0} | all-to-all | bytes 4325376 | tf_op jit(solution)/shard_map/all_to_all | solution.py:460
  151.2 0.7 combine.1
  151.9 18.0 %all_to_all.58.back_ref = bf16[8,8,4352]{2,1,0:T(8,128)(2,1)S(1)} all-to-all(bf16[8,8,4352]{2,1,0:T(8,128)(2,1)S(1)} %bitcast.21), channel_id=1, replica_groups=mesh['z'=8,'core'=2,'exp'=16] {'z'}, dimensions={0} | all-to-all | bytes 1114112 | tf_op jit(solution)/shard_map/all_to_all | solution.py:460
  169.8 1.6 finish.1
  (2 shorter events, 0.0 us)
Async XLA Ops:
  0.6 4.5 %collective-permute-start = (bf16[128,256]{1,0:T(8,128)(2,1)}, bf16[128,256]{1,0:T(8,128)(2,1)S(1)}, u32[]{:S(2)}, u32[]{:S(2)}) collective-permute-start(bf16[128,256]{1,0:T(8,128)(2,1)} %x_ref.3), channel_id=1, source_target_pairs={{0,16},{16,32},{32,48},{48,64},{64,80},{80,96},{96,112},{112,128},... | collective-permute-start | bytes 196616 | tf_op jit(solution)/shard_map/ppermute | solution.py:462
  31.9 1.8 %collective-permute-start.1 = (bf16[896,256]{1,0:T(8,128)(2,1)S(1)}, bf16[896,256]{1,0:T(8,128)(2,1)S(1)}, u32[]{:S(2)}, u32[]{:S(2)}) collective-permute-start(bf16[896,256]{1,0:T(8,128)(2,1)S(1)} %bitcast.22), channel_id=1, source_target_pairs={{0,16},{16,0},{1,17},{17,1},{2,18},{18,2},{3,19},{19,3},{4,20},{20... | collective-permute-start | bytes 1376264 | tf_op jit(solution)/shard_map/ppermute | solution.py:457
  33.8 55.5 %collective-permute-start.2 = (bf16[896,2048]{1,0:T(8,128)(2,1)}, bf16[896,2048]{1,0:T(8,128)(2,1)}, u32[]{:S(2)}, u32[]{:S(2)}) collective-permute-start(bf16[896,2048]{1,0:T(8,128)(2,1)} %bitcast.25), channel_id=1, source_target_pairs={{0,16},{16,0},{1,17},{17,1},{2,18},{18,2},{3,19},{19,3},{4,20},{20... | collective-permute-start | bytes 11010056 | tf_op jit(solution)/shard_map/ppermute | solution.py:457
  33.9 68.6 %collective-permute-start.3 = (bf16[2048,896]{1,0:T(8,128)(2,1)}, bf16[2048,896]{1,0:T(8,128)(2,1)}, u32[]{:S(2)}, u32[]{:S(2)}) collective-permute-start(bf16[2048,896]{1,0:T(8,128)(2,1)} %bitcast.28), channel_id=1, source_target_pairs={{0,16},{16,0},{1,17},{17,1},{2,18},{18,2},{3,19},{19,3},{4,20},{20... | collective-permute-start | bytes 11010056 | tf_op jit(solution)/shard_map/ppermute | solution.py:457
  34.3 68.2 %collective-permute-start.4 = (bf16[2048,896]{1,0:T(8,128)(2,1)}, bf16[2048,896]{1,0:T(8,128)(2,1)}, u32[]{:S(2)}, u32[]{:S(2)}) collective-permute-start(bf16[2048,896]{1,0:T(8,128)(2,1)} %bitcast.30), channel_id=1, source_target_pairs={{0,16},{16,0},{1,17},{17,1},{2,18},{18,2},{3,19},{19,3},{4,20},{20... | collective-permute-start | bytes 11010056 | tf_op jit(solution)/shard_map/ppermute | solution.py:457
  83.2 19.3 %all-to-all-start.3 = ((bf16[16,16,2048]{2,1,0:T(8,128)(2,1)}), bf16[16,16,2048]{2,1,0:T(8,128)(2,1)}, u32[]{:S(2)}, u32[]{:S(2)}) async-start(bf16[16,16,2048]{2,1,0:T(8,128)(2,1)} %bitcast.13), calls=%async_computation.3 | async-start | bytes 2097152 | tf_op jit(solution)/shard_map/all_to_all | solution.py:460

commit v5 on v4

--- a/solution.py
+++ b/solution.py
@@ -161,8 +161,7 @@
 
 def readout_body(
     mine_ref, own_ref, sib_ref, decay_ref, bcoef_ref, ccoef_ref, step_ref, inner_ref, first_ref,
-    skip_ref, gate_ref, weight_ref, out_ref, info_ref, drive_ref, read_ref, inner_all_ref,
-    tokens_ref,
+    skip_ref, gate_ref, weight_ref, out_ref, drive_ref, read_ref, inner_all_ref,
 ):
     rate = -decay_ref[...]
     shape = rate.shape
@@ -205,10 +204,14 @@
     lax.fori_loop(0, length // GROUP, group, (state, bcoef_ref[...], ccoef_ref[...]))
     output = read_ref[...] + skip_ref[...] * inner_all_ref[...]
     output = output * jax.nn.silu(gate_ref[...].astype(F32))
-    share = jnp.dot(output.astype(BF16), weight_ref[...], preferred_element_type=F32).astype(BF16)
-    experts, tall, width = out_ref.shape
-    rows = length // experts
-    slots = tall - rows
+    out_ref[...] = jnp.dot(
+        output.astype(BF16), weight_ref[...], preferred_element_type=F32
+    ).astype(BF16)
+
+
+def pack_grad_body(own_ref, packed_ref, info_ref, tokens_ref, *, count):
+    depth, _, channels = own_ref.shape
+    slots, width = packed_ref.shape
     tokens = info_ref.shape[0] // depth
     start = 2 * count + GROUP
     for z in range(depth):
@@ -221,17 +224,14 @@
                 z, first : first + tokens
             ].astype(F32)
     info = info_ref[...]
-    chosen = slot_maps(info, experts * slots)
-    packed = jnp.zeros((experts * slots, width), F32)
+    chosen = slot_maps(info, slots)
+    packed = jnp.zeros((slots, width), F32)
     for k in range(2):
         at = 2 + 3 * k
         score = info[:, at : at + 1] + info[:, at + 1 : at + 2] + info[:, at + 2 : at + 3]
         grad_rows = (score * tokens_ref[...]).astype(BF16)
         packed = packed + contract_first(chosen[k].astype(BF16), grad_rows)
-    packed = packed.astype(BF16)
-    for e in range(experts):
-        out_ref[e, 0:slots] = packed[e * slots : (e + 1) * slots]
-        out_ref[e, slots:] = share[e * rows : (e + 1) * rows]
+    packed_ref[...] = packed.astype(BF16)
 
 
 def slot_maps(info, slots):
@@ -245,34 +245,33 @@
 
 
 def norm_body(shares_ref, residual_ref, gain_ref, hidden_ref, send_ref):
-    rows = residual_ref.shape[0]
-    start = shares_ref.shape[1] - rows
-    total = shares_ref[0, start:].astype(F32)
+    total = shares_ref[0].astype(F32)
     for c in range(1, shares_ref.shape[0]):
-        total = total + shares_ref[c, start:].astype(F32)
+        total = total + shares_ref[c].astype(F32)
     hidden = residual_ref[...].astype(F32) + total
     hidden_ref[...] = hidden
     scale = lax.rsqrt(jnp.mean(hidden * hidden, axis=1, keepdims=True) + 1e-05)
-    normed = (hidden * scale * gain_ref[...]).astype(BF16)
-    for c in range(send_ref.shape[0]):
-        send_ref[c] = normed
-
-
-def pack_body(tokens_ref, info_ref, slots_ref):
+    send_ref[...] = (hidden * scale * gain_ref[...]).astype(BF16)
+
+
+def pack_body(mine_ref, blocks_ref, info_ref, slots_ref, tokens_ref):
+    core = lax.rem(mine_ref[0], 2)
+    rows = blocks_ref.shape[1]
+    for z in range(tokens_ref.shape[0] // rows):
+        at = slice(z * rows, (z + 1) * rows)
+        tokens_ref[at] = jnp.where(core == 0, blocks_ref[2 * z], blocks_ref[2 * z + 1])
     first, second = slot_maps(info_ref[...], slots_ref.shape[0])
     slots_ref[...] = contract_first((first + second).astype(BF16), tokens_ref[...]).astype(BF16)
 
 
-def grad_act_body(shares_ref, own_hbm, sib_hbm, out_ref, down_ref, sems):
-    experts = shares_ref.shape[0]
-    slots = out_ref.shape[1] // experts
+def grad_act_body(rows_ref, own_hbm, sib_hbm, out_ref, down_ref, sems):
     copies = [
         pltpu.make_async_copy(source, down_ref.at[half], sems.at[half])
         for half, source in enumerate((own_hbm, sib_hbm))
     ]
     for copy in copies:
         copy.start()
-    rows = shares_ref[:, 0:slots].reshape(experts * slots, shares_ref.shape[2])
+    rows = rows_ref[...]
     for half in range(2):
         copies[half].wait()
         out_ref[half] = contract_last(rows, down_ref[half])
@@ -298,26 +297,35 @@
     copies = {}
     for index, (name, source, target) in enumerate(plan):
         copies[name] = pltpu.make_async_copy(source, target, sems.at[index])
-        copies[name].start()
+    queue = [copies[name] for name, _, _ in plan]
+    for copy in queue[:3]:
+        copy.start()
+    waiting = queue[3:]
+
+    def ready(name):
+        copies[name].wait()
+        if waiting:
+            waiting.pop(0).start()
+
     dots_ref[...] = jnp.zeros(dots_ref.shape, F32)
     tall = 16
     rows = rows_ref[...]
     for half in range(2):
         if half == 0:
-            copies["gate_top"].wait()
+            ready("gate_top")
             top = jnp.dot(
                 rows[:, 0:half_width], gate_ref[0, 0:half_width], preferred_element_type=F32
             )
-            copies["gate_end"].wait()
+            ready("gate_end")
             gate_pre_ref[...] = top + jnp.dot(
                 rows[:, half_width:], gate_ref[0, half_width:], preferred_element_type=F32
             )
-            copies["up0"].wait()
+            ready("up0")
             up_pre_ref[...] = jnp.dot(rows, up_ref[0], preferred_element_type=F32)
         else:
-            copies["gate1"].wait()
+            ready("gate1")
             gate_pre_ref[...] = jnp.dot(rows, gate_ref[1], preferred_element_type=F32)
-            copies["up1"].wait()
+            ready("up1")
             up_pre_ref[...] = jnp.dot(rows, up_ref[1], preferred_element_type=F32)
 
         def chunk(r, carry):
@@ -345,9 +353,9 @@
     high = dots.astype(BF16).astype(F32)
     lane = lax.broadcasted_iota(jnp.int32, (slots, LANES), 1)
     out_ref[:, 2 * width :] = jnp.where(lane == 0, high, dots - high).astype(BF16)
-    copies["down0"].wait()
+    ready("down0")
     share = jnp.dot(act_ref[0], down_ref[0], preferred_element_type=F32)
-    copies["down1"].wait()
+    ready("down1")
     share = share + jnp.dot(act_ref[1], down_ref[1], preferred_element_type=F32)
     out_ref[:, 0:width] = share.astype(BF16)
     share = contract_last(grad_gate_ref[0], gate_ref[0]) + contract_last(grad_up_ref[0], up_ref[0])
@@ -375,12 +383,13 @@
         both, back_ref[:, width : 2 * width], preferred_element_type=F32
     ).astype(BF16)
     lane = lax.broadcasted_iota(jnp.int32, (tokens, LANES), 1)
+    packed = jnp.zeros(lane.shape, F32)
     for k, chosen in enumerate((first, second)):
         dots = jnp.dot(chosen.astype(BF16), back_ref[:, 2 * width :], preferred_element_type=F32)
         dots = jnp.broadcast_to(dots[:, 0:1] + dots[:, 1:2], dots.shape)
-        high = dots.astype(BF16).astype(F32)
-        start = 2 * width + k * LANES
-        out_ref[:, start : start + LANES] = jnp.where(lane == 0, high, dots - high).astype(BF16)
+        for part, value in enumerate(parts_of(dots, 2)):
+            packed = jnp.where(lane == 2 * k + part, value, packed)
+    out_ref[:, 2 * width :] = packed.astype(BF16)
 
 
 def finish_body(
@@ -403,7 +412,7 @@
     lane = lax.broadcasted_iota(jnp.int32, (rows, rows), 1)
     sub = lax.broadcasted_iota(jnp.int32, (rows, rows), 0)
     for k in range(2):
-        start = 2 * width + k * LANES
+        start = 2 * width + 2 * k
         dots = total[:, start : start + 1] + total[:, start + 1 : start + 2]
         spread = jnp.where(lane == sub, jnp.broadcast_to(dots, lane.shape), 0.0)
         dots = jnp.sum(spread, axis=0, keepdims=True)
@@ -501,38 +510,41 @@
         ups = (up_weight[0], sibling(up_sent))
         downs = (down_weight[0], sibling(down_sent))
         mine = lax.axis_index(("z", "core")).astype(jnp.int32).reshape(1)
-        tall = tok_rows + stride
-        share, info = call(
-            readout_body, "readout",
-            (near((experts, tall, width), BF16), near((depth * tok_rows, LANES), F32)),
+        own = gathered.reshape(summary.shape)
+        share = call(
+            readout_body, "readout", near((length, width), BF16),
             [SMEM] + [NEAR] * 2 + [VMEM] * 3 + [NEAR] * 3 + [VMEM] * 3,
             (
                 pltpu.VMEM((length, channels), F32), pltpu.VMEM((length, channels), F32),
-                pltpu.VMEM((length, channels), F32), pltpu.VMEM((depth * tok_rows, width), F32),
-            ),
-            (
-                mine, gathered.reshape(summary.shape), gathered_sib.reshape(summary.shape),
-                decay_rate, input_coef, output_coef, step, inner, inner_first,
-                skip_gain[None], mixer_gate, out_weight,
-            ),
-        )
-        shares = exchange(share.reshape(experts * tall, width), "exp")
-        shares = shares.reshape(experts, tall, width)
-        hidden, send = call(
-            norm_body, "norm",
-            (near((tok_rows, width), F32), near((depth, tok_rows, width), BF16)),
+                pltpu.VMEM((length, channels), F32),
+            ),
+            (
+                mine, own, gathered_sib.reshape(summary.shape), decay_rate, input_coef,
+                output_coef, step, inner, inner_first, skip_gain[None], mixer_gate, out_weight,
+            ),
+        )
+        packed_grad, info = call(
+            pack_grad_body, "pack_grad",
+            (near((slots, width), BF16), near((depth * tok_rows, LANES), F32)),
+            [NEAR], (pltpu.VMEM((depth * tok_rows, width), F32),), (own,), count=count,
+        )
+        shares, packed_grad = lax.optimization_barrier((exchange(share, "exp"), packed_grad))
+        rows_d = exchange(packed_grad, "exp")
+        hidden, normed = call(
+            norm_body, "norm", (near((tok_rows, width), F32), near((tok_rows, width), BF16)),
             [NEAR] + [VMEM] * 2,
-            operands=(shares, residual, norm_gain[None]),
-        )
-        tokens = exchange(send.reshape(depth * tok_rows, width), "z")
+            operands=(shares.reshape(experts, tok_rows, width), residual, norm_gain[None]),
+        )
+        blocks = lax.all_gather(normed, ("z", "core"), axis=0)
         packed = call(
-            pack_body, "pack", near((slots, width), BF16), [NEAR] * 2, operands=(tokens, info)
+            pack_body, "pack", near((slots, width), BF16), [SMEM] + [NEAR] * 2,
+            (pltpu.VMEM((depth * tok_rows, width), BF16),), (mine, blocks, info),
         )
         rows_x = exchange(packed, "exp")
         grad_act = call(
             grad_act_body, "grad_act", near((2, slots, units), F32), [NEAR] + [ANY] * 2,
             (pltpu.VMEM((2, units, width), BF16), pltpu.SemaphoreType.DMA((2,))),
-            (shares,) + downs,
+            (rows_d,) + downs,
         )
         result = call(
             expert_body, "expert", near((slots, 2 * width + LANES), BF16),
@@ -554,10 +566,10 @@
         )
         back = exchange(result, "exp")
         shares_back = call(
-            combine_body, "combine", near((depth * tok_rows, 2 * width + 2 * LANES), BF16),
+            combine_body, "combine", near((depth * tok_rows, 2 * width + LANES), BF16),
             [NEAR] * 2, operands=(back, info),
         )
-        mine_back = exchange(shares_back, "z").reshape(depth, tok_rows, 2 * width + 2 * LANES)
+        mine_back = exchange(shares_back, "z").reshape(depth, tok_rows, 2 * width + LANES)
         layer_out, grad_hidden, dots = call(
             finish_body, "finish",
             (

time: 172 us -> 175 us (1.017)
  blocking collectives: 118 us -> 93.8 us
  starting transfers between devices: 8.42 us -> 22.9 us
  waiting for transfers between devices: 10.4 us -> 21 us
  Pallas kernels: 34.3 us -> 36.3 us
    all_to_all x5 -> x3, blocking collectives: 118 us -> 77.6 us  [exchange(): return lax.all_to_all(rows, axis, split_axis=0, concat_axis=0, tiled=True)]
    all_gather x0 -> x1, blocking collectives: none -> 16.1 us  [per_device(): blocks = lax.all_gather(normed, ('z', 'core'), axis=0)]
    all_to_all x1 -> x3, starting transfers between devices: 6.03 us -> 20.6 us  [exchange(): return lax.all_to_all(rows, axis, split_axis=0, concat_axis=0, tiled=True)]
    all_to_all x1 -> x3, waiting for transfers between devices: 8.61 us -> 19.1 us  [exchange(): return lax.all_to_all(rows, axis, split_axis=0, concat_axis=0, tiled=True)]
    pallas_call x9 -> x10, Pallas kernels: 34.3 us -> 36.3 us  [call(): pl.pallas_call(body, out_shape=outs, in_specs=[VMEM if spec is NEAR else...]
  transfers between devices with their start and end apart: 6 -> 8, of which waited for: 2 -> 3; matrix products, arithmetic and copies ran while one was open for 0% -> 0% of each run, Pallas kernels for 8% -> 9%
where the time goes in v5:
time: 175 us
  blocking collectives  93.8 us (54%)
  Pallas kernels  36.3 us (21%)
  starting transfers between devices  22.9 us (13%)
  waiting for transfers between devices  21 us (12%)
    all_to_all x3, blocking collectives, exchange(): return lax.all_to_all(rows, axis, split_axis=0, concat_axis=0, tiled=True)  77.6 us
    pallas_call x10, Pallas kernels, call(): pl.pallas_call(body, out_shape=outs, in_specs=[VMEM if spec is NEAR else...  36.3 us
    all_to_all x3, starting transfers between devices, exchange(): return lax.all_to_all(rows, axis, split_axis=0, concat_axis=0, tiled=True)  20.6 us
    all_to_all x3, waiting for transfers between devices, exchange(): return lax.all_to_all(rows, axis, split_axis=0, concat_axis=0, tiled=True)  19.1 us
    all_gather x1, blocking collectives, per_device(): blocks = lax.all_gather(normed, ('z', 'core'), axis=0)  16.1 us
  transfers between devices with their start and end apart: 8, of which 3 were waited for; matrix products, arithmetic and copies ran while one was open for 0% of the time, Pallas kernels for 9%

profile of v5, /device:TPU:2, one launch (start us, length us, event | category | flops | bytes accessed | tf_op | source)
XLA Modules:
  0.0 174.6 jit_solution(17668065064166250608)
XLA Ops:
  0.6 1.7 collective-permute-start
  2.4 2.7 %local_state.1 = (f32[24,256]{1,0:T(8,128)S(1)}, f32[128,256]{1,0:T(8,128)S(1)}, f32[128,256]{1,0:T(8,128)S(1)}, bf16[72,256]{1,0:T(8,128)(2,1)S(1)}) custom-call(bf16[128,256]{1,0:T(8,128)(2,1)} %x_ref.3, bf16[128,128]{1,0:T(8,128)(2,1)} %low_ref.1, bf16[128,256]{1,0:T(8,128)(2,1)} %proj_ref.1, f32[1,256]{1,0:T(1,128)} %bitcast.44, f32[16,256]{1,0:T(8,128)} %decay_ref.5, ...), custom_call_target="tpu_custom_call" | custom-call | tf_op jit(solution)/shard_map/local_state/pallas_call | solution.py:436
  5.1 1.0 first_group.1
  6.1 25.8 %all_to_all.63.own_ref = bf16[8,112,256]{2,1,0:T(8,128)(2,1)S(1)} all-to-all(bf16[8,112,256]{2,1,0:T(8,128)(2,1)S(1)} %get-tuple-element.25), channel_id=1, replica_groups=mesh['z'=8,'core'=2,'exp'=16] {'z'}, dimensions={0} | all-to-all | bytes 917504 | tf_op jit(solution)/shard_map/all_to_all | solution.py:469
  31.9 1.8 %collective-permute-done.1 = bf16[896,256]{1,0:T(8,128)(2,1)S(1)} collective-permute-done((bf16[896,256]{1,0:T(8,128)(2,1)S(1)}, bf16[896,256]{1,0:T(8,128)(2,1)S(1)}, u32[]{:S(2)}, u32[]{:S(2)}) %collective-permute-start.1) | collective-permute-done | bytes 458784 | tf_op jit(solution)/shard_map/ppermute | solution.py:466
  33.8 0.1 collective-permute-start.2
  33.9 0.4 collective-permute-start.3
  34.3 0.1 collective-permute-start.4
  34.4 4.6 %readout.1 = bf16[128,2048]{1,0:T(8,128)(2,1)} custom-call(s32[1]{0:T(128)} %bitcast.mine_ref, bf16[8,112,256]{2,1,0:T(8,128)(2,1)S(1)} %all_to_all.63.own_ref, bf16[8,112,256]{2,1,0:T(8,128)(2,1)S(1)} %bitcast.30, f32[16,256]{1,0:T(8,128)} %decay_ref.5, f32[16,128]{1,0:T(8,128)} %bcoef_ref.5, f32[16,128]{1,0:T(8,128)} %ccoef_ref.1, ...), custom_call_target="tpu_custom_call" | custom-call | tf_op jit(solution)/shard_map/readout/pallas_call | solution.py:436
  39.0 7.5 %all-to-all-start.1 = ((bf16[16,8,2048]{2,1,0:T(8,128)(2,1)}), bf16[16,8,2048]{2,1,0:T(8,128)(2,1)S(1)}, u32[]{:S(2)}, u32[]{:S(2)}) async-start(bf16[16,8,2048]{2,1,0:T(8,128)(2,1)} %bitcast.11), calls=%async_computation.1 | async-start | bytes 1048576 | tf_op jit(solution)/shard_map/all_to_all | solution.py:469
  46.5 1.8 %pack_grad.1 = (bf16[256,2048]{1,0:T(8,128)(2,1)}, f32[64,128]{1,0:T(8,128)S(1)}) custom-call(bf16[8,112,256]{2,1,0:T(8,128)(2,1)S(1)} %all_to_all.63.own_ref), custom_call_target="tpu_custom_call" | custom-call | tf_op jit(solution)/shard_map/pack_grad/pallas_call | solution.py:436
  48.3 8.0 %all-to-all-done.1 = bf16[16,8,2048]{2,1,0:T(8,128)(2,1)S(1)} async-done(((bf16[16,8,2048]{2,1,0:T(8,128)(2,1)}), bf16[16,8,2048]{2,1,0:T(8,128)(2,1)S(1)}, u32[]{:S(2)}, u32[]{:S(2)}) %all-to-all-start.1) | async-done | bytes 524320 | tf_op jit(solution)/shard_map/all_to_all | solution.py:469
  56.2 5.8 %all-to-all-start.3 = ((bf16[16,16,2048]{2,1,0:T(8,128)(2,1)}), bf16[16,16,2048]{2,1,0:T(8,128)(2,1)S(1)}, u32[]{:S(2)}, u32[]{:S(2)}) async-start(bf16[16,16,2048]{2,1,0:T(8,128)(2,1)} %bitcast.18), calls=%async_computation.3 | async-start | bytes 2097152 | tf_op jit(solution)/shard_map/all_to_all | solution.py:469
  62.0 0.9 norm.1
  63.0 16.1 %all-gather = bf16[128,2048]{1,0:T(8,128)(2,1)S(1)} all-gather(bf16[8,2048]{1,0:T(8,128)(2,1)S(1)} %get-tuple-element.31), channel_id=2, replica_groups=mesh['z'=8,'core'=2,'exp'=16] {'z','core'}, dimensions={0}, use_global_device_ids=true | all-gather | bytes 557056 | tf_op jit(solution)/shard_map/all_gather | solution.py:538
  79.1 1.6 pack.1
  80.7 7.3 %all-to-all-start.2 = ((bf16[16,16,2048]{2,1,0:T(8,128)(2,1)}), bf16[16,16,2048]{2,1,0:T(8,128)(2,1)}, u32[]{:S(2)}, u32[]{:S(2)}) async-start(bf16[16,16,2048]{2,1,0:T(8,128)(2,1)} %bitcast.16), calls=%async_computation.2 | async-start | bytes 2097152 | tf_op jit(solution)/shard_map/all_to_all | solution.py:469
  87.9 4.6 %grad_act.1.grad_act_ref = f32[2,256,896]{2,1,0:T(8,128)S(1)} custom-call(bf16[256,2048]{1,0:T(8,128)(2,1)S(1)} %bitcast.26, bf16[896,2048]{1,0:T(8,128)(2,1)} %bitcast.32, bf16[896,2048]{1,0:T(8,128)(2,1)} %collective-permute-done.2.sib_hbm.down_sib_hbm), custom_call_target="tpu_custom_call" | custom-call | tf_op jit(solution)/shard_map/grad_act/pallas_call | solution.py:436
  92.5 11.2 %all-to-all-done.2 = bf16[16,16,2048]{2,1,0:T(8,128)(2,1)} async-done(((bf16[16,16,2048]{2,1,0:T(8,128)(2,1)}), bf16[16,16,2048]{2,1,0:T(8,128)(2,1)}, u32[]{:S(2)}, u32[]{:S(2)}) %all-to-all-start.2) | async-done | bytes 1048608 | tf_op jit(solution)/shard_map/all_to_all | solution.py:469
  103.7 16.8 %expert.1 = bf16[256,4224]{1,0:T(8,128)(2,1)S(1)} custom-call(bf16[256,2048]{1,0:T(8,128)(2,1)} %bitcast.17.rows_ref, f32[2,256,896]{2,1,0:T(8,128)S(1)} %grad_act.1.grad_act_ref, bf16[2048,896]{1,0:T(8,128)(2,1)} %bitcast.35, bf16[2048,896]{1,0:T(8,128)(2,1)} %collective-permute-done.3.gate_sib_hbm, bf16[2048,896]{1,0:T(8,128)(2,1)} %bitcast.37, ...), custom_call_target="tpu_custom_call" | custom-call | tf_op jit(solution)/shard_map/expert/pallas_call | solution.py:436
  120.6 32.7 %all_to_all.64 = bf16[16,16,4224]{2,1,0:T(8,128)(2,1)S(1)} all-to-all(bf16[16,16,4224]{2,1,0:T(8,128)(2,1)S(1)} %bitcast.24), channel_id=1, replica_groups=mesh['z'=8,'core'=2,'exp'=16] {'exp'}, dimensions={0} | all-to-all | bytes 4325376 | tf_op jit(solution)/shard_map/all_to_all | solution.py:469
  153.3 0.7 combine.1
  154.0 19.1 %all_to_all.65.back_ref = bf16[8,8,4224]{2,1,0:T(8,128)(2,1)S(1)} all-to-all(bf16[8,8,4224]{2,1,0:T(8,128)(2,1)S(1)} %bitcast.28), channel_id=1, replica_groups=mesh['z'=8,'core'=2,'exp'=16] {'z'}, dimensions={0} | all-to-all | bytes 1081344 | tf_op jit(solution)/shard_map/all_to_all | solution.py:469
  173.1 1.6 finish.1
  (6 shorter events, 0.0 us)
Async XLA Ops:
  0.6 4.5 %collective-permute-start = (bf16[128,256]{1,0:T(8,128)(2,1)}, bf16[128,256]{1,0:T(8,128)(2,1)S(1)}, u32[]{:S(2)}, u32[]{:S(2)}) collective-permute-start(bf16[128,256]{1,0:T(8,128)(2,1)} %x_ref.3), channel_id=1, source_target_pairs={{0,16},{16,32},{32,48},{48,64},{64,80},{80,96},{96,112},{112,128},... | collective-permute-start | bytes 196616 | tf_op jit(solution)/shard_map/ppermute | solution.py:471
  31.9 1.8 %collective-permute-start.1 = (bf16[896,256]{1,0:T(8,128)(2,1)S(1)}, bf16[896,256]{1,0:T(8,128)(2,1)S(1)}, u32[]{:S(2)}, u32[]{:S(2)}) collective-permute-start(bf16[896,256]{1,0:T(8,128)(2,1)S(1)} %bitcast.27), channel_id=1, source_target_pairs={{0,16},{16,0},{1,17},{17,1},{2,18},{18,2},{3,19},{19,3},{4,20},{20... | collective-permute-start | bytes 1376264 | tf_op jit(solution)/shard_map/ppermute | solution.py:466
  33.8 54.2 %collective-permute-start.2 = (bf16[896,2048]{1,0:T(8,128)(2,1)}, bf16[896,2048]{1,0:T(8,128)(2,1)}, u32[]{:S(2)}, u32[]{:S(2)}) collective-permute-start(bf16[896,2048]{1,0:T(8,128)(2,1)} %bitcast.31), channel_id=1, source_target_pairs={{0,16},{16,0},{1,17},{17,1},{2,18},{18,2},{3,19},{19,3},{4,20},{20... | collective-permute-start | bytes 11010056 | tf_op jit(solution)/shard_map/ppermute | solution.py:466
  33.9 69.8 %collective-permute-start.3 = (bf16[2048,896]{1,0:T(8,128)(2,1)}, bf16[2048,896]{1,0:T(8,128)(2,1)}, u32[]{:S(2)}, u32[]{:S(2)}) collective-permute-start(bf16[2048,896]{1,0:T(8,128)(2,1)} %bitcast.34), channel_id=1, source_target_pairs={{0,16},{16,0},{1,17},{17,1},{2,18},{18,2},{3,19},{19,3},{4,20},{20... | collective-permute-start | bytes 11010056 | tf_op jit(solution)/shard_map/ppermute | solution.py:466
  34.3 69.5 %collective-permute-start.4 = (bf16[2048,896]{1,0:T(8,128)(2,1)}, bf16[2048,896]{1,0:T(8,128)(2,1)}, u32[]{:S(2)}, u32[]{:S(2)}) collective-permute-start(bf16[2048,896]{1,0:T(8,128)(2,1)} %bitcast.36), channel_id=1, source_target_pairs={{0,16},{16,0},{1,17},{17,1},{2,18},{18,2},{3,19},{19,3},{4,20},{20... | collective-permute-start | bytes 11010056 | tf_op jit(solution)/shard_map/ppermute | solution.py:466
  39.0 17.3 %all-to-all-start.1 = ((bf16[16,8,2048]{2,1,0:T(8,128)(2,1)}), bf16[16,8,2048]{2,1,0:T(8,128)(2,1)S(1)}, u32[]{:S(2)}, u32[]{:S(2)}) async-start(bf16[16,8,2048]{2,1,0:T(8,128)(2,1)} %bitcast.11), calls=%async_computation.1 | async-start | bytes 1048576 | tf_op jit(solution)/shard_map/all_to_all | solution.py:469
  56.2 24.4 %all-to-all-start.3 = ((bf16[16,16,2048]{2,1,0:T(8,128)(2,1)}), bf16[16,16,2048]{2,1,0:T(8,128)(2,1)S(1)}, u32[]{:S(2)}, u32[]{:S(2)}) async-start(bf16[16,16,2048]{2,1,0:T(8,128)(2,1)} %bitcast.18), calls=%async_computation.3 | async-start | bytes 2097152 | tf_op jit(solution)/shard_map/all_to_all | solution.py:469
  80.7 23.1 %all-to-all-start.2 = ((bf16[16,16,2048]{2,1,0:T(8,128)(2,1)}), bf16[16,16,2048]{2,1,0:T(8,128)(2,1)}, u32[]{:S(2)}, u32[]{:S(2)}) async-start(bf16[16,16,2048]{2,1,0:T(8,128)(2,1)} %bitcast.16), calls=%async_computation.2 | async-start | bytes 2097152 | tf_op jit(solution)/shard_map/all_to_all | solution.py:469

commit v6 on v4

--- a/solution.py
+++ b/solution.py
@@ -153,14 +153,13 @@
     extra = extra_ref[0:GROUP].astype(F32)
     sums = jnp.concatenate([total, extra], 0).astype(BF16)
     rest = extra_ref[GROUP:]
-    for z in range(send_ref.shape[0]):
-        send_ref[z, 0 : 2 * count] = states
-        send_ref[z, 2 * count : 2 * count + 2 * GROUP] = sums
-        send_ref[z, 2 * count + 2 * GROUP :] = rest
+    send_ref[0 : 2 * count] = states
+    send_ref[2 * count : 2 * count + 2 * GROUP] = sums
+    send_ref[2 * count + 2 * GROUP :] = rest
 
 
 def readout_body(
-    mine_ref, own_ref, sib_ref, decay_ref, bcoef_ref, ccoef_ref, step_ref, inner_ref, first_ref,
+    mine_ref, gathered_ref, decay_ref, bcoef_ref, ccoef_ref, step_ref, inner_ref, first_ref,
     skip_ref, gate_ref, weight_ref, out_ref, info_ref, drive_ref, read_ref, inner_all_ref,
     tokens_ref,
 ):
@@ -168,21 +167,16 @@
     shape = rate.shape
     count, channels = shape
     length = step_ref.shape[0]
-    depth = own_ref.shape[0]
+    depth = gathered_ref.shape[0] // 2
     mine = mine_ref[0]
     core = lax.rem(mine, 2)
     state = jnp.zeros(shape, F32)
-    for z in range(depth):
-        pair = []
-        for ref in (own_ref, sib_ref):
-            piece = ref[z, 0 : 2 * count].astype(F32)
-            sums = ref[z, 2 * count : 2 * count + 2 * GROUP].astype(F32)
-            total = jnp.broadcast_to(sums[0:1] + sums[1:2], shape)
-            pair.append((jnp.exp(total * rate), piece[0:count] + piece[count:]))
-        for k in range(2):
-            factor = jnp.where(core == k, pair[0][0], pair[1][0])
-            offset = jnp.where(core == k, pair[0][1], pair[1][1])
-            state = jnp.where(2 * z + k < mine, factor * state + offset, state)
+    for c in range(2 * depth - 1):
+        piece = gathered_ref[c, 0 : 2 * count].astype(F32)
+        sums = gathered_ref[c, 2 * count : 2 * count + 2 * GROUP].astype(F32)
+        total = jnp.broadcast_to(sums[0:1] + sums[1:2], shape)
+        longer = jnp.exp(total * rate) * state + (piece[0:count] + piece[count:])
+        state = jnp.where(c < mine, longer, state)
     inner_all_ref[...] = inner_ref[...]
     inner_all_ref[0:GROUP] = first_ref[...]
     drive_ref[...] = step_ref[...] * inner_all_ref[...]
@@ -213,12 +207,13 @@
     start = 2 * count + GROUP
     for z in range(depth):
         at = slice(z * tokens, (z + 1) * tokens)
-        extra = own_ref[z, 2 * count : 2 * count + 2 * GROUP].astype(F32)
+        place = 2 * z + core
+        extra = gathered_ref[place, 2 * count : 2 * count + 2 * GROUP].astype(F32)
         info_ref[at] = extra[GROUP:, 0:LANES]
         for b in range(width // channels):
             first = start + (b + 1) * tokens
-            tokens_ref[at, b * channels : (b + 1) * channels] = own_ref[
-                z, first : first + tokens
+            tokens_ref[at, b * channels : (b + 1) * channels] = gathered_ref[
+                place, first : first + tokens
             ].astype(F32)
     info = info_ref[...]
     chosen = slot_maps(info, experts * slots)
@@ -263,62 +258,42 @@
     slots_ref[...] = contract_first((first + second).astype(BF16), tokens_ref[...]).astype(BF16)
 
 
-def grad_act_body(shares_ref, own_hbm, sib_hbm, out_ref, down_ref, sems):
-    experts = shares_ref.shape[0]
-    slots = out_ref.shape[1] // experts
-    copies = [
-        pltpu.make_async_copy(source, down_ref.at[half], sems.at[half])
-        for half, source in enumerate((own_hbm, sib_hbm))
-    ]
-    for copy in copies:
-        copy.start()
-    rows = shares_ref[:, 0:slots].reshape(experts * slots, shares_ref.shape[2])
-    for half in range(2):
-        copies[half].wait()
-        out_ref[half] = contract_last(rows, down_ref[half])
-
-
 def expert_body(
-    rows_ref, grad_act_ref, gate_hbm, gate_sib_hbm, up_hbm, up_sib_hbm, down_hbm, down_sib_hbm,
+    rows_ref, shares_ref, gate_hbm, gate_sib_hbm, up_hbm, up_sib_hbm, down_hbm, down_sib_hbm,
     out_ref, gate_ref, up_ref, down_ref, gate_pre_ref, up_pre_ref, act_ref, grad_gate_ref,
-    grad_up_ref, dots_ref, sems,
+    grad_up_ref, dots_ref, grad_act_ref, sems,
 ):
     slots, width = rows_ref.shape
     units = gate_ref.shape[2]
-    half_width = width // 2
     plan = (
-        ("gate_top", gate_hbm.at[0:half_width], gate_ref.at[0, 0:half_width]),
-        ("gate_end", gate_hbm.at[half_width:width], gate_ref.at[0, half_width:width]),
-        ("up0", up_hbm, up_ref.at[0]),
-        ("gate1", gate_sib_hbm, gate_ref.at[1]),
-        ("up1", up_sib_hbm, up_ref.at[1]),
-        ("down0", down_hbm, down_ref.at[0]),
-        ("down1", down_sib_hbm, down_ref.at[1]),
-    )
-    copies = {}
-    for index, (name, source, target) in enumerate(plan):
-        copies[name] = pltpu.make_async_copy(source, target, sems.at[index])
-        copies[name].start()
+        (down_hbm, down_ref, 0), (down_sib_hbm, down_ref, 1), (gate_hbm, gate_ref, 0),
+        (up_hbm, up_ref, 0), (gate_sib_hbm, gate_ref, 1), (up_sib_hbm, up_ref, 1),
+    )
+    copies = [
+        pltpu.make_async_copy(source, target.at[half], sems.at[index])
+        for index, (source, target, half) in enumerate(plan)
+    ]
+    for copy in copies[:3]:
+        copy.start()
+
+    def ready(index):
+        copies[index].wait()
+        if index + 3 < len(copies):
+            copies[index + 3].start()
+
+    experts = shares_ref.shape[0]
+    grad_rows = shares_ref[:, 0 : slots // experts].reshape(slots, width)
+    for half in range(2):
+        ready(half)
+        grad_act_ref[half] = contract_last(grad_rows, down_ref[half])
     dots_ref[...] = jnp.zeros(dots_ref.shape, F32)
     tall = 16
     rows = rows_ref[...]
     for half in range(2):
-        if half == 0:
-            copies["gate_top"].wait()
-            top = jnp.dot(
-                rows[:, 0:half_width], gate_ref[0, 0:half_width], preferred_element_type=F32
-            )
-            copies["gate_end"].wait()
-            gate_pre_ref[...] = top + jnp.dot(
-                rows[:, half_width:], gate_ref[0, half_width:], preferred_element_type=F32
-            )
-            copies["up0"].wait()
-            up_pre_ref[...] = jnp.dot(rows, up_ref[0], preferred_element_type=F32)
-        else:
-            copies["gate1"].wait()
-            gate_pre_ref[...] = jnp.dot(rows, gate_ref[1], preferred_element_type=F32)
-            copies["up1"].wait()
-            up_pre_ref[...] = jnp.dot(rows, up_ref[1], preferred_element_type=F32)
+        ready(2 + 2 * half)
+        gate_pre_ref[...] = jnp.dot(rows, gate_ref[half], preferred_element_type=F32)
+        ready(3 + 2 * half)
+        up_pre_ref[...] = jnp.dot(rows, up_ref[half], preferred_element_type=F32)
 
         def chunk(r, carry):
             at = pl.ds(pl.multiple_of(r * tall, tall), tall)
@@ -345,9 +320,7 @@
     high = dots.astype(BF16).astype(F32)
     lane = lax.broadcasted_iota(jnp.int32, (slots, LANES), 1)
     out_ref[:, 2 * width :] = jnp.where(lane == 0, high, dots - high).astype(BF16)
-    copies["down0"].wait()
     share = jnp.dot(act_ref[0], down_ref[0], preferred_element_type=F32)
-    copies["down1"].wait()
     share = share + jnp.dot(act_ref[1], down_ref[1], preferred_element_type=F32)
     out_ref[:, 0:width] = share.astype(BF16)
     share = contract_last(grad_gate_ref[0], gate_ref[0]) + contract_last(grad_up_ref[0], up_ref[0])
@@ -375,12 +348,13 @@
         both, back_ref[:, width : 2 * width], preferred_element_type=F32
     ).astype(BF16)
     lane = lax.broadcasted_iota(jnp.int32, (tokens, LANES), 1)
+    packed = jnp.zeros(lane.shape, F32)
     for k, chosen in enumerate((first, second)):
         dots = jnp.dot(chosen.astype(BF16), back_ref[:, 2 * width :], preferred_element_type=F32)
         dots = jnp.broadcast_to(dots[:, 0:1] + dots[:, 1:2], dots.shape)
-        high = dots.astype(BF16).astype(F32)
-        start = 2 * width + k * LANES
-        out_ref[:, start : start + LANES] = jnp.where(lane == 0, high, dots - high).astype(BF16)
+        for part, value in enumerate(parts_of(dots, 2)):
+            packed = jnp.where(lane == 2 * k + part, value, packed)
+    out_ref[:, 2 * width :] = packed.astype(BF16)
 
 
 def finish_body(
@@ -403,7 +377,7 @@
     lane = lax.broadcasted_iota(jnp.int32, (rows, rows), 1)
     sub = lax.broadcasted_iota(jnp.int32, (rows, rows), 0)
     for k in range(2):
-        start = 2 * width + k * LANES
+        start = 2 * width + 2 * k
         dots = total[:, start : start + 1] + total[:, start + 1 : start + 2]
         spread = jnp.where(lane == sub, jnp.broadcast_to(dots, lane.shape), 0.0)
         dots = jnp.sum(spread, axis=0, keepdims=True)
@@ -481,7 +455,7 @@
         summary, inner_first = call(
             first_group_body, "first_group",
             (
-                near((depth, 2 * count + GROUP + extra_rows, channels), BF16),
+                near((2 * count + GROUP + extra_rows, channels), BF16),
                 near((GROUP, channels), F32),
             ),
             [NEAR] + [VMEM] * 3 + [NEAR] + [VMEM] * 2 + [NEAR] * 2,
@@ -491,11 +465,9 @@
                 late, extra,
             ),
         )
-        tall = summary.shape[1]
-        gathered = exchange(summary.reshape(depth * tall, channels), "z")
-        gathered_sib = sibling(gathered)
-        gathered_sib, gate_sent, up_sent, down_sent = lax.optimization_barrier(
-            (gathered_sib, gate_weight[0], up_weight[0], down_weight[0])
+        gathered = lax.all_gather(summary, ("z", "core"), axis=0)
+        gathered, gate_sent, up_sent, down_sent = lax.optimization_barrier(
+            (gathered, gate_weight[0], up_weight[0], down_weight[0])
         )
         gates = (gate_weight[0], sibling(gate_sent))
         ups = (up_weight[0], sibling(up_sent))
@@ -505,14 +477,13 @@
         share, info = call(
             readout_body, "readout",
             (near((experts, tall, width), BF16), near((depth * tok_rows, LANES), F32)),
-            [SMEM] + [NEAR] * 2 + [VMEM] * 3 + [NEAR] * 3 + [VMEM] * 3,
+            [SMEM, NEAR] + [VMEM] * 3 + [NEAR] * 3 + [VMEM] * 3,
             (
                 pltpu.VMEM((length, channels), F32), pltpu.VMEM((length, channels), F32),
                 pltpu.VMEM((length, channels), F32), pltpu.VMEM((depth * tok_rows, width), F32),
             ),
             (
-                mine, gathered.reshape(summary.shape), gathered_sib.reshape(summary.shape),
-                decay_rate, input_coef, output_coef, step, inner, inner_first,
+                mine, gathered, decay_rate, input_coef, output_coef, step, inner, inner_first,
                 skip_gain[None], mixer_gate, out_weight,
             ),
         )
@@ -529,11 +500,6 @@
             pack_body, "pack", near((slots, width), BF16), [NEAR] * 2, operands=(tokens, info)
         )
         rows_x = exchange(packed, "exp")
-        grad_act = call(
-            grad_act_body, "grad_act", near((2, slots, units), F32), [NEAR] + [ANY] * 2,
-            (pltpu.VMEM((2, units, width), BF16), pltpu.SemaphoreType.DMA((2,))),
-            (shares,) + downs,
-        )
         result = call(
             expert_body, "expert", near((slots, 2 * width + LANES), BF16),
             [NEAR] * 2 + [ANY] * 6,
@@ -547,17 +513,18 @@
                 pltpu.VMEM((2, slots, units), BF16),
                 pltpu.VMEM((2, slots, units), BF16),
                 pltpu.VMEM((slots, LANES), F32),
-                pltpu.SemaphoreType.DMA((7,)),
-            ),
-            (rows_x, grad_act) + gates + ups + downs,
+                pltpu.VMEM((2, slots, units), F32),
+                pltpu.SemaphoreType.DMA((6,)),
+            ),
+            (rows_x, shares) + gates + ups + downs,
             48,
         )
         back = exchange(result, "exp")
         shares_back = call(
-            combine_body, "combine", near((depth * tok_rows, 2 * width + 2 * LANES), BF16),
+            combine_body, "combine", near((depth * tok_rows, 2 * width + LANES), BF16),
             [NEAR] * 2, operands=(back, info),
         )
-        mine_back = exchange(shares_back, "z").reshape(depth, tok_rows, 2 * width + 2 * LANES)
+        mine_back = exchange(shares_back, "z").reshape(depth, tok_rows, 2 * width + LANES)
         layer_out, grad_hidden, dots = call(
             finish_body, "finish",
             (

time: 172 us -> 167 us (0.971)
  blocking collectives: 118 us -> 133 us
  waiting for transfers between devices: 10.4 us -> 0.01 us
  starting transfers between devices: 8.42 us -> 2.6 us
  Pallas kernels: 34.3 us -> 29.6 us
    all_gather x0 -> x1, blocking collectives: none -> 23.8 us  [per_device(): gathered = lax.all_gather(summary, ('z', 'core'), axis=0)]
    all_to_all x1 -> x0, waiting for transfers between devices: 8.61 us -> none  [exchange(): return lax.all_to_all(rows, axis, split_axis=0, concat_axis=0, tiled=True)]
    all_to_all x5, blocking collectives: 118 us -> 110 us  [exchange(): return lax.all_to_all(rows, axis, split_axis=0, concat_axis=0, tiled=True)]
    all_to_all x1 -> x0, starting transfers between devices: 6.03 us -> none  [exchange(): return lax.all_to_all(rows, axis, split_axis=0, concat_axis=0, tiled=True)]
    pallas_call x9 -> x8, Pallas kernels: 34.3 us -> 29.6 us  [call(): pl.pallas_call(body, out_shape=outs, in_specs=[VMEM if spec is NEAR else...]
    ppermute x4 -> x3, waiting for transfers between devices: 1.82 us -> 0.01 us  [sibling(): return lax.ppermute(value, 'core', swap)]
  transfers between devices with their start and end apart: 6 -> 4, of which waited for: 2 -> 0; matrix products, arithmetic and copies ran while one was open for 0% -> 0% of each run, Pallas kernels for 8% -> 5%
where the time goes in v6:
time: 167 us; the launch traced here: 166 us
  blocking collectives  133 us (80%)
  Pallas kernels  29.6 us (18%)
  starting transfers between devices  2.6 us (2%)
    all_to_all x5, blocking collectives, exchange(): return lax.all_to_all(rows, axis, split_axis=0, concat_axis=0, tiled=True)  110 us
    pallas_call x8, Pallas kernels, call(): pl.pallas_call(body, out_shape=outs, in_specs=[VMEM if spec is NEAR else...  29.6 us
    all_gather x1, blocking collectives, per_device(): gathered = lax.all_gather(summary, ('z', 'core'), axis=0)  23.8 us
  transfers between devices with their start and end apart: 4, of which 0 were waited for; matrix products, arithmetic and copies ran while one was open for 0% of the time, Pallas kernels for 5%

profile of v6, /device:TPU:2, one launch (start us, length us, event | category | flops | bytes accessed | tf_op | source)
XLA Modules:
  0.0 166.3 jit_solution(15779047652491523532)
XLA Ops:
  0.6 1.7 %collective-permute-start = (bf16[128,256]{1,0:T(8,128)(2,1)}, bf16[128,256]{1,0:T(8,128)(2,1)S(1)}, u32[]{:S(2)}, u32[]{:S(2)}) collective-permute-start(bf16[128,256]{1,0:T(8,128)(2,1)} %x_ref.3), channel_id=1, source_target_pairs={{0,16},{16,32},{32,48},{48,64},{64,80},{80,96},{96,112},{112,128},... | collective-permute-start | bytes 196616 | tf_op jit(solution)/shard_map/ppermute | solution.py:436
  2.4 2.7 %local_state.1 = (f32[24,256]{1,0:T(8,128)S(1)}, f32[128,256]{1,0:T(8,128)S(1)}, f32[128,256]{1,0:T(8,128)S(1)}, bf16[72,256]{1,0:T(8,128)(2,1)S(1)}) custom-call(bf16[128,256]{1,0:T(8,128)(2,1)} %x_ref.3, bf16[128,128]{1,0:T(8,128)(2,1)} %low_ref.1, bf16[128,256]{1,0:T(8,128)(2,1)} %proj_ref.1, f32[1,256]{1,0:T(1,128)} %bitcast.37, f32[16,256]{1,0:T(8,128)} %decay_ref.5, ...), custom_call_target="tpu_custom_call" | custom-call | tf_op jit(solution)/shard_map/local_state/pallas_call | solution.py:401
  5.1 0.0 collective-permute-done.before_ref
  5.1 1.0 first_group.1
  6.1 23.8 %all-gather = bf16[1792,256]{1,0:T(8,128)(2,1)S(1)} all-gather(bf16[112,256]{1,0:T(8,128)(2,1)S(1)} %get-tuple-element.23), channel_id=2, replica_groups=mesh['z'=8,'core'=2,'exp'=16] {'z','core'}, dimensions={0}, use_global_device_ids=true | all-gather | bytes 974848 | tf_op jit(solution)/shard_map/all_gather | solution.py:468
  29.9 0.4 collective-permute-start.1
  30.3 0.2 collective-permute-start.2
  30.4 0.4 collective-permute-start.3
  30.8 4.3 %readout.1 = (bf16[16,24,2048]{2,1,0:T(8,128)(2,1)S(1)}, f32[64,128]{1,0:T(8,128)S(1)}) custom-call(s32[1]{0:T(128)} %bitcast.mine_ref, bf16[16,112,256]{2,1,0:T(8,128)(2,1)S(1)} %bitcast.22, f32[16,256]{1,0:T(8,128)} %decay_ref.5, f32[16,128]{1,0:T(8,128)} %bcoef_ref.5, f32[16,128]{1,0:T(8,128)} %ccoef_ref.1, f32[128,256]{1,0:T(8,128)S(1)} %get-tuple-element.20.step_ref, ...), custom_call_target="tpu_custom_call" | custom-call | tf_op jit(solution)/shard_map/readout/pallas_call | solution.py:401
  35.1 28.0 %all_to_all.45.shares_ref = bf16[16,24,2048]{2,1,0:T(8,128)(2,1)S(1)} all-to-all(bf16[16,24,2048]{2,1,0:T(8,128)(2,1)S(1)} %get-tuple-element.27), channel_id=1, replica_groups=mesh['z'=8,'core'=2,'exp'=16] {'exp'}, dimensions={0} | all-to-all | bytes 3145728 | tf_op jit(solution)/shard_map/all_to_all | solution.py:434
  63.1 0.9 norm.1
  64.1 15.2 %all_to_all.46 = bf16[8,8,2048]{2,1,0:T(8,128)(2,1)S(1)} all-to-all(bf16[8,8,2048]{2,1,0:T(8,128)(2,1)S(1)} %get-tuple-element.28), channel_id=1, replica_groups=mesh['z'=8,'core'=2,'exp'=16] {'z'}, dimensions={0} | all-to-all | bytes 524288 | tf_op jit(solution)/shard_map/all_to_all | solution.py:434
  79.2 0.5 pack.1
  79.8 18.1 %all_to_all.47 = bf16[16,16,2048]{2,1,0:T(8,128)(2,1)S(1)} all-to-all(bf16[16,16,2048]{2,1,0:T(8,128)(2,1)S(1)} %bitcast.21), channel_id=1, replica_groups=mesh['z'=8,'core'=2,'exp'=16] {'exp'}, dimensions={0} | all-to-all | bytes 2097152 | tf_op jit(solution)/shard_map/all_to_all | solution.py:434
  97.9 0.0 collective-permute-done.1.gate_sib_hbm
  97.9 0.0 collective-permute-done.2.up_sib_hbm
  97.9 0.0 collective-permute-done.3.down_sib_hbm
  97.9 17.8 %expert.1 = bf16[256,4224]{1,0:T(8,128)(2,1)S(1)} custom-call(bf16[256,2048]{1,0:T(8,128)(2,1)S(1)} %bitcast.20, bf16[16,24,2048]{2,1,0:T(8,128)(2,1)S(1)} %all_to_all.45.shares_ref, bf16[2048,896]{1,0:T(8,128)(2,1)} %bitcast.26, bf16[2048,896]{1,0:T(8,128)(2,1)} %collective-permute-done.1.gate_sib_hbm, bf16[2048,896]{1,0:T(8,128)(2,1)} %bitcast.28, ...), custom_call_target="tpu_custom_call" | custom-call | tf_op jit(solution)/shard_map/expert/pallas_call | solution.py:401
  115.7 29.3 %all_to_all.48 = bf16[16,16,4224]{2,1,0:T(8,128)(2,1)S(1)} all-to-all(bf16[16,16,4224]{2,1,0:T(8,128)(2,1)S(1)} %bitcast.18), channel_id=1, replica_groups=mesh['z'=8,'core'=2,'exp'=16] {'exp'}, dimensions={0} | all-to-all | bytes 4325376 | tf_op jit(solution)/shard_map/all_to_all | solution.py:434
  145.0 0.7 combine.1
  145.7 19.0 %all_to_all.49.back_ref = bf16[8,8,4224]{2,1,0:T(8,128)(2,1)S(1)} all-to-all(bf16[8,8,4224]{2,1,0:T(8,128)(2,1)S(1)} %bitcast.23), channel_id=1, replica_groups=mesh['z'=8,'core'=2,'exp'=16] {'z'}, dimensions={0} | all-to-all | bytes 1081344 | tf_op jit(solution)/shard_map/all_to_all | solution.py:434
  164.7 1.6 finish.1
Async XLA Ops:
  0.6 4.5 %collective-permute-start = (bf16[128,256]{1,0:T(8,128)(2,1)}, bf16[128,256]{1,0:T(8,128)(2,1)S(1)}, u32[]{:S(2)}, u32[]{:S(2)}) collective-permute-start(bf16[128,256]{1,0:T(8,128)(2,1)} %x_ref.3), channel_id=1, source_target_pairs={{0,16},{16,32},{32,48},{48,64},{64,80},{80,96},{96,112},{112,128},... | collective-permute-start | bytes 196616 | tf_op jit(solution)/shard_map/ppermute | solution.py:436
  29.9 68.0 %collective-permute-start.1 = (bf16[2048,896]{1,0:T(8,128)(2,1)}, bf16[2048,896]{1,0:T(8,128)(2,1)}, u32[]{:S(2)}, u32[]{:S(2)}) collective-permute-start(bf16[2048,896]{1,0:T(8,128)(2,1)} %bitcast.25), channel_id=1, source_target_pairs={{0,16},{16,0},{1,17},{17,1},{2,18},{18,2},{3,19},{19,3},{4,20},{20... | collective-permute-start | bytes 11010056 | tf_op jit(solution)/shard_map/ppermute | solution.py:431
  30.3 67.6 %collective-permute-start.2 = (bf16[2048,896]{1,0:T(8,128)(2,1)}, bf16[2048,896]{1,0:T(8,128)(2,1)}, u32[]{:S(2)}, u32[]{:S(2)}) collective-permute-start(bf16[2048,896]{1,0:T(8,128)(2,1)} %bitcast.27), channel_id=1, source_target_pairs={{0,16},{16,0},{1,17},{17,1},{2,18},{18,2},{3,19},{19,3},{4,20},{20... | collective-permute-start | bytes 11010056 | tf_op jit(solution)/shard_map/ppermute | solution.py:431
  30.4 67.5 %collective-permute-start.3 = (bf16[896,2048]{1,0:T(8,128)(2,1)}, bf16[896,2048]{1,0:T(8,128)(2,1)}, u32[]{:S(2)}, u32[]{:S(2)}) collective-permute-start(bf16[896,2048]{1,0:T(8,128)(2,1)} %bitcast.29), channel_id=1, source_target_pairs={{0,16},{16,0},{1,17},{17,1},{2,18},{18,2},{3,19},{19,3},{4,20},{20... | collective-permute-start | bytes 11010056 | tf_op jit(solution)/shard_map/ppermute | solution.py:431

commit v7 on v6

--- a/solution.py
+++ b/solution.py
@@ -160,7 +160,7 @@
 
 def readout_body(
     mine_ref, gathered_ref, decay_ref, bcoef_ref, ccoef_ref, step_ref, inner_ref, first_ref,
-    skip_ref, gate_ref, weight_ref, out_ref, info_ref, drive_ref, read_ref, inner_all_ref,
+    skip_ref, gate_ref, weight_ref, out_ref, packed_ref, info_ref, drive_ref, read_ref, inner_all_ref,
     tokens_ref,
 ):
     rate = -decay_ref[...]
@@ -199,10 +199,10 @@
     lax.fori_loop(0, length // GROUP, group, (state, bcoef_ref[...], ccoef_ref[...]))
     output = read_ref[...] + skip_ref[...] * inner_all_ref[...]
     output = output * jax.nn.silu(gate_ref[...].astype(F32))
-    share = jnp.dot(output.astype(BF16), weight_ref[...], preferred_element_type=F32).astype(BF16)
-    experts, tall, width = out_ref.shape
-    rows = length // experts
-    slots = tall - rows
+    out_ref[...] = jnp.dot(
+        output.astype(BF16), weight_ref[...], preferred_element_type=F32
+    ).astype(BF16)
+    slots, width = packed_ref.shape
     tokens = info_ref.shape[0] // depth
     start = 2 * count + GROUP
     for z in range(depth):
@@ -216,17 +216,14 @@
                 place, first : first + tokens
             ].astype(F32)
     info = info_ref[...]
-    chosen = slot_maps(info, experts * slots)
-    packed = jnp.zeros((experts * slots, width), F32)
+    chosen = slot_maps(info, slots)
+    packed = jnp.zeros((slots, width), F32)
     for k in range(2):
         at = 2 + 3 * k
         score = info[:, at : at + 1] + info[:, at + 1 : at + 2] + info[:, at + 2 : at + 3]
         grad_rows = (score * tokens_ref[...]).astype(BF16)
         packed = packed + contract_first(chosen[k].astype(BF16), grad_rows)
-    packed = packed.astype(BF16)
-    for e in range(experts):
-        out_ref[e, 0:slots] = packed[e * slots : (e + 1) * slots]
-        out_ref[e, slots:] = share[e * rows : (e + 1) * rows]
+    packed_ref[...] = packed.astype(BF16)
 
 
 def slot_maps(info, slots):
@@ -240,11 +237,9 @@
 
 
 def norm_body(shares_ref, residual_ref, gain_ref, hidden_ref, send_ref):
-    rows = residual_ref.shape[0]
-    start = shares_ref.shape[1] - rows
-    total = shares_ref[0, start:].astype(F32)
+    total = shares_ref[0].astype(F32)
     for c in range(1, shares_ref.shape[0]):
-        total = total + shares_ref[c, start:].astype(F32)
+        total = total + shares_ref[c].astype(F32)
     hidden = residual_ref[...].astype(F32) + total
     hidden_ref[...] = hidden
     scale = lax.rsqrt(jnp.mean(hidden * hidden, axis=1, keepdims=True) + 1e-05)
@@ -253,18 +248,21 @@
         send_ref[c] = normed
 
 
-def pack_body(tokens_ref, info_ref, slots_ref):
-    first, second = slot_maps(info_ref[...], slots_ref.shape[0])
-    slots_ref[...] = contract_first((first + second).astype(BF16), tokens_ref[...]).astype(BF16)
+def pack_body(tokens_ref, info_ref, packed_ref, slots_ref):
+    slots, width = packed_ref.shape
+    first, second = slot_maps(info_ref[...], slots)
+    rows = contract_first((first + second).astype(BF16), tokens_ref[...])
+    slots_ref[:, 0:width] = rows.astype(BF16)
+    slots_ref[:, width:] = packed_ref[...]
 
 
 def expert_body(
-    rows_ref, shares_ref, gate_hbm, gate_sib_hbm, up_hbm, up_sib_hbm, down_hbm, down_sib_hbm,
+    rows_ref, gate_hbm, gate_sib_hbm, up_hbm, up_sib_hbm, down_hbm, down_sib_hbm,
     out_ref, gate_ref, up_ref, down_ref, gate_pre_ref, up_pre_ref, act_ref, grad_gate_ref,
     grad_up_ref, dots_ref, grad_act_ref, sems,
 ):
-    slots, width = rows_ref.shape
-    units = gate_ref.shape[2]
+    slots = rows_ref.shape[0]
+    width, units = gate_ref.shape[1:]
     plan = (
         (down_hbm, down_ref, 0), (down_sib_hbm, down_ref, 1), (gate_hbm, gate_ref, 0),
         (up_hbm, up_ref, 0), (gate_sib_hbm, gate_ref, 1), (up_sib_hbm, up_ref, 1),
@@ -281,14 +279,13 @@
         if index + 3 < len(copies):
             copies[index + 3].start()
 
-    experts = shares_ref.shape[0]
-    grad_rows = shares_ref[:, 0 : slots // experts].reshape(slots, width)
+    grad_rows = rows_ref[:, width:]
     for half in range(2):
         ready(half)
         grad_act_ref[half] = contract_last(grad_rows, down_ref[half])
     dots_ref[...] = jnp.zeros(dots_ref.shape, F32)
     tall = 16
-    rows = rows_ref[...]
+    rows = rows_ref[:, 0:width]
     for half in range(2):
         ready(2 + 2 * half)
         gate_pre_ref[...] = jnp.dot(rows, gate_ref[half], preferred_element_type=F32)
@@ -473,10 +470,12 @@
         ups = (up_weight[0], sibling(up_sent))
         downs = (down_weight[0], sibling(down_sent))
         mine = lax.axis_index(("z", "core")).astype(jnp.int32).reshape(1)
-        tall = tok_rows + stride
-        share, info = call(
+        share, packed_grad, info = call(
             readout_body, "readout",
-            (near((experts, tall, width), BF16), near((depth * tok_rows, LANES), F32)),
+            (
+                near((length, width), BF16), near((slots, width), BF16),
+                near((depth * tok_rows, LANES), F32),
+            ),
             [SMEM, NEAR] + [VMEM] * 3 + [NEAR] * 3 + [VMEM] * 3,
             (
                 pltpu.VMEM((length, channels), F32), pltpu.VMEM((length, channels), F32),
@@ -487,8 +486,7 @@
                 skip_gain[None], mixer_gate, out_weight,
             ),
         )
-        shares = exchange(share.reshape(experts * tall, width), "exp")
-        shares = shares.reshape(experts, tall, width)
+        shares = exchange(share, "exp").reshape(experts, tok_rows, width)
         hidden, send = call(
             norm_body, "norm",
             (near((tok_rows, width), F32), near((depth, tok_rows, width), BF16)),
@@ -497,12 +495,13 @@
         )
         tokens = exchange(send.reshape(depth * tok_rows, width), "z")
         packed = call(
-            pack_body, "pack", near((slots, width), BF16), [NEAR] * 2, operands=(tokens, info)
+            pack_body, "pack", near((slots, 2 * width), BF16), [NEAR] * 3,
+            operands=(tokens, info, packed_grad),
         )
         rows_x = exchange(packed, "exp")
         result = call(
             expert_body, "expert", near((slots, 2 * width + LANES), BF16),
-            [NEAR] * 2 + [ANY] * 6,
+            [NEAR] + [ANY] * 6,
             (
                 pltpu.VMEM((2, width, units), BF16),
                 pltpu.VMEM((2, width, units), BF16),
@@ -516,7 +515,7 @@
                 pltpu.VMEM((2, slots, units), F32),
                 pltpu.SemaphoreType.DMA((6,)),
             ),
-            (rows_x, shares) + gates + ups + downs,
+            (rows_x,) + gates + ups + downs,
             48,
         )
         back = exchange(result, "exp")

time: 167 us -> 167 us (level)
  no operation moved by 1% of the time
where the time goes in v7:
time: 167 us; the launch traced here: 166 us
  blocking collectives  134 us (80%)
  Pallas kernels  29.6 us (18%)
  starting transfers between devices  2.6 us (2%)
    all_to_all x5, blocking collectives, exchange(): return lax.all_to_all(rows, axis, split_axis=0, concat_axis=0, tiled=True)  110 us
    pallas_call x8, Pallas kernels, call(): pl.pallas_call(body, out_shape=outs, in_specs=[VMEM if spec is NEAR else...  29.6 us
    all_gather x1, blocking collectives, per_device(): gathered = lax.all_gather(summary, ('z', 'core'), axis=0)  23.8 us
  transfers between devices with their start and end apart: 4, of which 0 were waited for; matrix products, arithmetic and copies ran while one was open for 0% of the time, Pallas kernels for 5%

profile of v7, /device:TPU:2, one launch (start us, length us, event | category | flops | bytes accessed | tf_op | source)
XLA Modules:
  0.0 166.5 jit_solution(13806190803605437245)
XLA Ops:
  0.6 1.7 %collective-permute-start = (bf16[128,256]{1,0:T(8,128)(2,1)}, bf16[128,256]{1,0:T(8,128)(2,1)S(1)}, u32[]{:S(2)}, u32[]{:S(2)}) collective-permute-start(bf16[128,256]{1,0:T(8,128)(2,1)} %x_ref.3), channel_id=1, source_target_pairs={{0,16},{16,32},{32,48},{48,64},{64,80},{80,96},{96,112},{112,128},... | collective-permute-start | bytes 196616 | tf_op jit(solution)/shard_map/ppermute | solution.py:433
  2.4 2.7 %local_state.1 = (f32[24,256]{1,0:T(8,128)S(1)}, f32[128,256]{1,0:T(8,128)S(1)}, f32[128,256]{1,0:T(8,128)S(1)}, bf16[72,256]{1,0:T(8,128)(2,1)S(1)}) custom-call(bf16[128,256]{1,0:T(8,128)(2,1)} %x_ref.3, bf16[128,128]{1,0:T(8,128)(2,1)} %low_ref.1, bf16[128,256]{1,0:T(8,128)(2,1)} %proj_ref.1, f32[1,256]{1,0:T(1,128)} %bitcast.39, f32[16,256]{1,0:T(8,128)} %decay_ref.5, ...), custom_call_target="tpu_custom_call" | custom-call | tf_op jit(solution)/shard_map/local_state/pallas_call | solution.py:398
  5.1 0.0 collective-permute-done.before_ref
  5.1 1.0 first_group.1
  6.1 23.8 %all-gather = bf16[1792,256]{1,0:T(8,128)(2,1)S(1)} all-gather(bf16[112,256]{1,0:T(8,128)(2,1)S(1)} %get-tuple-element.24), channel_id=2, replica_groups=mesh['z'=8,'core'=2,'exp'=16] {'z','core'}, dimensions={0}, use_global_device_ids=true | all-gather | bytes 974848 | tf_op jit(solution)/shard_map/all_gather | solution.py:465
  29.9 0.4 collective-permute-start.1
  30.3 0.2 collective-permute-start.2
  30.4 0.4 collective-permute-start.3
  30.8 4.3 %readout.1 = (bf16[128,2048]{1,0:T(8,128)(2,1)S(1)}, bf16[256,2048]{1,0:T(8,128)(2,1)S(1)}, f32[64,128]{1,0:T(8,128)S(1)}) custom-call(s32[1]{0:T(128)} %bitcast.mine_ref, bf16[16,112,256]{2,1,0:T(8,128)(2,1)S(1)} %bitcast.23, f32[16,256]{1,0:T(8,128)} %decay_ref.5, f32[16,128]{1,0:T(8,128)} %bcoef_ref.5, f32[16,128]{1,0:T(8,128)} %ccoef_ref.1, ...), custom_call_target="tpu_custom_call" | custom-call | tf_op jit(solution)/shard_map/readout/pallas_call | solution.py:398
  35.1 16.8 %all_to_all.48.shares_ref = bf16[16,8,2048]{2,1,0:T(8,128)(2,1)S(1)} all-to-all(bf16[16,8,2048]{2,1,0:T(8,128)(2,1)S(1)} %bitcast.26), channel_id=1, replica_groups=mesh['z'=8,'core'=2,'exp'=16] {'exp'}, dimensions={0} | all-to-all | bytes 1048576 | tf_op jit(solution)/shard_map/all_to_all | solution.py:431
  51.9 0.9 norm.1
  52.9 15.2 %all_to_all.49 = bf16[8,8,2048]{2,1,0:T(8,128)(2,1)S(1)} all-to-all(bf16[8,8,2048]{2,1,0:T(8,128)(2,1)S(1)} %get-tuple-element.29), channel_id=1, replica_groups=mesh['z'=8,'core'=2,'exp'=16] {'z'}, dimensions={0} | all-to-all | bytes 524288 | tf_op jit(solution)/shard_map/all_to_all | solution.py:431
  68.1 0.5 pack.1
  68.6 29.5 %all_to_all.50 = bf16[16,16,4096]{2,1,0:T(8,128)(2,1)S(1)} all-to-all(bf16[16,16,4096]{2,1,0:T(8,128)(2,1)S(1)} %bitcast.22), channel_id=1, replica_groups=mesh['z'=8,'core'=2,'exp'=16] {'exp'}, dimensions={0} | all-to-all | bytes 4194304 | tf_op jit(solution)/shard_map/all_to_all | solution.py:431
  98.1 0.0 collective-permute-done.1.gate_sib_hbm
  98.1 0.0 collective-permute-done.2.up_sib_hbm
  98.1 0.0 collective-permute-done.3.down_sib_hbm
  98.1 17.8 %expert.1 = bf16[256,4224]{1,0:T(8,128)(2,1)S(1)} custom-call(bf16[256,4096]{1,0:T(8,128)(2,1)S(1)} %bitcast.21, bf16[2048,896]{1,0:T(8,128)(2,1)} %bitcast.28, bf16[2048,896]{1,0:T(8,128)(2,1)} %collective-permute-done.1.gate_sib_hbm, bf16[2048,896]{1,0:T(8,128)(2,1)} %bitcast.30, bf16[2048,896]{1,0:T(8,128)(2,1)} %collective-permute-done.2.up_sib_hbm, ...), custom_call_target="tpu_custom_call" | custom-call | tf_op jit(solution)/shard_map/expert/pallas_call | solution.py:398
  115.9 29.3 %all_to_all.51 = bf16[16,16,4224]{2,1,0:T(8,128)(2,1)S(1)} all-to-all(bf16[16,16,4224]{2,1,0:T(8,128)(2,1)S(1)} %bitcast.19), channel_id=1, replica_groups=mesh['z'=8,'core'=2,'exp'=16] {'exp'}, dimensions={0} | all-to-all | bytes 4325376 | tf_op jit(solution)/shard_map/all_to_all | solution.py:431
  145.2 0.7 combine.1
  145.9 19.0 %all_to_all.52.back_ref = bf16[8,8,4224]{2,1,0:T(8,128)(2,1)S(1)} all-to-all(bf16[8,8,4224]{2,1,0:T(8,128)(2,1)S(1)} %bitcast.24), channel_id=1, replica_groups=mesh['z'=8,'core'=2,'exp'=16] {'z'}, dimensions={0} | all-to-all | bytes 1081344 | tf_op jit(solution)/shard_map/all_to_all | solution.py:431
  164.9 1.6 finish.1
Async XLA Ops:
  0.6 4.5 %collective-permute-start = (bf16[128,256]{1,0:T(8,128)(2,1)}, bf16[128,256]{1,0:T(8,128)(2,1)S(1)}, u32[]{:S(2)}, u32[]{:S(2)}) collective-permute-start(bf16[128,256]{1,0:T(8,128)(2,1)} %x_ref.3), channel_id=1, source_target_pairs={{0,16},{16,32},{32,48},{48,64},{64,80},{80,96},{96,112},{112,128},... | collective-permute-start | bytes 196616 | tf_op jit(solution)/shard_map/ppermute | solution.py:433
  29.9 68.2 %collective-permute-start.1 = (bf16[2048,896]{1,0:T(8,128)(2,1)}, bf16[2048,896]{1,0:T(8,128)(2,1)}, u32[]{:S(2)}, u32[]{:S(2)}) collective-permute-start(bf16[2048,896]{1,0:T(8,128)(2,1)} %bitcast.27), channel_id=1, source_target_pairs={{0,16},{16,0},{1,17},{17,1},{2,18},{18,2},{3,19},{19,3},{4,20},{20... | collective-permute-start | bytes 11010056 | tf_op jit(solution)/shard_map/ppermute | solution.py:428
  30.3 67.9 %collective-permute-start.2 = (bf16[2048,896]{1,0:T(8,128)(2,1)}, bf16[2048,896]{1,0:T(8,128)(2,1)}, u32[]{:S(2)}, u32[]{:S(2)}) collective-permute-start(bf16[2048,896]{1,0:T(8,128)(2,1)} %bitcast.29), channel_id=1, source_target_pairs={{0,16},{16,0},{1,17},{17,1},{2,18},{18,2},{3,19},{19,3},{4,20},{20... | collective-permute-start | bytes 11010056 | tf_op jit(solution)/shard_map/ppermute | solution.py:428
  30.4 67.7 %collective-permute-start.3 = (bf16[896,2048]{1,0:T(8,128)(2,1)}, bf16[896,2048]{1,0:T(8,128)(2,1)}, u32[]{:S(2)}, u32[]{:S(2)}) collective-permute-start(bf16[896,2048]{1,0:T(8,128)(2,1)} %bitcast.31), channel_id=1, source_target_pairs={{0,16},{16,0},{1,17},{17,1},{2,18},{18,2},{3,19},{19,3},{4,20},{20... | collective-permute-start | bytes 11010056 | tf_op jit(solution)/shard_map/ppermute | solution.py:428
